TPU v7x, 256 devices: a whole 4x4x8 slice. The times are simulated.
256 devices in a mesh: sx: 32 (over z_lo, x, y), sy: 8 (over z_hi, core).
Axes of the slice: x: 4, y: 4, z: 8 (z_hi: 4, z_lo: 2; z = z_hi * 2 + z_lo), core: 2. Of those that a mesh axis runs over, the one named last changes fastest.
Arguments:
- snapshots: bfloat16 [1024, 3, 64, 1024], P(None, None, 'sx', 'sy'), may hold values from -6 to 6
- quad_weight: float32 [3, 64, 1024], P(None, 'sx', 'sy'), may hold values from 0.5 to 1200
- mode_guess: float32 [16, 64, 2, 8], replicated, may hold values from -6 to 6
- bins: int32 [16], replicated, may hold values from 1 to 127
- starts: int32 [64], replicated, may hold values from 0 to 768
Outputs:
- modes: float32 [16, 2, 8, 3, 64, 1024], P(None, None, None, None, 'sx', 'sy')
- energy: float32 [16, 8], replicated
All inputs are finite; a program needn't handle non-finite values.
Results may differ from a plain program's by a relative error of at most 0.0024.
Values may be sent and summed in bfloat16 or wider, within the bound.
No kernel may reach another device: no remote copies, remote signals or barrier semaphores. Data moves between devices by JAX's collectives and lax.ppermute only.
A program may use at most 64 MiB of HBM per device.

v0:
```python
import functools

import jax
import jax.numpy as jnp
from jax import lax
from jax.sharding import Mesh
from jax.sharding import PartitionSpec as P

NFFT = 256
SX_SY = ("sx_0", "sx_1", "sx_2", "sy_0", "sy_1")
SX = ("sx_0", "sx_1", "sx_2")
SY = ("sy_0", "sy_1")


EPS = 1e-06


def one_axis_at_a_time(x, axes):
    return functools.reduce(lax.psum, axes, x)


def cut_along(x, dim, count):
    dims = x.shape
    parts = x.reshape(*dims[:dim], count, dims[dim] // count, *dims[dim + 1 :])
    return jnp.moveaxis(parts, dim, 0)


def sum_at_owner(x, axis, dim):
    count = lax.axis_size(axis)
    parts = lax.all_to_all(cut_along(x, dim, count), axis, 0, 0, tiled=True)
    return jnp.sum(parts.astype(jnp.float32), axis=0)


def copy_for_each(x, axis):
    copies = jnp.broadcast_to(x, (lax.axis_size(axis), *x.shape))
    return lax.all_to_all(copies, axis, split_axis=0, concat_axis=0, tiled=True)


def taken_together(x, axis):
    return copy_for_each(x, axis).sum(axis=0)


def laid_out(parts, dim):
    dims = list(parts.shape[1:])
    dims[dim] *= parts.shape[0]
    return jnp.moveaxis(parts, 0, dim).reshape(dims)


def gathered_copies(x, axis, dim):
    parts = copy_for_each(x, axis)
    return laid_out(parts, dim)


def make_twiddle(bins):
    steps = jnp.arange(NFFT, dtype=jnp.int32)
    window = 0.5 - 0.5 * jnp.cos(2.0 * jnp.pi * steps.astype(jnp.float32) / NFFT)
    norm_c = 1.0 / jnp.sqrt(jnp.sum(window * window))
    phase = bins[:, None] * steps[None, :] % NFFT
    angle = 2.0 * jnp.pi * phase.astype(jnp.float32) / NFFT
    twid = jnp.stack(
        [norm_c * window * jnp.cos(angle), -(norm_c * window) * jnp.sin(angle)], axis=1
    )
    return twid.astype(jnp.bfloat16)


def row_terms(rows, start, guess, nblock):
    count = rows.shape[0]
    nbins = guess.shape[0]
    hp = lax.Precision.HIGHEST
    which = (start + jnp.arange(count, dtype=jnp.int32)) // nblock
    onehot = (which[:, None] == jnp.arange(nbins, dtype=jnp.int32)[None, :]).astype(jnp.float32)
    picked = jnp.einsum("rf,fcpn->rcpn", onehot, guess, precision=hp)
    gram_re = rows[:, :nblock]
    gram_im = rows[:, nblock:]
    zre = jnp.einsum("rc,rcn->rn", gram_re, picked[:, :, 0], precision=hp) - jnp.einsum(
        "rc,rcn->rn", gram_im, picked[:, :, 1], precision=hp
    )
    zim = jnp.einsum("rc,rcn->rn", gram_re, picked[:, :, 1], precision=hp) + jnp.einsum(
        "rc,rcn->rn", gram_im, picked[:, :, 0], precision=hp
    )
    partial_norm = jnp.einsum("rf,rn->fn", onehot, zre * zre + zim * zim, precision=hp)
    return (zre, zim, partial_norm, onehot)


def finish_rows(zre, zim, norms, onehot):
    row_norm = jnp.dot(onehot, norms, precision=lax.Precision.HIGHEST)
    inv = lax.rsqrt(row_norm + EPS)
    return jnp.concatenate([zre * inv, zim * inv], axis=-1).astype(jnp.bfloat16)


def shards(snapshots, quad_weight, mode_guess, bins, starts):
    length, nvar, cols_x, cols_y = snapshots.shape
    nbins = bins.shape[0]
    nblock = starts.shape[0]
    nmode = mode_guess.shape[-1]
    points = nvar * cols_x * cols_y
    local_sq = jnp.sum(
        jnp.square(snapshots.astype(jnp.float32)) * quad_weight[None], axis=(0, 2, 3)
    )
    total_sq = one_axis_at_a_time(local_sq, SX_SY)
    grid_points = cols_x * cols_y * lax.axis_size(SX) * lax.axis_size(SY)
    scale = lax.rsqrt(total_sq / (length * grid_points) + EPS)
    colscale = (scale[:, None, None] * jnp.sqrt(quad_weight)).reshape(points)
    twid = make_twiddle(bins).reshape(nbins * 2, NFFT)
    flat = snapshots.reshape(length, points)
    group = 8

    def block_step(number):
        first_block = lax.dynamic_slice_in_dim(starts, number * group, group)
        times = first_block[:, None] + jnp.arange(NFFT, dtype=jnp.int32)[None, :]
        windows = jnp.take(flat, times, axis=0)
        qhat = jnp.einsum("qt,btx->bqx", twid, windows, preferred_element_type=jnp.float32)
        return (qhat * colscale[None, None, :]).astype(jnp.bfloat16)

    blocks = lax.map(block_step, jnp.arange(nblock // group, dtype=jnp.int32))
    blocks = blocks.reshape(nblock, nbins, 2, points)
    ydata = jnp.transpose(blocks, (1, 2, 0, 3)).reshape(nbins, 2 * nblock, points)
    gram = jnp.einsum("fax,fbx->fab", ydata, ydata, preferred_element_type=jnp.float32)
    gram_re = gram[:, :nblock, :nblock] + gram[:, nblock:, nblock:]
    gram_im = gram[:, :nblock, nblock:] - gram[:, nblock:, :nblock]
    local_gram = jnp.concatenate([gram_re, gram_im], axis=-1).reshape(nbins * nblock, 2 * nblock)
    denom = 3.0 * grid_points
    halves = sum_at_owner(local_gram.astype(jnp.bfloat16), SY, 0)
    owned = taken_together(halves, SX) / denom
    first = lax.axis_index(SY) * owned.shape[0]
    zre, zim, partial_norm, onehot = row_terms(owned, first, mode_guess, nblock)
    norms = taken_together(partial_norm, SY)
    coef = gathered_copies(finish_rows(zre, zim, norms, onehot), SY, 0)
    energy = jnp.sqrt(norms / nblock)
    coef = coef.reshape(nbins, nblock, 2 * nmode)
    coef_re = coef[:, :, :nmode]
    coef_im = coef[:, :, nmode:]
    upper = jnp.concatenate([coef_re, coef_im], axis=-1)
    lower = jnp.concatenate([-coef_im, coef_re], axis=-1)
    stacked = jnp.concatenate([upper, lower], axis=1)
    modes = jnp.einsum("fan,fax->fnx", stacked, ydata, preferred_element_type=jnp.float32)
    return (modes.reshape(nbins, 2, nmode, nvar, cols_x, cols_y), energy)


def solution(mesh):
    finer = Mesh(mesh.devices.reshape(2, 4, 4, 4, 2), ("sx_0", "sx_1", "sx_2", "sy_0", "sy_1"))
    placed = (P(None, None, SX, SY), P(None, SX, SY), P(), P(), P())
    return jax.shard_map(
        shards,
        mesh=finer,
        in_specs=placed,
        out_specs=(P(None, None, None, None, SX, SY), P()),
        check_vma=False,
    )
```

profile of v0, /device:TPU:1, one launch (start us, length us, event | category | flops | bytes accessed | tf_op | source)
XLA Modules:
  0.0 260.9 jit_solution(8880993724121743045)
XLA Ops:
  2.0 3.8 %multiply_reduce_fusion = f32[3]{0:T(128)S(1)} fusion(bf16[1024,3,2,128]{3,2,1,0:T(2,128)(2,1)} %param.7, f32[3,2,128]{2,1,0:T(2,128)} %param.8), kind=kLoop, calls=%fused_computation.18 | loop fusion | flops 3145725 | bytes 1575948 | tf_op jit(solution)/shard_map/reduce_sum | solution.py:97
  5.9 4.8 %psum.35 = f32[3]{0:T(128)S(1)} all-reduce(f32[3]{0:T(128)S(1)} %multiply_reduce_fusion), channel_id=1, replica_groups=mesh['sx_0'=2,'sx_1'=4,'sx_2'=4,'sy_0'=4,'sy_1'=2] {'sx_0'}, use_global_device_ids=true, to_apply=%region_2.0 | all-reduce | flops 3 | bytes 24 | tf_op jit(solution)/shard_map/psum | solution.py:19
  10.7 8.4 %psum.36 = f32[3]{0:T(128)S(1)} all-reduce(f32[3]{0:T(128)S(1)} %psum.35), channel_id=1, replica_groups=mesh['sx_0'=2,'sx_1'=4,'sx_2'=4,'sy_0'=4,'sy_1'=2] {'sx_1'}, use_global_device_ids=true, to_apply=%region_3.0 | all-reduce | flops 3 | bytes 24 | tf_op jit(solution)/shard_map/psum | solution.py:19
  19.1 3.9 %reshape.248 = bf16[1024,768]{1,0:T(8,128)(2,1)S(1)} reshape(bf16[1024,3,2,128]{3,2,1,0:T(2,128)(2,1)} %param.7) | data formatting | bytes 3145728 | tf_op jit(solution)/shard_map/reshape | solution.py:105
  23.0 8.7 %psum.37 = f32[3]{0:T(128)S(1)} all-reduce(f32[3]{0:T(128)S(1)} %psum.36), channel_id=1, replica_groups=mesh['sx_0'=2,'sx_1'=4,'sx_2'=4,'sy_0'=4,'sy_1'=2] {'sx_2'}, use_global_device_ids=true, to_apply=%region_4.0 | all-reduce | flops 3 | bytes 24 | tf_op jit(solution)/shard_map/psum | solution.py:19
  32.0 12.8 %psum.38 = f32[3]{0:T(128)S(1)} all-reduce(f32[3]{0:T(128)S(1)} %psum.37), channel_id=1, replica_groups=mesh['sx_0'=2,'sx_1'=4,'sx_2'=4,'sy_0'=4,'sy_1'=2] {'sy_0'}, use_global_device_ids=true, to_apply=%region_5.0 | all-reduce | flops 3 | bytes 24 | tf_op jit(solution)/shard_map/psum | solution.py:19
  44.7 10.0 %psum.39 = f32[3]{0:T(128)S(1)} all-reduce(f32[3]{0:T(128)S(1)} %psum.38), channel_id=1, replica_groups=mesh['sx_0'=2,'sx_1'=4,'sx_2'=4,'sy_0'=4,'sy_1'=2] {'sy_1'}, use_global_device_ids=true, to_apply=%region_6.0 | all-reduce | flops 3 | bytes 24 | tf_op jit(solution)/shard_map/psum | solution.py:19
  54.8 115.3 %while.10 = (s32[]{:T(128)}, bf16[8,8,32,768]{3,2,1,0:T(8,128)(2,1)}, s32[8]{0:T(128)S(1)}, s32[64]{0:T(128)S(1)}, bf16[1024,768]{1,0:T(8,128)(2,1)S(1)}, /*inde...) while((s32[]{:T(128)}, ...), condition=%wide.region_8.9_spmd, body=%wide.region_7.8_spmd.sunk | while | flops 102653960 | bytes 9910059 | solution.py:115
  56.3 9.4 %gather_fusion = bf16[2048,768]{1,0:T(8,128)(2,1)} fusion(bf16[1024,768]{1,0:T(8,128)(2,1)S(1)} %get-tuple-element.153, s32[2048]{0:T(1024)S(1)} %broadcast_clamp_fusion.2), kind=kCustom, calls=%fused_computation.clone.1 | custom fusion | bytes 6299648 | tf_op jit(solution)/shard_map/while/body/eval_jaxpr/jit(_take)/gather | solution.py:111
  65.7 3.5 %fusion.66 = bf16[8,8,32,768]{3,2,1,0:T(8,128)(2,1)} fusion(bf16[8,8,32,768]{3,2,1,0:T(8,128)(2,1)} %get-tuple-element.139, s32[]{:T(128)} %get-tuple-element.138, bf16[8,256,768]{2,1,0:T(8,128)(2,1)} %bitcast.62, pred[8,256]{1,0:T(8,128)(4,1)S(1)} %fusion.65, f32[768]{0:T(1024)S(1)} %mul.248, bf16[32,256]{1,0:T(8,128)(2,1)S(1)} %get-tuple-element.154), kind=kOutput, calls=%fused_computation.8.clone.1 | convolution fusion | flops 102629376 | bytes 3560960 | tf_op jit(solution)/shard_map/while/body/eval_jaxpr/qt,btx->bqx/dot_general | solution.py:112
  70.6 9.4 %gather_fusion = bf16[2048,768]{1,0:T(8,128)(2,1)} fusion(bf16[1024,768]{1,0:T(8,128)(2,1)S(1)} %get-tuple-element.153, s32[2048]{0:T(1024)S(1)} %broadcast_clamp_fusion.2), kind=kCustom, calls=%fused_computation.clone.1 | custom fusion | bytes 6299648 | tf_op jit(solution)/shard_map/while/body/eval_jaxpr/jit(_take)/gather | solution.py:111
  80.1 3.5 %fusion.66 = bf16[8,8,32,768]{3,2,1,0:T(8,128)(2,1)} fusion(bf16[8,8,32,768]{3,2,1,0:T(8,128)(2,1)} %get-tuple-element.139, s32[]{:T(128)} %get-tuple-element.138, bf16[8,256,768]{2,1,0:T(8,128)(2,1)} %bitcast.62, pred[8,256]{1,0:T(8,128)(4,1)S(1)} %fusion.65, f32[768]{0:T(1024)S(1)} %mul.248, bf16[32,256]{1,0:T(8,128)(2,1)S(1)} %get-tuple-element.154), kind=kOutput, calls=%fused_computation.8.clone.1 | convolution fusion | flops 102629376 | bytes 3560960 | tf_op jit(solution)/shard_map/while/body/eval_jaxpr/qt,btx->bqx/dot_general | solution.py:112
  85.0 9.4 %gather_fusion = bf16[2048,768]{1,0:T(8,128)(2,1)} fusion(bf16[1024,768]{1,0:T(8,128)(2,1)S(1)} %get-tuple-element.153, s32[2048]{0:T(1024)S(1)} %broadcast_clamp_fusion.2), kind=kCustom, calls=%fused_computation.clone.1 | custom fusion | bytes 6299648 | tf_op jit(solution)/shard_map/while/body/eval_jaxpr/jit(_take)/gather | solution.py:111
  94.5 3.5 %fusion.66 = bf16[8,8,32,768]{3,2,1,0:T(8,128)(2,1)} fusion(bf16[8,8,32,768]{3,2,1,0:T(8,128)(2,1)} %get-tuple-element.139, s32[]{:T(128)} %get-tuple-element.138, bf16[8,256,768]{2,1,0:T(8,128)(2,1)} %bitcast.62, pred[8,256]{1,0:T(8,128)(4,1)S(1)} %fusion.65, f32[768]{0:T(1024)S(1)} %mul.248, bf16[32,256]{1,0:T(8,128)(2,1)S(1)} %get-tuple-element.154), kind=kOutput, calls=%fused_computation.8.clone.1 | convolution fusion | flops 102629376 | bytes 3560960 | tf_op jit(solution)/shard_map/while/body/eval_jaxpr/qt,btx->bqx/dot_general | solution.py:112
  99.4 9.4 %gather_fusion = bf16[2048,768]{1,0:T(8,128)(2,1)} fusion(bf16[1024,768]{1,0:T(8,128)(2,1)S(1)} %get-tuple-element.153, s32[2048]{0:T(1024)S(1)} %broadcast_clamp_fusion.2), kind=kCustom, calls=%fused_computation.clone.1 | custom fusion | bytes 6299648 | tf_op jit(solution)/shard_map/while/body/eval_jaxpr/jit(_take)/gather | solution.py:111
  108.9 3.5 %fusion.66 = bf16[8,8,32,768]{3,2,1,0:T(8,128)(2,1)} fusion(bf16[8,8,32,768]{3,2,1,0:T(8,128)(2,1)} %get-tuple-element.139, s32[]{:T(128)} %get-tuple-element.138, bf16[8,256,768]{2,1,0:T(8,128)(2,1)} %bitcast.62, pred[8,256]{1,0:T(8,128)(4,1)S(1)} %fusion.65, f32[768]{0:T(1024)S(1)} %mul.248, bf16[32,256]{1,0:T(8,128)(2,1)S(1)} %get-tuple-element.154), kind=kOutput, calls=%fused_computation.8.clone.1 | convolution fusion | flops 102629376 | bytes 3560960 | tf_op jit(solution)/shard_map/while/body/eval_jaxpr/qt,btx->bqx/dot_general | solution.py:112
  113.8 9.4 %gather_fusion = bf16[2048,768]{1,0:T(8,128)(2,1)} fusion(bf16[1024,768]{1,0:T(8,128)(2,1)S(1)} %get-tuple-element.153, s32[2048]{0:T(1024)S(1)} %broadcast_clamp_fusion.2), kind=kCustom, calls=%fused_computation.clone.1 | custom fusion | bytes 6299648 | tf_op jit(solution)/shard_map/while/body/eval_jaxpr/jit(_take)/gather | solution.py:111
  123.3 3.5 %fusion.66 = bf16[8,8,32,768]{3,2,1,0:T(8,128)(2,1)} fusion(bf16[8,8,32,768]{3,2,1,0:T(8,128)(2,1)} %get-tuple-element.139, s32[]{:T(128)} %get-tuple-element.138, bf16[8,256,768]{2,1,0:T(8,128)(2,1)} %bitcast.62, pred[8,256]{1,0:T(8,128)(4,1)S(1)} %fusion.65, f32[768]{0:T(1024)S(1)} %mul.248, bf16[32,256]{1,0:T(8,128)(2,1)S(1)} %get-tuple-element.154), kind=kOutput, calls=%fused_computation.8.clone.1 | convolution fusion | flops 102629376 | bytes 3560960 | tf_op jit(solution)/shard_map/while/body/eval_jaxpr/qt,btx->bqx/dot_general | solution.py:112
  128.3 9.4 %gather_fusion = bf16[2048,768]{1,0:T(8,128)(2,1)} fusion(bf16[1024,768]{1,0:T(8,128)(2,1)S(1)} %get-tuple-element.153, s32[2048]{0:T(1024)S(1)} %broadcast_clamp_fusion.2), kind=kCustom, calls=%fused_computation.clone.1 | custom fusion | bytes 6299648 | tf_op jit(solution)/shard_map/while/body/eval_jaxpr/jit(_take)/gather | solution.py:111
  137.7 3.5 %fusion.66 = bf16[8,8,32,768]{3,2,1,0:T(8,128)(2,1)} fusion(bf16[8,8,32,768]{3,2,1,0:T(8,128)(2,1)} %get-tuple-element.139, s32[]{:T(128)} %get-tuple-element.138, bf16[8,256,768]{2,1,0:T(8,128)(2,1)} %bitcast.62, pred[8,256]{1,0:T(8,128)(4,1)S(1)} %fusion.65, f32[768]{0:T(1024)S(1)} %mul.248, bf16[32,256]{1,0:T(8,128)(2,1)S(1)} %get-tuple-element.154), kind=kOutput, calls=%fused_computation.8.clone.1 | convolution fusion | flops 102629376 | bytes 3560960 | tf_op jit(solution)/shard_map/while/body/eval_jaxpr/qt,btx->bqx/dot_general | solution.py:112
  142.7 9.4 %gather_fusion = bf16[2048,768]{1,0:T(8,128)(2,1)} fusion(bf16[1024,768]{1,0:T(8,128)(2,1)S(1)} %get-tuple-element.153, s32[2048]{0:T(1024)S(1)} %broadcast_clamp_fusion.2), kind=kCustom, calls=%fused_computation.clone.1 | custom fusion | bytes 6299648 | tf_op jit(solution)/shard_map/while/body/eval_jaxpr/jit(_take)/gather | solution.py:111
  152.1 3.6 %fusion.66 = bf16[8,8,32,768]{3,2,1,0:T(8,128)(2,1)} fusion(bf16[8,8,32,768]{3,2,1,0:T(8,128)(2,1)} %get-tuple-element.139, s32[]{:T(128)} %get-tuple-element.138, bf16[8,256,768]{2,1,0:T(8,128)(2,1)} %bitcast.62, pred[8,256]{1,0:T(8,128)(4,1)S(1)} %fusion.65, f32[768]{0:T(1024)S(1)} %mul.248, bf16[32,256]{1,0:T(8,128)(2,1)S(1)} %get-tuple-element.154), kind=kOutput, calls=%fused_computation.8.clone.1 | convolution fusion | flops 102629376 | bytes 3560960 | tf_op jit(solution)/shard_map/while/body/eval_jaxpr/qt,btx->bqx/dot_general | solution.py:112
  157.1 9.4 %gather_fusion = bf16[2048,768]{1,0:T(8,128)(2,1)} fusion(bf16[1024,768]{1,0:T(8,128)(2,1)S(1)} %get-tuple-element.153, s32[2048]{0:T(1024)S(1)} %broadcast_clamp_fusion.2), kind=kCustom, calls=%fused_computation.clone.1 | custom fusion | bytes 6299648 | tf_op jit(solution)/shard_map/while/body/eval_jaxpr/jit(_take)/gather | solution.py:111
  166.6 3.5 %fusion.66 = bf16[8,8,32,768]{3,2,1,0:T(8,128)(2,1)} fusion(bf16[8,8,32,768]{3,2,1,0:T(8,128)(2,1)} %get-tuple-element.139, s32[]{:T(128)} %get-tuple-element.138, bf16[8,256,768]{2,1,0:T(8,128)(2,1)} %bitcast.62, pred[8,256]{1,0:T(8,128)(4,1)S(1)} %fusion.65, f32[768]{0:T(1024)S(1)} %mul.248, bf16[32,256]{1,0:T(8,128)(2,1)S(1)} %get-tuple-element.154), kind=kOutput, calls=%fused_computation.8.clone.1 | convolution fusion | flops 102629376 | bytes 3560960 | tf_op jit(solution)/shard_map/while/body/eval_jaxpr/qt,btx->bqx/dot_general | solution.py:112
  170.1 7.3 %reshape.249 = bf16[64,16,2,768]{3,2,1,0:T(2,128)(2,1)} reshape(bf16[8,8,32,768]{3,2,1,0:T(8,128)(2,1)} %get-tuple-element.39) | data formatting | bytes 6291456 | tf_op jit(solution)/shard_map/reshape | solution.py:116
  177.4 3.6 %copy.41 = bf16[16,2,64,768]{3,2,1,0:T(8,128)(2,1)S(1)} copy(bf16[16,2,64,768]{3,1,0,2:T(2,128)(2,1)} %bitcast.65) | data formatting | bytes 6291456 | tf_op jit(solution)/shard_map/transpose | solution.py:117
  182.5 13.9 %all_to_all.20 = bf16[8,128,128]{2,1,0:T(8,128)(2,1)S(1)} all-to-all(bf16[8,128,128]{2,1,0:T(8,128)(2,1)S(1)} %bitcast.67), channel_id=1, replica_groups=mesh['sx_0'=2,'sx_1'=4,'sx_2'=4,'sy_0'=4,'sy_1'=2] {'sy_0','sy_1'}, dimensions={0} | all-to-all | bytes 524288 | tf_op jit(solution)/shard_map/all_to_all | solution.py:30
  197.9 4.8 %all-to-all-start.1 = ((f32[32,128,128]{2,1,0:T(8,128)}), f32[32,128,128]{2,1,0:T(8,128)}, u32[]{:S(2)}, u32[]{:S(2)}) async-start(f32[32,128,128]{2,1,0:T(8,128)} %broadcast_in_dim.37), calls=%async_computation.1 | async-start | bytes 4194304 | tf_op jit(solution)/shard_map/all_to_all | solution.py:36
  204.2 23.4 %all-to-all-done.1 = f32[32,128,128]{2,1,0:T(8,128)} async-done(((f32[32,128,128]{2,1,0:T(8,128)}), f32[32,128,128]{2,1,0:T(8,128)}, u32[]{:S(2)}, u32[]{:S(2)}) %all-to-all-start.1) | async-done | bytes 2097184 | tf_op jit(solution)/shard_map/all_to_all | solution.py:36
  230.9 14.8 %all_to_all.21 = f32[8,1,128]{2,1,0:T(1,128)S(1)} all-to-all(f32[8,1,128]{2,1,0:T(1,128)S(1)} %reshape.271), channel_id=1, replica_groups=mesh['sx_0'=2,'sx_1'=4,'sx_2'=4,'sy_0'=4,'sy_1'=2] {'sy_0','sy_1'}, dimensions={0} | all-to-all | bytes 8192 | tf_op jit(solution)/shard_map/all_to_all | solution.py:36
  247.7 3.9 %all-to-all-start.3 = ((bf16[8,128,16]{1,2,0:T(8,128)(2,1)}), bf16[8,128,16]{1,2,0:T(8,128)(2,1)S(1)}, u32[]{:S(2)}, u32[]{:S(2)}) async-start(bf16[8,128,16]{1,2,0:T(8,128)(2,1)} %broadcast_in_dim.39), calls=%async_computation.3 | async-start | bytes 65536 | tf_op jit(solution)/shard_map/all_to_all | solution.py:36
  252.3 6.6 %all-to-all-done.3 = bf16[8,128,16]{1,2,0:T(8,128)(2,1)S(1)} async-done(((bf16[8,128,16]{1,2,0:T(8,128)(2,1)}), bf16[8,128,16]{1,2,0:T(8,128)(2,1)S(1)}, u32[]{:S(2)}, u32[]{:S(2)}) %all-to-all-start.3) | async-done | bytes 32800 | tf_op jit(solution)/shard_map/all_to_all | solution.py:36
  (106 shorter events, 20.1 us)
Async XLA Ops:
  0.6 202.1 %copy-start = (f32[16,64,2,8]{1,3,2,0:T(8,128)S(1)}, f32[16,64,2,8]{1,3,2,0:T(8,128)}, u32[]{:S(2)}) copy-start(f32[16,64,2,8]{1,3,2,0:T(8,128)} %param.9) | copy-start | bytes 196612
  0.6 54.1 %copy-start.1 = (f32[3,2,128]{2,1,0:T(2,128)S(1)}, f32[3,2,128]{2,1,0:T(2,128)}, u32[]{:S(2)}) copy-start(f32[3,2,128]{2,1,0:T(2,128)} %param.8) | copy-start | bytes 9220
  0.7 31.1 %copy-start.2 = (s32[16]{0:T(128)S(1)}, s32[16]{0:T(128)}, u32[]{:S(2)}) copy-start(s32[16]{0:T(128)} %param.10) | copy-start | bytes 196
  0.7 54.2 %copy-start.3 = (s32[64]{0:T(128)S(1)}, s32[64]{0:T(128)}, u32[]{:S(2)}) copy-start(s32[64]{0:T(128)} %param.11) | copy-start | bytes 772
  197.9 29.6 %all-to-all-start.1 = ((f32[32,128,128]{2,1,0:T(8,128)}), f32[32,128,128]{2,1,0:T(8,128)}, u32[]{:S(2)}, u32[]{:S(2)}) async-start(f32[32,128,128]{2,1,0:T(8,128)} %broadcast_in_dim.37), calls=%async_computation.1 | async-start | bytes 4194304 | tf_op jit(solution)/shard_map/all_to_all | solution.py:36
  247.7 11.2 %all-to-all-start.3 = ((bf16[8,128,16]{1,2,0:T(8,128)(2,1)}), bf16[8,128,16]{1,2,0:T(8,128)(2,1)S(1)}, u32[]{:S(2)}, u32[]{:S(2)}) async-start(bf16[8,128,16]{1,2,0:T(8,128)(2,1)} %broadcast_in_dim.39), calls=%async_computation.3 | async-start | bytes 65536 | tf_op jit(solution)/shard_map/all_to_all | solution.py:36
where the time goes:
time: 262 us; the launch traced here: 261 us
  local copies, waits for them, and re-layouts  99.8 us (38%)
  blocking collectives  73.4 us (28%)
  matrix products  31.5 us (12%)
  waiting for transfers between devices  30 us (11%)
  other arithmetic  10.8 us (4%)
  starting transfers between devices  8.7 us (3%)
  loops' own time  5.28 us (2%)
    gather x8, local copies, waits for them, and re-layouts, block_step(): windows = jnp.take(flat, times, axis=0)  75 us
    psum x5, blocking collectives, one_axis_at_a_time(): return functools.reduce(lax.psum, axes, x)  44.7 us
    all_to_all x2, waiting for transfers between devices, copy_for_each(): return lax.all_to_all(copies, axis, split_axis=0, concat_axis=0, tiled=True)  30 us
    dot_general x8, matrix products, block_step(): jnp.einsum('qt,btx->bqx', twid, windows, preferred_element_type=jnp.float32)  28.3 us
    all_to_all x1, blocking collectives, copy_for_each(): return lax.all_to_all(copies, axis, split_axis=0, concat_axis=0, tiled=True)  14.8 us
    all_to_all x1, blocking collectives, sum_at_owner(): parts = lax.all_to_all(cut_along(x, dim, count), axis, 0, 0, tiled=True)  13.9 us
    all_to_all x2, starting transfers between devices, copy_for_each(): return lax.all_to_all(copies, axis, split_axis=0, concat_axis=0, tiled=True)  8.7 us
    reshape x1, local copies, waits for them, and re-layouts, shards(): blocks = blocks.reshape(nblock, nbins, 2, points)  7.28 us
  transfers between devices with their start and end apart: 2, of which 2 were waited for; matrix products, arithmetic and copies ran while one was open for 1% of the time, Pallas kernels for 0%

commit v1 on v0

v1 whole, which is shorter than its diff:
```python
import functools
import math

import jax
import jax.numpy as jnp
from jax import lax
from jax.experimental import pallas as pl
from jax.experimental.pallas import tpu as pltpu
from jax.sharding import Mesh
from jax.sharding import PartitionSpec as P

NFFT = 256
EPS = 1e-06
AXES = ("sx_0", "sx_1", "sx_2", "sy_0", "sy_1")
SX = AXES[:3]
SY = AXES[3:]
OWNERS = ("sx_1", "sx_2", "sy_1")
COLUMN = ("sx_0", "sy_0")
MIB = 1 << 20


def split3(x):
    hi = x.astype(jnp.bfloat16).astype(jnp.float32)
    mid = (x - hi).astype(jnp.bfloat16).astype(jnp.float32)
    lo = (x - hi - mid).astype(jnp.bfloat16).astype(jnp.float32)
    return hi, mid, lo


def split2(x):
    hi = x.astype(jnp.bfloat16)
    lo = (x - hi.astype(jnp.float32)).astype(jnp.bfloat16)
    return hi, lo


def local_kernel(starts_ref, bins_ref, x_ref, w_ref, g_ref, y_ref, pay_ref,
                 xf, xs, st, bn, ta, tb, win, amat, *, nf, nb, nt, nm, nv, nx):
    nvx = nv * nx
    half = nm // 2
    rows = nt * nvx
    chunk = rows // 8

    for i in range(8):
        xf[i * chunk:(i + 1) * chunk, :] = x_ref[i * chunk:(i + 1) * chunk, :].astype(jnp.float32)
    sums = []
    for v in range(nv):
        acc = jnp.zeros((1, 128), jnp.float32)
        for k in range(nx):
            col = v * nx + k
            part = xf[pl.ds(col, nt, stride=nvx), :]
            xs[:, col * 128:(col + 1) * 128] = part.astype(jnp.bfloat16)
            sq = jnp.sum(part * part, axis=0, keepdims=True)
            acc = acc + sq * w_ref[col:col + 1, :]
        sums.append(jnp.sum(acc, axis=1, keepdims=True))
    lane = lax.broadcasted_iota(jnp.int32, (1, 128), 1)
    msq_row = jnp.zeros((1, 128), jnp.float32)
    for v in range(nv):
        for k, piece in enumerate(split3(sums[v])):
            msq_row = jnp.where(lane == k * nv + v, piece, msq_row)
    tail = jnp.concatenate([msq_row, jnp.zeros((16 - nv * half - 1, 128), jnp.float32)], axis=0)

    for b in range(nb):
        st[b:b + 1, :] = jnp.full((1, 128), starts_ref[b], jnp.int32)
    for f in range(nf):
        bn[f:f + 1, :] = jnp.full((1, 128), bins_ref[f], jnp.int32)
    bn[nf:nf + 8, :] = jnp.ones((8, 128), jnp.int32)
    unit = 2.0 * math.pi / NFFT
    times = lax.broadcasted_iota(jnp.int32, (nf + 8, nt), 1)
    phase = ((bn[:, :1] * times) & (NFFT - 1)).astype(jnp.float32) * unit
    ta[0] = jnp.cos(phase)
    ta[1] = jnp.sin(phase)
    bin_lane = jnp.ones((1, 128), jnp.int32)
    for f in range(nf):
        bin_lane = jnp.where(lane == f, bins_ref[f], bin_lane)
    phase_b = ((st[:, :1] * bin_lane) & (NFFT - 1)).astype(jnp.float32) * unit
    tb[0] = jnp.cos(phase_b)
    tb[1] = jnp.sin(phase_b)
    norm_c = 1.0 / math.sqrt(sum((0.5 - 0.5 * math.cos(unit * t)) ** 2 for t in range(NFFT)))
    since = lax.broadcasted_iota(jnp.int32, (nb, nt), 1) - st[:, :1]
    cosd = ta[0, nf:nf + 1, :] * tb[0, :, nf:nf + 1] + ta[1, nf:nf + 1, :] * tb[1, :, nf:nf + 1]
    inside = (since >= 0) & (since < NFFT)
    win[...] = jnp.where(inside, norm_c * (0.5 - 0.5 * cosd), 0.0)

    low = lax.broadcasted_iota(jnp.int32, (nm, 2 * nb), 1) < nb
    sqrt_w = [jnp.sqrt(w_ref[c:c + 1, :]) for c in range(nvx)]
    sqrt_w = jnp.concatenate(sqrt_w, axis=1)
    for f in range(nf):
        slot = f % 2
        ca = ta[0, f:f + 1, :]
        sa = ta[1, f:f + 1, :]
        cb = tb[0, :, f:f + 1]
        sb = tb[1, :, f:f + 1]
        ww = win[...]
        amat[slot, :nb, :] = (ww * (ca * cb + sa * sb)).astype(jnp.bfloat16)
        amat[slot, nb:, :] = (ww * (ca * sb - sa * cb)).astype(jnp.bfloat16)
        q = jnp.dot(amat[slot], xs[...], preferred_element_type=jnp.float32)
        yf = (q * sqrt_w).astype(jnp.bfloat16)
        y_ref[f] = yf
        pr = g_ref[f, 0]
        pi = g_ref[f, 1]
        upper = jnp.concatenate([pr, -pi], axis=1)
        lower = jnp.concatenate([pi, pr], axis=1)
        guess = jnp.concatenate([upper, lower], axis=0)
        ghi, glo = split2(guess)
        proj = jnp.dot(jnp.concatenate([ghi, glo], axis=0), yf, preferred_element_type=jnp.float32)
        proj = proj[:2 * nm] + proj[2 * nm:]
        phi, plo = split2(proj)
        pst = jnp.concatenate([phi, plo], axis=0)
        zs = []
        span = nx * 128
        for v in range(nv):
            r = lax.dot_general(pst[:, v * span:(v + 1) * span], yf[:, v * span:(v + 1) * span],
                                (((1,), (1,)), ((), ())), preferred_element_type=jnp.float32)
            r = r[:2 * nm] + r[2 * nm:]
            ru = r[:nm]
            rv = pltpu.roll(r[nm:], nb, 1)
            zs.append(jnp.where(low, ru, -ru) + rv)
        for h in range(2):
            block = jnp.concatenate([z[h * half:(h + 1) * half] for z in zs] + [tail], axis=0)
            pay_ref[2 * f + h] = block.astype(jnp.bfloat16)


def partial_kernel(r_ref, o_ref):
    total = jnp.sum(r_ref[...].astype(jnp.float32), axis=0)
    for i in range(o_ref.shape[0]):
        o_ref[i] = total


def owner_kernel(r_ref, o_ref, s_ref, *, nv, half, count, denom):
    total = jnp.sum(r_ref[...], axis=0)
    row = total[nv * half:nv * half + 1, :]
    lane = lax.broadcasted_iota(jnp.int32, (1, 128), 1)
    z = jnp.zeros((half, 128), jnp.float32)
    for v in range(nv):
        mine = (lane == v) | (lane == nv + v) | (lane == 2 * nv + v)
        msq = jnp.sum(jnp.where(mine, row, 0.0), axis=1, keepdims=True) / count
        scale = lax.rsqrt(msq + EPS)
        s_ref[v:v + 1, :] = jnp.broadcast_to(scale, (1, 128))
        z = z + total[v * half:(v + 1) * half, :] * (scale * scale)
    s_ref[nv:, :] = jnp.zeros((8 - nv, 128), jnp.float32)
    z = z / denom
    norms = jnp.sum(z * z, axis=1, keepdims=True)
    coef = z * lax.rsqrt(norms + EPS)
    lanes = lax.broadcasted_iota(jnp.int32, (half, 128), 1)
    extra = jnp.zeros((half, 128), jnp.float32)
    for k, piece in enumerate(split3(norms)):
        extra = jnp.where(lanes == k, piece, extra)
    block = jnp.concatenate([coef, extra], axis=0).astype(jnp.bfloat16)
    for i in range(o_ref.shape[0]):
        o_ref[i] = block


def modes_kernel(c_ref, s_ref, y_ref, o_ref, e_ref, *, nf, nb, nm, nv, nx):
    half = nm // 2
    nvx = nv * nx
    low = lax.broadcasted_iota(jnp.int32, (nm, 2 * nb), 1) < nb
    lane = lax.broadcasted_iota(jnp.int32, (nm, nf), 1)
    energy = jnp.zeros((nm, nf), jnp.float32)
    for f in range(nf):
        both = c_ref[2 * f:2 * f + 2].astype(jnp.float32)
        coef = jnp.concatenate([both[0, :half], both[1, :half]], axis=0)
        extra = jnp.concatenate([both[0, half:], both[1, half:]], axis=0)
        norm = extra[:, 0:1] + extra[:, 1:2] + extra[:, 2:3]
        energy = jnp.where(lane == f, norm, energy)
        left = jnp.concatenate([jnp.where(low, coef, -coef), pltpu.roll(coef, nb, 1)], axis=0)
        m = jnp.dot(left.astype(jnp.bfloat16), y_ref[f], preferred_element_type=jnp.float32)
        base = f * 2 * nm * nvx
        for c in range(nvx):
            v = c // nx
            o_ref[pl.ds(base + c, 2 * nm, stride=nvx), :] = (
                m[:, c * 128:(c + 1) * 128] * s_ref[v:v + 1, :])
    e_ref[...] = jnp.sqrt(energy / nb)


def shards(snapshots, quad_weight, mode_guess, bins, starts):
    nt, nv, nx, ny = snapshots.shape
    nf, nb, _, nm = mode_guess.shape
    nvx = nv * nx
    half = nm // 2
    grid_points = nx * ny * lax.axis_size(SX) * lax.axis_size(SY)
    owners = lax.axis_size(OWNERS)
    column = lax.axis_size(COLUMN)
    vmem = pl.BlockSpec(memory_space=pltpu.VMEM)
    smem = pl.BlockSpec(memory_space=pltpu.SMEM)
    params = pltpu.CompilerParams(vmem_limit_bytes=40 * MIB)

    x = snapshots.reshape(nt * nvx, ny)
    w = quad_weight.reshape(nvx, ny)
    guess = jnp.transpose(mode_guess, (0, 2, 3, 1))
    y, payload = pl.pallas_call(
        functools.partial(local_kernel, nf=nf, nb=nb, nt=nt, nm=nm, nv=nv, nx=nx),
        out_shape=(jax.ShapeDtypeStruct((nf, 2 * nb, nvx * ny), jnp.bfloat16),
                   jax.ShapeDtypeStruct((2 * nf, 16, 128), jnp.bfloat16)),
        in_specs=[smem, smem, vmem, vmem, vmem],
        out_specs=(vmem, vmem),
        scratch_shapes=[
            pltpu.VMEM((nt * nvx, ny), jnp.float32),
            pltpu.VMEM((nt, nvx * ny), jnp.bfloat16),
            pltpu.VMEM((nb, 128), jnp.int32),
            pltpu.VMEM((nf + 8, 128), jnp.int32),
            pltpu.VMEM((2, nf + 8, nt), jnp.float32),
            pltpu.VMEM((2, nb, 128), jnp.float32),
            pltpu.VMEM((nb, nt), jnp.float32),
            pltpu.VMEM((2, 2 * nb, nt), jnp.bfloat16),
        ],
        compiler_params=params,
        name="local_part",
    )(starts, bins, x, w, guess)
    received = lax.all_to_all(payload, OWNERS, 0, 0, tiled=True)
    copies = pl.pallas_call(
        partial_kernel,
        out_shape=jax.ShapeDtypeStruct((column, 16, 128), jnp.float32),
        in_specs=[vmem], out_specs=vmem, compiler_params=params, name="plane_sum",
    )(received)
    received = lax.all_to_all(copies, COLUMN, 0, 0, tiled=True)
    copies, scale = pl.pallas_call(
        functools.partial(owner_kernel, nv=nv, half=half, count=float(nt * grid_points),
                          denom=float(nv * grid_points)),
        out_shape=(jax.ShapeDtypeStruct((owners, 2 * half, 128), jnp.bfloat16),
                   jax.ShapeDtypeStruct((8, 128), jnp.float32)),
        in_specs=[vmem], out_specs=(vmem, vmem), compiler_params=params, name="owner_part",
    )(received)
    coef = lax.all_to_all(copies, OWNERS, 0, 0, tiled=True)
    modes, energy = pl.pallas_call(
        functools.partial(modes_kernel, nf=nf, nb=nb, nm=nm, nv=nv, nx=nx),
        out_shape=(jax.ShapeDtypeStruct((nf * 2 * nm * nvx, ny), jnp.float32),
                   jax.ShapeDtypeStruct((nm, nf), jnp.float32)),
        in_specs=[vmem, vmem, vmem], out_specs=(vmem, vmem), compiler_params=params,
        name="modes_part",
    )(coef, scale, y)
    return modes.reshape(nf, 2, nm, nv, nx, ny), energy.T


def solution(mesh):
    finer = Mesh(mesh.devices.reshape(2, 4, 4, 4, 2), AXES)
    placed = (P(None, None, SX, SY), P(None, SX, SY), P(), P(), P())
    return jax.shard_map(
        shards,
        mesh=finer,
        in_specs=placed,
        out_specs=(P(None, None, None, None, SX, SY), P()),
        check_vma=False,
    )
```

time: 262 us -> 60.1 us (0.23)
  local copies, waits for them, and re-layouts: 99.8 us -> 4.31 us
  matrix products: 31.5 us -> 0 us
  blocking collectives: 73.4 us -> 43.1 us
  waiting for transfers between devices: 30 us -> 0 us
  Pallas kernels: 0 us -> 11.8 us
  other arithmetic: 10.8 us -> 0 us
  starting transfers between devices: 8.7 us -> 0 us
  loops' own time: 5.28 us -> 0 us
    gather x8 -> x0, local copies, waits for them, and re-layouts: 75 us -> none  [block_step(): windows = jnp.take(flat, times, axis=0)]
    psum x5 -> x0, blocking collectives: 44.7 us -> none  [one_axis_at_a_time(): return functools.reduce(lax.psum, axes, x)]
    dot_general x13 -> x0, matrix products: 31.5 us -> none  [the longest x8 28.3 us: block_step(): jnp.einsum('qt,btx->bqx', twid, windows, preferred_element_type=jnp.float32)]
    all_to_all x2 -> x0, waiting for transfers between devices: 30 us -> none  [copy_for_each(): return lax.all_to_all(copies, axis, split_axis=0, concat_axis=0, tiled=True)]
    all_to_all x2 -> x3, blocking collectives: 28.7 us -> 43.1 us  [the longest x1 16.1 us: shards(): received = lax.all_to_all(payload, OWNERS, 0, 0, tiled=True)]
    pallas_call x0 -> x4, Pallas kernels: none -> 11.8 us  [the longest x1 10.1 us: shards(): pl.pallas_call(functools.partial(local_kernel, nf=nf, nb=nb, nt=nt, nm=nm...]
    reshape x2 -> x1, local copies, waits for them, and re-layouts: 11.2 us -> 0.69 us  [shards(): w = quad_weight.reshape(nvx, ny)]
    all_to_all x2 -> x0, starting transfers between devices: 8.7 us -> none  [copy_for_each(): return lax.all_to_all(copies, axis, split_axis=0, concat_axis=0, tiled=True)]
  transfers between devices with their start and end apart: 2 -> 0, of which waited for: 2 -> 0; matrix products, arithmetic and copies ran while one was open for 1% -> 0% of each run, Pallas kernels for 0% -> 0%
where the time goes in v1:
time: 60.1 us; the launch traced here: 59.8 us
  blocking collectives  43.1 us (72%)
  Pallas kernels  11.8 us (20%)
  local copies, waits for them, and re-layouts  4.31 us (7%)
  between operations  0.64 us (1%)
    all_to_all x1, blocking collectives, shards(): received = lax.all_to_all(payload, OWNERS, 0, 0, tiled=True)  16.1 us
    all_to_all x1, blocking collectives, shards(): received = lax.all_to_all(copies, COLUMN, 0, 0, tiled=True)  14.6 us
    all_to_all x1, blocking collectives, shards(): coef = lax.all_to_all(copies, OWNERS, 0, 0, tiled=True)  12.4 us
    pallas_call x1, Pallas kernels, shards(): pl.pallas_call(functools.partial(local_kernel, nf=nf, nb=nb, nt=nt, nm=nm...  10.1 us
    unnamed x8, local copies, waits for them, and re-layouts  3.62 us
    pallas_call x1, Pallas kernels, shards(): pl.pallas_call(functools.partial(modes_kernel, nf=nf, nb=nb, nm=nm, nv=nv...  1.46 us

profile of v1, /device:TPU:1, one launch (start us, length us, event | category | flops | bytes accessed | tf_op | source)
XLA Modules:
  0.0 59.8 jit_solution(15967680542296305157)
XLA Ops:
  0.6 0.7 %reshape.14.w_ref = f32[6,128]{1,0:T(8,128)S(1)} reshape(f32[3,2,128]{2,1,0:T(2,128)} %param.6) | data formatting | bytes 6144 | tf_op jit(solution)/shard_map/reshape | solution.py:187
  1.3 0.0 copy-start
  1.3 1.4 %copy-done = bf16[1024,3,2,128]{3,2,1,0:T(2,128)(2,1)S(1)} copy-done((bf16[1024,3,2,128]{3,2,1,0:T(2,128)(2,1)S(1)}, bf16[1024,3,2,128]{3,2,1,0:T(2,128)(2,1)}, u32[]{:S(2)}) %copy-start) | copy-done | bytes 1572888
  2.7 0.0 copy-start.1
  2.7 0.9 %copy-done.1 = f32[16,64,2,8]{1,3,2,0:T(8,128)S(1)} copy-done((f32[16,64,2,8]{1,3,2,0:T(8,128)S(1)}, f32[16,64,2,8]{1,3,2,0:T(8,128)}, u32[]{:S(2)}) %copy-start.1) | copy-done | bytes 65560
  3.6 0.0 copy-start.2
  3.6 0.7 %copy-done.2 = s32[64]{0:T(128)S(1)} copy-done((s32[64]{0:T(128)S(1)}, s32[64]{0:T(128)}, u32[]{:S(2)}) %copy-start.2) | copy-done | bytes 280
  4.3 0.0 copy-start.3
  4.3 0.7 %copy-done.3 = s32[16]{0:T(128)S(1)} copy-done((s32[16]{0:T(128)S(1)}, s32[16]{0:T(128)}, u32[]{:S(2)}) %copy-start.3) | copy-done | bytes 88
  4.9 10.1 %local_part.1 = (bf16[16,128,768]{2,1,0:T(8,128)(2,1)S(1)}, bf16[32,16,128]{2,1,0:T(8,128)(2,1)S(1)}) custom-call(s32[64]{0:T(128)S(1)} %copy-done.2, s32[16]{0:T(128)S(1)} %copy-done.3, bf16[6144,128]{1,0:T(8,128)(2,1)S(1)} %bitcast.4, f32[6,128]{1,0:T(8,128)S(1)} %reshape.14.w_ref, f32[16,2,8,64]{3,2,1,0:T(8,128)S(1)} %bitcast.5), custom_call_target="tpu_custom_call" | custom-call | tf_op jit(solution)/shard_map/local_part/pallas_call | solution.py:189
  15.0 16.1 %all_to_all.15.r_ref = bf16[32,16,128]{2,1,0:T(8,128)(2,1)S(1)} all-to-all(bf16[32,16,128]{2,1,0:T(8,128)(2,1)S(1)} %get-tuple-element.8), channel_id=1, replica_groups=mesh['sx_0'=2,'sx_1'=4,'sx_2'=4,'sy_0'=4,'sy_1'=2] {'sx_1','sx_2','sy_1'}, dimensions={0} | all-to-all | bytes 262144 | tf_op jit(solution)/shard_map/all_to_all | solution.py:208
  31.2 14.6 %all_to_all.16.r_ref = f32[8,16,128]{2,1,0:T(8,128)S(1)} all-to-all(f32[8,16,128]{2,1,0:T(8,128)S(1)} %plane_sum.1), channel_id=1, replica_groups=mesh['sx_0'=2,'sx_1'=4,'sx_2'=4,'sy_0'=4,'sy_1'=2] {'sx_0','sy_0'}, dimensions={0} | all-to-all | bytes 131072 | tf_op jit(solution)/shard_map/all_to_all | solution.py:214
  45.8 0.2 owner_part.1
  46.0 12.4 %all_to_all.17.c_ref = bf16[32,8,128]{2,1,0:T(8,128)(2,1)S(1)} all-to-all(bf16[32,8,128]{2,1,0:T(8,128)(2,1)S(1)} %get-tuple-element.9), channel_id=1, replica_groups=mesh['sx_0'=2,'sx_1'=4,'sx_2'=4,'sy_0'=4,'sy_1'=2] {'sx_1','sx_2','sy_1'}, dimensions={0} | all-to-all | bytes 131072 | tf_op jit(solution)/shard_map/all_to_all | solution.py:222
  58.4 1.5 %modes_part.1 = (f32[1536,128]{1,0:T(8,128)}, f32[8,16]{1,0:T(8,128)}) custom-call(bf16[32,8,128]{2,1,0:T(8,128)(2,1)S(1)} %all_to_all.17.c_ref, f32[8,128]{1,0:T(8,128)S(1)} %get-tuple-element.10.s_ref, bf16[16,128,768]{2,1,0:T(8,128)(2,1)S(1)} %get-tuple-element.11.y_ref), custom_call_target="tpu_custom_call" | custom-call | tf_op jit(solution)/shard_map/modes_part/pallas_call | solution.py:223
  (1 shorter events, 0.0 us)
Async XLA Ops:
  1.3 1.4 %copy-start = (bf16[1024,3,2,128]{3,2,1,0:T(2,128)(2,1)S(1)}, bf16[1024,3,2,128]{3,2,1,0:T(2,128)(2,1)}, u32[]{:S(2)}) copy-start(bf16[1024,3,2,128]{3,2,1,0:T(2,128)(2,1)} %param.5) | copy-start | bytes 4718596
  2.7 0.9 %copy-start.1 = (f32[16,64,2,8]{1,3,2,0:T(8,128)S(1)}, f32[16,64,2,8]{1,3,2,0:T(8,128)}, u32[]{:S(2)}) copy-start(f32[16,64,2,8]{1,3,2,0:T(8,128)} %param.7) | copy-start | bytes 196612
  3.6 0.7 %copy-start.2 = (s32[64]{0:T(128)S(1)}, s32[64]{0:T(128)}, u32[]{:S(2)}) copy-start(s32[64]{0:T(128)} %starts_ref.1) | copy-start | bytes 772
  4.3 0.7 %copy-start.3 = (s32[16]{0:T(128)S(1)}, s32[16]{0:T(128)}, u32[]{:S(2)}) copy-start(s32[16]{0:T(128)} %bins_ref.1) | copy-start | bytes 196

commit v2 on v1

--- a/solution.py
+++ b/solution.py
@@ -32,32 +32,27 @@
     return hi, lo
 
 
-def local_kernel(starts_ref, bins_ref, x_ref, w_ref, g_ref, y_ref, pay_ref,
-                 xf, xs, st, bn, ta, tb, win, amat, *, nf, nb, nt, nm, nv, nx):
+def local_kernel(starts_hbm, bins_hbm, x_hbm, w_hbm, g_hbm, y_ref, pay_ref,
+                 xb, xf, xs, wv, gv, st, bn, ta, tb, win, amat, starts_ref, bins_ref, sems,
+                 *, nf, nb, nt, nm, nv, nx):
     nvx = nv * nx
     half = nm // 2
     rows = nt * nvx
-    chunk = rows // 8
-
-    for i in range(8):
-        xf[i * chunk:(i + 1) * chunk, :] = x_ref[i * chunk:(i + 1) * chunk, :].astype(jnp.float32)
-    sums = []
-    for v in range(nv):
-        acc = jnp.zeros((1, 128), jnp.float32)
-        for k in range(nx):
-            col = v * nx + k
-            part = xf[pl.ds(col, nt, stride=nvx), :]
-            xs[:, col * 128:(col + 1) * 128] = part.astype(jnp.bfloat16)
-            sq = jnp.sum(part * part, axis=0, keepdims=True)
-            acc = acc + sq * w_ref[col:col + 1, :]
-        sums.append(jnp.sum(acc, axis=1, keepdims=True))
+    nchunk = xb.shape[0]
+    chunk = rows // nchunk
+
+    copies = [pltpu.make_async_copy(starts_hbm, starts_ref, sems.at[0]),
+              pltpu.make_async_copy(bins_hbm, bins_ref, sems.at[1]),
+              pltpu.make_async_copy(w_hbm, wv, sems.at[2]),
+              pltpu.make_async_copy(g_hbm, gv, sems.at[3])]
+    pieces = [pltpu.make_async_copy(x_hbm.at[pl.ds(i * chunk, chunk)], xb.at[i], sems.at[4 + i])
+              for i in range(nchunk)]
+    for c in copies[:2] + pieces + copies[2:]:
+        c.start()
+    copies[0].wait()
+    copies[1].wait()
+
     lane = lax.broadcasted_iota(jnp.int32, (1, 128), 1)
-    msq_row = jnp.zeros((1, 128), jnp.float32)
-    for v in range(nv):
-        for k, piece in enumerate(split3(sums[v])):
-            msq_row = jnp.where(lane == k * nv + v, piece, msq_row)
-    tail = jnp.concatenate([msq_row, jnp.zeros((16 - nv * half - 1, 128), jnp.float32)], axis=0)
-
     for b in range(nb):
         st[b:b + 1, :] = jnp.full((1, 128), starts_ref[b], jnp.int32)
     for f in range(nf):
@@ -80,43 +75,81 @@
     inside = (since >= 0) & (since < NFFT)
     win[...] = jnp.where(inside, norm_c * (0.5 - 0.5 * cosd), 0.0)
 
+    for i in range(nchunk):
+        pieces[i].wait()
+        xf[i * chunk:(i + 1) * chunk, :] = xb[i].astype(jnp.float32)
+    copies[2].wait()
+    copies[3].wait()
+    sums = []
+    for v in range(nv):
+        acc = jnp.zeros((1, 128), jnp.float32)
+        for k in range(nx):
+            col = v * nx + k
+            part = xf[pl.ds(col, nt, stride=nvx), :]
+            xs[:, col * 128:(col + 1) * 128] = part.astype(jnp.bfloat16)
+            sq = jnp.sum(part * part, axis=0, keepdims=True)
+            acc = acc + sq * wv[v, k:k + 1, :]
+        sums.append(jnp.sum(acc, axis=1, keepdims=True))
+    msq_row = jnp.zeros((1, 128), jnp.float32)
+    for v in range(nv):
+        for k, piece in enumerate(split3(sums[v])):
+            msq_row = jnp.where(lane == k * nv + v, piece, msq_row)
+    tail = jnp.concatenate([msq_row, jnp.zeros((16 - nv * half - 1, 128), jnp.float32)], axis=0)
+
     low = lax.broadcasted_iota(jnp.int32, (nm, 2 * nb), 1) < nb
-    sqrt_w = [jnp.sqrt(w_ref[c:c + 1, :]) for c in range(nvx)]
-    sqrt_w = jnp.concatenate(sqrt_w, axis=1)
-    for f in range(nf):
-        slot = f % 2
-        ca = ta[0, f:f + 1, :]
-        sa = ta[1, f:f + 1, :]
-        cb = tb[0, :, f:f + 1]
-        sb = tb[1, :, f:f + 1]
-        ww = win[...]
-        amat[slot, :nb, :] = (ww * (ca * cb + sa * sb)).astype(jnp.bfloat16)
-        amat[slot, nb:, :] = (ww * (ca * sb - sa * cb)).astype(jnp.bfloat16)
+    sqrt_w = jnp.concatenate([jnp.sqrt(wv[c // nx, c % nx:c % nx + 1, :]) for c in range(nvx)], axis=1)
+    span = nx * 128
+    zeros = jnp.zeros((2 * nm, 2 * nb), jnp.float32)
+
+    def transform(j):
+        slot = j % 2
+        for i in range(2):
+            f = 2 * j + i
+            ca = ta[0, f:f + 1, :]
+            sa = ta[1, f:f + 1, :]
+            cb = tb[0, :, f:f + 1]
+            sb = tb[1, :, f:f + 1]
+            ww = win[...]
+            base = i * 2 * nb
+            amat[slot, base:base + nb, :] = (ww * (ca * cb + sa * sb)).astype(jnp.bfloat16)
+            amat[slot, base + nb:base + 2 * nb, :] = (ww * (ca * sb - sa * cb)).astype(jnp.bfloat16)
         q = jnp.dot(amat[slot], xs[...], preferred_element_type=jnp.float32)
-        yf = (q * sqrt_w).astype(jnp.bfloat16)
-        y_ref[f] = yf
-        pr = g_ref[f, 0]
-        pi = g_ref[f, 1]
-        upper = jnp.concatenate([pr, -pi], axis=1)
-        lower = jnp.concatenate([pi, pr], axis=1)
-        guess = jnp.concatenate([upper, lower], axis=0)
-        ghi, glo = split2(guess)
+        y_ref[4 * nb * j:4 * nb * (j + 1), :] = (q * sqrt_w).astype(jnp.bfloat16)
+
+    def project(j):
+        yf = y_ref[4 * nb * j:4 * nb * (j + 1), :]
+        both = []
+        for i in range(2):
+            pr = gv[2 * j + i, 0]
+            pi = gv[2 * j + i, 1]
+            guess = jnp.concatenate([jnp.concatenate([pr, -pi], axis=1),
+                                     jnp.concatenate([pi, pr], axis=1)], axis=0)
+            both.append(jnp.concatenate([guess, zeros] if i == 0 else [zeros, guess], axis=1))
+        ghi, glo = split2(jnp.concatenate(both, axis=0))
         proj = jnp.dot(jnp.concatenate([ghi, glo], axis=0), yf, preferred_element_type=jnp.float32)
-        proj = proj[:2 * nm] + proj[2 * nm:]
+        proj = proj[:4 * nm] + proj[4 * nm:]
         phi, plo = split2(proj)
         pst = jnp.concatenate([phi, plo], axis=0)
-        zs = []
-        span = nx * 128
+        zs = [[], []]
         for v in range(nv):
             r = lax.dot_general(pst[:, v * span:(v + 1) * span], yf[:, v * span:(v + 1) * span],
                                 (((1,), (1,)), ((), ())), preferred_element_type=jnp.float32)
-            r = r[:2 * nm] + r[2 * nm:]
-            ru = r[:nm]
-            rv = pltpu.roll(r[nm:], nb, 1)
-            zs.append(jnp.where(low, ru, -ru) + rv)
-        for h in range(2):
-            block = jnp.concatenate([z[h * half:(h + 1) * half] for z in zs] + [tail], axis=0)
-            pay_ref[2 * f + h] = block.astype(jnp.bfloat16)
+            r = r[:4 * nm] + r[4 * nm:]
+            for i in range(2):
+                part = r[i * 2 * nm:(i + 1) * 2 * nm, i * 2 * nb:(i + 1) * 2 * nb]
+                ru = part[:nm]
+                rv = pltpu.roll(part[nm:], nb, 1)
+                zs[i].append(jnp.where(low, ru, -ru) + rv)
+        for i in range(2):
+            for h in range(2):
+                block = jnp.concatenate([z[h * half:(h + 1) * half] for z in zs[i]] + [tail], axis=0)
+                pay_ref[2 * (2 * j + i) + h] = block.astype(jnp.bfloat16)
+
+    transform(0)
+    for j in range(1, nf // 2):
+        transform(j)
+        project(j - 1)
+    project(nf // 2 - 1)
 
 
 def partial_kernel(r_ref, o_ref):
@@ -162,7 +195,7 @@
         norm = extra[:, 0:1] + extra[:, 1:2] + extra[:, 2:3]
         energy = jnp.where(lane == f, norm, energy)
         left = jnp.concatenate([jnp.where(low, coef, -coef), pltpu.roll(coef, nb, 1)], axis=0)
-        m = jnp.dot(left.astype(jnp.bfloat16), y_ref[f], preferred_element_type=jnp.float32)
+        m = jnp.dot(left.astype(jnp.bfloat16), y_ref[2 * nb * f:2 * nb * (f + 1), :], preferred_element_type=jnp.float32)
         base = f * 2 * nm * nvx
         for c in range(nvx):
             v = c // nx
@@ -180,31 +213,37 @@
     owners = lax.axis_size(OWNERS)
     column = lax.axis_size(COLUMN)
     vmem = pl.BlockSpec(memory_space=pltpu.VMEM)
-    smem = pl.BlockSpec(memory_space=pltpu.SMEM)
+    hbm = pl.BlockSpec(memory_space=pltpu.HBM)
     params = pltpu.CompilerParams(vmem_limit_bytes=40 * MIB)
 
     x = snapshots.reshape(nt * nvx, ny)
-    w = quad_weight.reshape(nvx, ny)
     guess = jnp.transpose(mode_guess, (0, 2, 3, 1))
+    nchunk = 4
     y, payload = pl.pallas_call(
         functools.partial(local_kernel, nf=nf, nb=nb, nt=nt, nm=nm, nv=nv, nx=nx),
-        out_shape=(jax.ShapeDtypeStruct((nf, 2 * nb, nvx * ny), jnp.bfloat16),
+        out_shape=(jax.ShapeDtypeStruct((nf * 2 * nb, nvx * ny), jnp.bfloat16),
                    jax.ShapeDtypeStruct((2 * nf, 16, 128), jnp.bfloat16)),
-        in_specs=[smem, smem, vmem, vmem, vmem],
+        in_specs=[hbm] * 5,
         out_specs=(vmem, vmem),
         scratch_shapes=[
+            pltpu.VMEM((nchunk, nt * nvx // nchunk, ny), jnp.bfloat16),
             pltpu.VMEM((nt * nvx, ny), jnp.float32),
             pltpu.VMEM((nt, nvx * ny), jnp.bfloat16),
+            pltpu.VMEM((nv, nx, ny), jnp.float32),
+            pltpu.VMEM((nf, 2, nm, nb), jnp.float32),
             pltpu.VMEM((nb, 128), jnp.int32),
             pltpu.VMEM((nf + 8, 128), jnp.int32),
             pltpu.VMEM((2, nf + 8, nt), jnp.float32),
             pltpu.VMEM((2, nb, 128), jnp.float32),
             pltpu.VMEM((nb, nt), jnp.float32),
-            pltpu.VMEM((2, 2 * nb, nt), jnp.bfloat16),
+            pltpu.VMEM((2, 4 * nb, nt), jnp.bfloat16),
+            pltpu.SMEM((nb,), jnp.int32),
+            pltpu.SMEM((nf,), jnp.int32),
+            pltpu.SemaphoreType.DMA((4 + nchunk,)),
         ],
         compiler_params=params,
         name="local_part",
-    )(starts, bins, x, w, guess)
+    )(*[pltpu.with_memory_space_constraint(a, pltpu.HBM) for a in (starts, bins, x, quad_weight, guess)])
     received = lax.all_to_all(payload, OWNERS, 0, 0, tiled=True)
     copies = pl.pallas_call(
         partial_kernel,

time: 60.1 us -> 52.6 us (0.88)
  local copies, waits for them, and re-layouts: 4.31 us -> 0 us
  Pallas kernels: 11.8 us -> 8.66 us
    unnamed x8 -> x0, local copies, waits for them, and re-layouts: 3.62 us -> none
    pallas_call x1, Pallas kernels: 10.1 us -> 6.97 us  [shards(): pl.pallas_call(functools.partial(local_kernel, nf=nf, nb=nb, nt=nt, nm=nm...]
    reshape x1 -> x0, local copies, waits for them, and re-layouts: 0.69 us -> none  [shards(): w = quad_weight.reshape(nvx, ny)]
where the time goes in v2:
time: 52.6 us; the launch traced here: 52.4 us
  blocking collectives  43.1 us (82%)
  Pallas kernels  8.66 us (16%)
  between operations  0.64 us (1%)
    all_to_all x1, blocking collectives, shards(): received = lax.all_to_all(payload, OWNERS, 0, 0, tiled=True)  16.1 us
    all_to_all x1, blocking collectives, shards(): received = lax.all_to_all(copies, COLUMN, 0, 0, tiled=True)  14.6 us
    all_to_all x1, blocking collectives, shards(): coef = lax.all_to_all(copies, OWNERS, 0, 0, tiled=True)  12.4 us
    pallas_call x1, Pallas kernels, shards(): pl.pallas_call(functools.partial(local_kernel, nf=nf, nb=nb, nt=nt, nm=nm...  6.97 us
    pallas_call x1, Pallas kernels, shards(): pl.pallas_call(functools.partial(modes_kernel, nf=nf, nb=nb, nm=nm, nv=nv...  1.46 us

profile of v2, /device:TPU:1, one launch (start us, length us, event | category | flops | bytes accessed | tf_op | source)
XLA Modules:
  0.0 52.4 jit_solution(8201722102852061984)
XLA Ops:
  0.6 7.0 %local_part.1 = (bf16[2048,768]{1,0:T(8,128)(2,1)S(1)}, bf16[32,16,128]{2,1,0:T(8,128)(2,1)S(1)}) custom-call(s32[64]{0:T(128)} %starts_hbm.1, s32[16]{0:T(128)} %bins_hbm.1, bf16[6144,128]{1,0:T(8,128)(2,1)} %bitcast.4, f32[3,2,128]{2,1,0:T(2,128)} %w_hbm.1, f32[16,2,8,64]{3,2,1,0:T(8,128)} %bitcast.5), custom_call_target="tpu_custom_call" | custom-call | tf_op jit(solution)/shard_map/local_part/pallas_call | solution.py:222
  7.6 16.1 %all_to_all.15.r_ref = bf16[32,16,128]{2,1,0:T(8,128)(2,1)S(1)} all-to-all(bf16[32,16,128]{2,1,0:T(8,128)(2,1)S(1)} %get-tuple-element.8), channel_id=1, replica_groups=mesh['sx_0'=2,'sx_1'=4,'sx_2'=4,'sy_0'=4,'sy_1'=2] {'sx_1','sx_2','sy_1'}, dimensions={0} | all-to-all | bytes 262144 | tf_op jit(solution)/shard_map/all_to_all | solution.py:247
  23.7 14.6 %all_to_all.16.r_ref = f32[8,16,128]{2,1,0:T(8,128)S(1)} all-to-all(f32[8,16,128]{2,1,0:T(8,128)S(1)} %plane_sum.1), channel_id=1, replica_groups=mesh['sx_0'=2,'sx_1'=4,'sx_2'=4,'sy_0'=4,'sy_1'=2] {'sx_0','sy_0'}, dimensions={0} | all-to-all | bytes 131072 | tf_op jit(solution)/shard_map/all_to_all | solution.py:253
  38.4 0.2 owner_part.1
  38.5 12.4 %all_to_all.17.c_ref = bf16[32,8,128]{2,1,0:T(8,128)(2,1)S(1)} all-to-all(bf16[32,8,128]{2,1,0:T(8,128)(2,1)S(1)} %get-tuple-element.9), channel_id=1, replica_groups=mesh['sx_0'=2,'sx_1'=4,'sx_2'=4,'sy_0'=4,'sy_1'=2] {'sx_1','sx_2','sy_1'}, dimensions={0} | all-to-all | bytes 131072 | tf_op jit(solution)/shard_map/all_to_all | solution.py:261
  50.9 1.5 %modes_part.1 = (f32[1536,128]{1,0:T(8,128)}, f32[8,16]{1,0:T(8,128)}) custom-call(bf16[32,8,128]{2,1,0:T(8,128)(2,1)S(1)} %all_to_all.17.c_ref, f32[8,128]{1,0:T(8,128)S(1)} %get-tuple-element.10.s_ref, bf16[2048,768]{1,0:T(8,128)(2,1)S(1)} %get-tuple-element.11.y_ref), custom_call_target="tpu_custom_call" | custom-call | tf_op jit(solution)/shard_map/modes_part/pallas_call | solution.py:262
  (1 shorter events, 0.0 us)

commit v3 on v2

--- a/solution.py
+++ b/solution.py
@@ -14,8 +14,12 @@
 AXES = ("sx_0", "sx_1", "sx_2", "sy_0", "sy_1")
 SX = AXES[:3]
 SY = AXES[3:]
-OWNERS = ("sx_1", "sx_2", "sy_1")
-COLUMN = ("sx_0", "sy_0")
+NEAR4 = ((0, 1), (1, 0), (2, 3), (3, 2))
+RING4 = ((0, 3), (3, 0), (1, 2), (2, 1))
+PAIR = ((0, 1), (1, 0))
+STAGES = (("sx_0", PAIR), ("sx_1", NEAR4), ("sx_2", NEAR4), ("sx_1", RING4), ("sx_2", RING4),
+          ("sy_0", NEAR4), ("sy_0", RING4))
+CORE = "sy_1"
 MIB = 1 << 20
 
 
@@ -32,12 +36,24 @@
     return hi, lo
 
 
-def local_kernel(starts_hbm, bins_hbm, x_hbm, w_hbm, g_hbm, y_ref, pay_ref,
+TAIL = 16
+
+
+def as_rows(row):
+    parts = split3(row)
+    return jnp.concatenate(list(parts) + [jnp.zeros((TAIL - 3, 128), jnp.float32)], axis=0).astype(jnp.bfloat16)
+
+
+def from_rows(tile):
+    return tile[0:1] + tile[1:2] + tile[2:3]
+
+
+def local_kernel(starts_hbm, bins_hbm, x_hbm, w_hbm, g_hbm, y_ref, mine_ref, other_ref,
                  xb, xf, xs, wv, gv, st, bn, ta, tb, win, amat, starts_ref, bins_ref, sems,
                  *, nf, nb, nt, nm, nv, nx):
     nvx = nv * nx
-    half = nm // 2
     rows = nt * nvx
+    core = lax.axis_index(CORE)
     nchunk = xb.shape[0]
     chunk = rows // nchunk
 
@@ -90,11 +106,12 @@
             sq = jnp.sum(part * part, axis=0, keepdims=True)
             acc = acc + sq * wv[v, k:k + 1, :]
         sums.append(jnp.sum(acc, axis=1, keepdims=True))
-    msq_row = jnp.zeros((1, 128), jnp.float32)
+    msq = jnp.zeros((1, 128), jnp.float32)
     for v in range(nv):
-        for k, piece in enumerate(split3(sums[v])):
-            msq_row = jnp.where(lane == k * nv + v, piece, msq_row)
-    tail = jnp.concatenate([msq_row, jnp.zeros((16 - nv * half - 1, 128), jnp.float32)], axis=0)
+        msq = jnp.where(lane == v, sums[v], msq)
+    tail = as_rows(msq)
+    mine_ref[mine_ref.shape[0] - TAIL:, :] = tail
+    other_ref[other_ref.shape[0] - TAIL:, :] = tail
 
     low = lax.broadcasted_iota(jnp.int32, (nm, 2 * nb), 1) < nb
     sqrt_w = jnp.concatenate([jnp.sqrt(wv[c // nx, c % nx:c % nx + 1, :]) for c in range(nvx)], axis=1)
@@ -140,10 +157,16 @@
                 ru = part[:nm]
                 rv = pltpu.roll(part[nm:], nb, 1)
                 zs[i].append(jnp.where(low, ru, -ru) + rv)
-        for i in range(2):
-            for h in range(2):
-                block = jnp.concatenate([z[h * half:(h + 1) * half] for z in zs[i]] + [tail], axis=0)
-                pay_ref[2 * (2 * j + i) + h] = block.astype(jnp.bfloat16)
+        npair = nf // 4
+        base = (j % npair) * nv * 2 * nm
+
+        def put(ref):
+            for v in range(nv):
+                block = jnp.concatenate([zs[0][v], zs[1][v]], axis=0).astype(jnp.bfloat16)
+                ref[base + v * 2 * nm:base + (v + 1) * 2 * nm, :] = block
+
+        pl.when(core == j // npair)(lambda: put(mine_ref))
+        pl.when(core != j // npair)(lambda: put(other_ref))
 
     transform(0)
     for j in range(1, nf // 2):
@@ -152,50 +175,60 @@
     project(nf // 2 - 1)
 
 
-def partial_kernel(r_ref, o_ref):
-    total = jnp.sum(r_ref[...].astype(jnp.float32), axis=0)
-    for i in range(o_ref.shape[0]):
-        o_ref[i] = total
-
-
-def owner_kernel(r_ref, o_ref, s_ref, *, nv, half, count, denom):
-    total = jnp.sum(r_ref[...], axis=0)
-    row = total[nv * half:nv * half + 1, :]
-    lane = lax.broadcasted_iota(jnp.int32, (1, 128), 1)
-    z = jnp.zeros((half, 128), jnp.float32)
+def add_kernel(a_ref, b_ref, o_ref):
+    cut = o_ref.shape[0] - TAIL
+    total = a_ref[...].astype(jnp.float32) + b_ref[...].astype(jnp.float32)
+    o_ref[:cut, :] = total[:cut].astype(jnp.bfloat16)
+    o_ref[cut:, :] = as_rows(from_rows(total[cut:]))
+
+
+def owner_kernel(a_ref, b_ref, o_ref, s_ref, *, nv, nm, count, denom):
+    cut = a_ref.shape[0] - TAIL
+    total = a_ref[...].astype(jnp.float32) + b_ref[...].astype(jnp.float32)
+    msq = from_rows(total[cut:])
+    scales = []
     for v in range(nv):
-        mine = (lane == v) | (lane == nv + v) | (lane == 2 * nv + v)
-        msq = jnp.sum(jnp.where(mine, row, 0.0), axis=1, keepdims=True) / count
-        scale = lax.rsqrt(msq + EPS)
-        s_ref[v:v + 1, :] = jnp.broadcast_to(scale, (1, 128))
-        z = z + total[v * half:(v + 1) * half, :] * (scale * scale)
+        scale = lax.rsqrt(jnp.broadcast_to(msq[:, v:v + 1], (1, 128)) / count + EPS)
+        s_ref[v:v + 1, :] = scale
+        scales.append(scale * scale)
     s_ref[nv:, :] = jnp.zeros((8 - nv, 128), jnp.float32)
-    z = z / denom
-    norms = jnp.sum(z * z, axis=1, keepdims=True)
-    coef = z * lax.rsqrt(norms + EPS)
-    lanes = lax.broadcasted_iota(jnp.int32, (half, 128), 1)
-    extra = jnp.zeros((half, 128), jnp.float32)
-    for k, piece in enumerate(split3(norms)):
-        extra = jnp.where(lanes == k, piece, extra)
-    block = jnp.concatenate([coef, extra], axis=0).astype(jnp.bfloat16)
-    for i in range(o_ref.shape[0]):
-        o_ref[i] = block
-
-
-def modes_kernel(c_ref, s_ref, y_ref, o_ref, e_ref, *, nf, nb, nm, nv, nx):
-    half = nm // 2
+    step = 2 * nm
+    lanes = lax.broadcasted_iota(jnp.int32, (step, 128), 1)
+    rows = cut // nv
+    for j in range(rows // step):
+        z = jnp.zeros((step, 128), jnp.float32)
+        for v in range(nv):
+            base = (j * nv + v) * step
+            z = z + total[base:base + step] * scales[v]
+        z = z / denom
+        norms = jnp.sum(z * z, axis=1, keepdims=True)
+        o_ref[j * step:(j + 1) * step, :] = (z * lax.rsqrt(norms + EPS)).astype(jnp.bfloat16)
+        extra = jnp.zeros((step, 128), jnp.float32)
+        for k, piece in enumerate(split3(norms)):
+            extra = jnp.where(lanes == k, piece, extra)
+        o_ref[rows + j * step:rows + (j + 1) * step, :] = extra.astype(jnp.bfloat16)
+
+
+def modes_kernel(mine_ref, other_ref, s_ref, y_ref, o_ref, e_ref, *, nf, nb, nm, nv, nx):
     nvx = nv * nx
+    core = lax.axis_index(CORE)
+    first = core == 0
+    mine = mine_ref[...].astype(jnp.float32)
+    other = other_ref[...].astype(jnp.float32)
+    halves = (jnp.where(first, mine, other), jnp.where(first, other, mine))
+    rows = mine.shape[0] // 2
     low = lax.broadcasted_iota(jnp.int32, (nm, 2 * nb), 1) < nb
     lane = lax.broadcasted_iota(jnp.int32, (nm, nf), 1)
     energy = jnp.zeros((nm, nf), jnp.float32)
     for f in range(nf):
-        both = c_ref[2 * f:2 * f + 2].astype(jnp.float32)
-        coef = jnp.concatenate([both[0, :half], both[1, :half]], axis=0)
-        extra = jnp.concatenate([both[0, half:], both[1, half:]], axis=0)
-        norm = extra[:, 0:1] + extra[:, 1:2] + extra[:, 2:3]
-        energy = jnp.where(lane == f, norm, energy)
+        part = halves[f // (nf // 2)]
+        at = (f % (nf // 2)) * nm
+        coef = part[at:at + nm]
+        extra = part[rows + at:rows + at + nm]
+        energy = jnp.where(lane == f, extra[:, 0:1] + extra[:, 1:2] + extra[:, 2:3], energy)
         left = jnp.concatenate([jnp.where(low, coef, -coef), pltpu.roll(coef, nb, 1)], axis=0)
-        m = jnp.dot(left.astype(jnp.bfloat16), y_ref[2 * nb * f:2 * nb * (f + 1), :], preferred_element_type=jnp.float32)
+        m = jnp.dot(left.astype(jnp.bfloat16), y_ref[2 * nb * f:2 * nb * (f + 1), :],
+                    preferred_element_type=jnp.float32)
         base = f * 2 * nm * nvx
         for c in range(nvx):
             v = c // nx
@@ -208,10 +241,7 @@
     nt, nv, nx, ny = snapshots.shape
     nf, nb, _, nm = mode_guess.shape
     nvx = nv * nx
-    half = nm // 2
     grid_points = nx * ny * lax.axis_size(SX) * lax.axis_size(SY)
-    owners = lax.axis_size(OWNERS)
-    column = lax.axis_size(COLUMN)
     vmem = pl.BlockSpec(memory_space=pltpu.VMEM)
     hbm = pl.BlockSpec(memory_space=pltpu.HBM)
     params = pltpu.CompilerParams(vmem_limit_bytes=40 * MIB)
@@ -219,12 +249,14 @@
     x = snapshots.reshape(nt * nvx, ny)
     guess = jnp.transpose(mode_guess, (0, 2, 3, 1))
     nchunk = 4
-    y, payload = pl.pallas_call(
+    packed = nf // 2 * nv * nm + TAIL
+    y, mine, other = pl.pallas_call(
         functools.partial(local_kernel, nf=nf, nb=nb, nt=nt, nm=nm, nv=nv, nx=nx),
         out_shape=(jax.ShapeDtypeStruct((nf * 2 * nb, nvx * ny), jnp.bfloat16),
-                   jax.ShapeDtypeStruct((2 * nf, 16, 128), jnp.bfloat16)),
+                   jax.ShapeDtypeStruct((packed, 128), jnp.bfloat16),
+                   jax.ShapeDtypeStruct((packed, 128), jnp.bfloat16)),
         in_specs=[hbm] * 5,
-        out_specs=(vmem, vmem),
+        out_specs=(vmem, vmem, vmem),
         scratch_shapes=[
             pltpu.VMEM((nchunk, nt * nvx // nchunk, ny), jnp.bfloat16),
             pltpu.VMEM((nt * nvx, ny), jnp.float32),
@@ -244,28 +276,29 @@
         compiler_params=params,
         name="local_part",
     )(*[pltpu.with_memory_space_constraint(a, pltpu.HBM) for a in (starts, bins, x, quad_weight, guess)])
-    received = lax.all_to_all(payload, OWNERS, 0, 0, tiled=True)
-    copies = pl.pallas_call(
-        partial_kernel,
-        out_shape=jax.ShapeDtypeStruct((column, 16, 128), jnp.float32),
-        in_specs=[vmem], out_specs=vmem, compiler_params=params, name="plane_sum",
-    )(received)
-    received = lax.all_to_all(copies, COLUMN, 0, 0, tiled=True)
-    copies, scale = pl.pallas_call(
-        functools.partial(owner_kernel, nv=nv, half=half, count=float(nt * grid_points),
+    received = lax.ppermute(other, CORE, PAIR)
+    for axis, pairs in STAGES:
+        mine = pl.pallas_call(
+            add_kernel,
+            out_shape=jax.ShapeDtypeStruct((packed, 128), jnp.bfloat16),
+            in_specs=[vmem, vmem], out_specs=vmem, compiler_params=params, name="add_partials",
+        )(mine, received)
+        received = lax.ppermute(mine, axis, pairs)
+    coef, scale = pl.pallas_call(
+        functools.partial(owner_kernel, nv=nv, nm=nm, count=float(nt * grid_points),
                           denom=float(nv * grid_points)),
-        out_shape=(jax.ShapeDtypeStruct((owners, 2 * half, 128), jnp.bfloat16),
+        out_shape=(jax.ShapeDtypeStruct((nf * nm, 128), jnp.bfloat16),
                    jax.ShapeDtypeStruct((8, 128), jnp.float32)),
-        in_specs=[vmem], out_specs=(vmem, vmem), compiler_params=params, name="owner_part",
-    )(received)
-    coef = lax.all_to_all(copies, OWNERS, 0, 0, tiled=True)
+        in_specs=[vmem, vmem], out_specs=(vmem, vmem), compiler_params=params, name="owner_part",
+    )(mine, received)
+    coef_other = lax.ppermute(coef, CORE, PAIR)
     modes, energy = pl.pallas_call(
         functools.partial(modes_kernel, nf=nf, nb=nb, nm=nm, nv=nv, nx=nx),
         out_shape=(jax.ShapeDtypeStruct((nf * 2 * nm * nvx, ny), jnp.float32),
                    jax.ShapeDtypeStruct((nm, nf), jnp.float32)),
-        in_specs=[vmem, vmem, vmem], out_specs=(vmem, vmem), compiler_params=params,
+        in_specs=[vmem] * 4, out_specs=(vmem, vmem), compiler_params=params,
         name="modes_part",
-    )(coef, scale, y)
+    )(coef, coef_other, scale, y)
     return modes.reshape(nf, 2, nm, nv, nx, ny), energy.T
 
 

time: 52.6 us -> 52.7 us (level)
  blocking collectives: 43.1 us -> 0 us
  waiting for transfers between devices: 0 us -> 22 us
  starting transfers between devices: 0 us -> 19.1 us
  Pallas kernels: 8.66 us -> 10.9 us
    all_to_all x3 -> x0, blocking collectives: 43.1 us -> none  [the longest x1 16.1 us: shards(): received = lax.all_to_all(payload, OWNERS, 0, 0, tiled=True)]
    ppermute x0 -> x9, waiting for transfers between devices: none -> 22 us  [the longest x7 20.2 us: shards(): received = lax.ppermute(mine, axis, pairs)]
    ppermute x0 -> x9, starting transfers between devices: none -> 19.1 us  [the longest x1 7.98 us: shards(): coef_other = lax.ppermute(coef, CORE, PAIR)]
    pallas_call x1, Pallas kernels: 6.97 us -> 9.05 us  [shards(): pl.pallas_call(functools.partial(local_kernel, nf=nf, nb=nb, nt=nt, nm=nm...]
  transfers between devices with their start and end apart: 0 -> 9, of which waited for: 0 -> 9; matrix products, arithmetic and copies ran while one was open for 0% -> 0% of each run, Pallas kernels for 0% -> 0%
where the time goes in v3:
time: 52.7 us; the launch traced here: 52.6 us
  waiting for transfers between devices  22 us (42%)
  starting transfers between devices  19.1 us (36%)
  Pallas kernels  10.9 us (21%)
  between operations  0.68 us (1%)
    ppermute x7, waiting for transfers between devices, shards(): received = lax.ppermute(mine, axis, pairs)  20.2 us
    pallas_call x1, Pallas kernels, shards(): pl.pallas_call(functools.partial(local_kernel, nf=nf, nb=nb, nt=nt, nm=nm...  9.05 us
    ppermute x1, starting transfers between devices, shards(): coef_other = lax.ppermute(coef, CORE, PAIR)  7.98 us
    ppermute x7, starting transfers between devices, shards(): received = lax.ppermute(mine, axis, pairs)  7.77 us
    ppermute x1, starting transfers between devices, shards(): received = lax.ppermute(other, CORE, PAIR)  3.33 us
    pallas_call x1, Pallas kernels, shards(): pl.pallas_call(functools.partial(modes_kernel, nf=nf, nb=nb, nm=nm, nv=nv...  1.47 us
  transfers between devices with their start and end apart: 9, of which 9 were waited for; matrix products, arithmetic and copies ran while one was open for 0% of the time, Pallas kernels for 0%

profile of v3, /device:TPU:1, one launch (start us, length us, event | category | flops | bytes accessed | tf_op | source)
XLA Modules:
  0.0 52.6 jit_solution(10955791322363560729)
XLA Ops:
  0.6 9.0 %local_part.1 = (bf16[2048,768]{1,0:T(8,128)(2,1)S(1)}, bf16[208,128]{1,0:T(8,128)(2,1)S(1)}, bf16[208,128]{1,0:T(8,128)(2,1)S(1)}) custom-call(s32[64]{0:T(128)} %starts_hbm.1, s32[16]{0:T(128)} %bins_hbm.1, bf16[6144,128]{1,0:T(8,128)(2,1)} %bitcast.4, f32[3,2,128]{2,1,0:T(2,128)} %w_hbm.1, f32[16,2,8,64]{3,2,1,0:T(8,128)} %bitcast.5), custom_call_target="tpu_custom_call" | custom-call | tf_op jit(solution)/shard_map/local_part/pallas_call | solution.py:253
  9.7 3.3 %collective-permute-start = (bf16[208,128]{1,0:T(8,128)(2,1)S(1)}, bf16[208,128]{1,0:T(8,128)(2,1)S(1)}, u32[]{:S(2)}, u32[]{:S(2)}) collective-permute-start(bf16[208,128]{1,0:T(8,128)(2,1)S(1)} %get-tuple-element.10), channel_id=1, source_target_pairs={{0,1},{1,0},{2,3},{3,2},{4,5},{5,4},{6,7},{7,6},{8,9},{9,8},{10,11... | collective-permute-start | bytes 159752 | tf_op jit(solution)/shard_map/ppermute | solution.py:279
  13.0 0.9 %collective-permute-done.b_ref = bf16[208,128]{1,0:T(8,128)(2,1)S(1)} collective-permute-done((bf16[208,128]{1,0:T(8,128)(2,1)S(1)}, bf16[208,128]{1,0:T(8,128)(2,1)S(1)}, u32[]{:S(2)}, u32[]{:S(2)}) %collective-permute-start) | collective-permute-done | bytes 53280 | tf_op jit(solution)/shard_map/ppermute | solution.py:279
  13.9 0.1 collective-permute-start.1
  14.0 3.0 %collective-permute-done.1.b_ref = bf16[208,128]{1,0:T(8,128)(2,1)S(1)} collective-permute-done((bf16[208,128]{1,0:T(8,128)(2,1)S(1)}, bf16[208,128]{1,0:T(8,128)(2,1)S(1)}, u32[]{:S(2)}, u32[]{:S(2)}) %collective-permute-start.1) | collective-permute-done | bytes 53280 | tf_op jit(solution)/shard_map/ppermute | solution.py:286
  17.0 0.1 collective-permute-start.2
  17.1 3.0 %collective-permute-done.2.b_ref = bf16[208,128]{1,0:T(8,128)(2,1)S(1)} collective-permute-done((bf16[208,128]{1,0:T(8,128)(2,1)S(1)}, bf16[208,128]{1,0:T(8,128)(2,1)S(1)}, u32[]{:S(2)}, u32[]{:S(2)}) %collective-permute-start.2) | collective-permute-done | bytes 53280 | tf_op jit(solution)/shard_map/ppermute | solution.py:286
  20.1 0.1 collective-permute-start.3
  20.2 3.0 %collective-permute-done.3.b_ref = bf16[208,128]{1,0:T(8,128)(2,1)S(1)} collective-permute-done((bf16[208,128]{1,0:T(8,128)(2,1)S(1)}, bf16[208,128]{1,0:T(8,128)(2,1)S(1)}, u32[]{:S(2)}, u32[]{:S(2)}) %collective-permute-start.3) | collective-permute-done | bytes 53280 | tf_op jit(solution)/shard_map/ppermute | solution.py:286
  23.2 1.0 %collective-permute-start.4 = (bf16[208,128]{1,0:T(8,128)(2,1)S(1)}, bf16[208,128]{1,0:T(8,128)(2,1)S(1)}, u32[]{:S(2)}, u32[]{:S(2)}) collective-permute-start(bf16[208,128]{1,0:T(8,128)(2,1)S(1)} %add_partials.10.a_ref), channel_id=1, source_target_pairs={{0,96},{96,0},{32,64},{64,32},{1,97},{97,1},{33,65},{65,33},{2,98}... | collective-permute-start | bytes 159752 | tf_op jit(solution)/shard_map/ppermute | solution.py:286
  24.2 3.3 %collective-permute-done.4.b_ref = bf16[208,128]{1,0:T(8,128)(2,1)S(1)} collective-permute-done((bf16[208,128]{1,0:T(8,128)(2,1)S(1)}, bf16[208,128]{1,0:T(8,128)(2,1)S(1)}, u32[]{:S(2)}, u32[]{:S(2)}) %collective-permute-start.4) | collective-permute-done | bytes 53280 | tf_op jit(solution)/shard_map/ppermute | solution.py:286
  27.5 1.3 %collective-permute-start.5 = (bf16[208,128]{1,0:T(8,128)(2,1)S(1)}, bf16[208,128]{1,0:T(8,128)(2,1)S(1)}, u32[]{:S(2)}, u32[]{:S(2)}) collective-permute-start(bf16[208,128]{1,0:T(8,128)(2,1)S(1)} %add_partials.11.a_ref), channel_id=1, source_target_pairs={{0,24},{24,0},{8,16},{16,8},{1,25},{25,1},{9,17},{17,9},{2,26},{26... | collective-permute-start | bytes 159752 | tf_op jit(solution)/shard_map/ppermute | solution.py:286
  28.8 3.3 %collective-permute-done.5.b_ref = bf16[208,128]{1,0:T(8,128)(2,1)S(1)} collective-permute-done((bf16[208,128]{1,0:T(8,128)(2,1)S(1)}, bf16[208,128]{1,0:T(8,128)(2,1)S(1)}, u32[]{:S(2)}, u32[]{:S(2)}) %collective-permute-start.5) | collective-permute-done | bytes 53280 | tf_op jit(solution)/shard_map/ppermute | solution.py:286
  32.1 1.3 %collective-permute-start.6 = (bf16[208,128]{1,0:T(8,128)(2,1)S(1)}, bf16[208,128]{1,0:T(8,128)(2,1)S(1)}, u32[]{:S(2)}, u32[]{:S(2)}) collective-permute-start(bf16[208,128]{1,0:T(8,128)(2,1)S(1)} %add_partials.12.a_ref), channel_id=1, source_target_pairs={{0,2},{2,0},{4,6},{6,4},{1,3},{3,1},{5,7},{7,5},{8,10},{10,8},{12,... | collective-permute-start | bytes 159752 | tf_op jit(solution)/shard_map/ppermute | solution.py:286
  33.4 3.2 %collective-permute-done.6.b_ref = bf16[208,128]{1,0:T(8,128)(2,1)S(1)} collective-permute-done((bf16[208,128]{1,0:T(8,128)(2,1)S(1)}, bf16[208,128]{1,0:T(8,128)(2,1)S(1)}, u32[]{:S(2)}, u32[]{:S(2)}) %collective-permute-start.6) | collective-permute-done | bytes 53280 | tf_op jit(solution)/shard_map/ppermute | solution.py:286
  36.7 3.9 %collective-permute-start.7 = (bf16[208,128]{1,0:T(8,128)(2,1)S(1)}, bf16[208,128]{1,0:T(8,128)(2,1)S(1)}, u32[]{:S(2)}, u32[]{:S(2)}) collective-permute-start(bf16[208,128]{1,0:T(8,128)(2,1)S(1)} %add_partials.13.a_ref), channel_id=1, source_target_pairs={{0,6},{6,0},{2,4},{4,2},{1,7},{7,1},{3,5},{5,3},{8,14},{14,8},{10,... | collective-permute-start | bytes 159752 | tf_op jit(solution)/shard_map/ppermute | solution.py:286
  40.6 1.6 %collective-permute-done.7.b_ref = bf16[208,128]{1,0:T(8,128)(2,1)S(1)} collective-permute-done((bf16[208,128]{1,0:T(8,128)(2,1)S(1)}, bf16[208,128]{1,0:T(8,128)(2,1)S(1)}, u32[]{:S(2)}, u32[]{:S(2)}) %collective-permute-start.7) | collective-permute-done | bytes 53280 | tf_op jit(solution)/shard_map/ppermute | solution.py:286
  42.1 0.2 owner_part.1
  42.3 8.0 %collective-permute-start.8 = (bf16[128,128]{1,0:T(8,128)(2,1)S(1)}, bf16[128,128]{1,0:T(8,128)(2,1)S(1)}, u32[]{:S(2)}, u32[]{:S(2)}) collective-permute-start(bf16[128,128]{1,0:T(8,128)(2,1)S(1)} %get-tuple-element.11.mine_ref), channel_id=1, source_target_pairs={{0,1},{1,0},{2,3},{3,2},{4,5},{5,4},{6,7},{7,6},{8,9},{9,8},{10,11... | collective-permute-start | bytes 98312 | tf_op jit(solution)/shard_map/ppermute | solution.py:294
  50.3 0.9 %collective-permute-done.8.other_ref = bf16[128,128]{1,0:T(8,128)(2,1)S(1)} collective-permute-done((bf16[128,128]{1,0:T(8,128)(2,1)S(1)}, bf16[128,128]{1,0:T(8,128)(2,1)S(1)}, u32[]{:S(2)}, u32[]{:S(2)}) %collective-permute-start.8) | collective-permute-done | bytes 32800 | tf_op jit(solution)/shard_map/ppermute | solution.py:294
  51.2 1.5 %modes_part.1 = (f32[1536,128]{1,0:T(8,128)}, f32[8,16]{1,0:T(8,128)}) custom-call(bf16[128,128]{1,0:T(8,128)(2,1)S(1)} %get-tuple-element.11.mine_ref, bf16[128,128]{1,0:T(8,128)(2,1)S(1)} %collective-permute-done.8.other_ref, f32[8,128]{1,0:T(8,128)S(1)} %get-tuple-element.12.s_ref, bf16[2048,768]{1,0:T(8,128)(2,1)S(1)} %get-tuple-element.13.y_ref), custom_call_target="tpu_custom_call" | custom-call | tf_op jit(solution)/shard_map/modes_part/pallas_call | solution.py:295
  (7 shorter events, 0.2 us)
Async XLA Ops:
  9.7 4.2 %collective-permute-start = (bf16[208,128]{1,0:T(8,128)(2,1)S(1)}, bf16[208,128]{1,0:T(8,128)(2,1)S(1)}, u32[]{:S(2)}, u32[]{:S(2)}) collective-permute-start(bf16[208,128]{1,0:T(8,128)(2,1)S(1)} %get-tuple-element.10), channel_id=1, source_target_pairs={{0,1},{1,0},{2,3},{3,2},{4,5},{5,4},{6,7},{7,6},{8,9},{9,8},{10,11... | collective-permute-start | bytes 159752 | tf_op jit(solution)/shard_map/ppermute | solution.py:279
  13.9 3.1 %collective-permute-start.1 = (bf16[208,128]{1,0:T(8,128)(2,1)S(1)}, bf16[208,128]{1,0:T(8,128)(2,1)S(1)}, u32[]{:S(2)}, u32[]{:S(2)}) collective-permute-start(bf16[208,128]{1,0:T(8,128)(2,1)S(1)} %add_partials.7.a_ref), channel_id=1, source_target_pairs={{0,128},{128,0},{1,129},{129,1},{2,130},{130,2},{3,131},{131,3},{4... | collective-permute-start | bytes 159752 | tf_op jit(solution)/shard_map/ppermute | solution.py:286
  17.0 3.1 %collective-permute-start.2 = (bf16[208,128]{1,0:T(8,128)(2,1)S(1)}, bf16[208,128]{1,0:T(8,128)(2,1)S(1)}, u32[]{:S(2)}, u32[]{:S(2)}) collective-permute-start(bf16[208,128]{1,0:T(8,128)(2,1)S(1)} %add_partials.8.a_ref), channel_id=1, source_target_pairs={{0,32},{32,0},{64,96},{96,64},{1,33},{33,1},{65,97},{97,65},{2,34}... | collective-permute-start | bytes 159752 | tf_op jit(solution)/shard_map/ppermute | solution.py:286
  20.1 3.1 %collective-permute-start.3 = (bf16[208,128]{1,0:T(8,128)(2,1)S(1)}, bf16[208,128]{1,0:T(8,128)(2,1)S(1)}, u32[]{:S(2)}, u32[]{:S(2)}) collective-permute-start(bf16[208,128]{1,0:T(8,128)(2,1)S(1)} %add_partials.9.a_ref), channel_id=1, source_target_pairs={{0,8},{8,0},{16,24},{24,16},{1,9},{9,1},{17,25},{25,17},{2,10},{10... | collective-permute-start | bytes 159752 | tf_op jit(solution)/shard_map/ppermute | solution.py:286
  23.2 4.3 %collective-permute-start.4 = (bf16[208,128]{1,0:T(8,128)(2,1)S(1)}, bf16[208,128]{1,0:T(8,128)(2,1)S(1)}, u32[]{:S(2)}, u32[]{:S(2)}) collective-permute-start(bf16[208,128]{1,0:T(8,128)(2,1)S(1)} %add_partials.10.a_ref), channel_id=1, source_target_pairs={{0,96},{96,0},{32,64},{64,32},{1,97},{97,1},{33,65},{65,33},{2,98}... | collective-permute-start | bytes 159752 | tf_op jit(solution)/shard_map/ppermute | solution.py:286
  27.5 4.5 %collective-permute-start.5 = (bf16[208,128]{1,0:T(8,128)(2,1)S(1)}, bf16[208,128]{1,0:T(8,128)(2,1)S(1)}, u32[]{:S(2)}, u32[]{:S(2)}) collective-permute-start(bf16[208,128]{1,0:T(8,128)(2,1)S(1)} %add_partials.11.a_ref), channel_id=1, source_target_pairs={{0,24},{24,0},{8,16},{16,8},{1,25},{25,1},{9,17},{17,9},{2,26},{26... | collective-permute-start | bytes 159752 | tf_op jit(solution)/shard_map/ppermute | solution.py:286
  32.1 4.5 %collective-permute-start.6 = (bf16[208,128]{1,0:T(8,128)(2,1)S(1)}, bf16[208,128]{1,0:T(8,128)(2,1)S(1)}, u32[]{:S(2)}, u32[]{:S(2)}) collective-permute-start(bf16[208,128]{1,0:T(8,128)(2,1)S(1)} %add_partials.12.a_ref), channel_id=1, source_target_pairs={{0,2},{2,0},{4,6},{6,4},{1,3},{3,1},{5,7},{7,5},{8,10},{10,8},{12,... | collective-permute-start | bytes 159752 | tf_op jit(solution)/shard_map/ppermute | solution.py:286
  36.7 5.5 %collective-permute-start.7 = (bf16[208,128]{1,0:T(8,128)(2,1)S(1)}, bf16[208,128]{1,0:T(8,128)(2,1)S(1)}, u32[]{:S(2)}, u32[]{:S(2)}) collective-permute-start(bf16[208,128]{1,0:T(8,128)(2,1)S(1)} %add_partials.13.a_ref), channel_id=1, source_target_pairs={{0,6},{6,0},{2,4},{4,2},{1,7},{7,1},{3,5},{5,3},{8,14},{14,8},{10,... | collective-permute-start | bytes 159752 | tf_op jit(solution)/shard_map/ppermute | solution.py:286
  42.3 8.8 %collective-permute-start.8 = (bf16[128,128]{1,0:T(8,128)(2,1)S(1)}, bf16[128,128]{1,0:T(8,128)(2,1)S(1)}, u32[]{:S(2)}, u32[]{:S(2)}) collective-permute-start(bf16[128,128]{1,0:T(8,128)(2,1)S(1)} %get-tuple-element.11.mine_ref), channel_id=1, source_target_pairs={{0,1},{1,0},{2,3},{3,2},{4,5},{5,4},{6,7},{7,6},{8,9},{9,8},{10,11... | collective-permute-start | bytes 98312 | tf_op jit(solution)/shard_map/ppermute | solution.py:294

commit v4 on v3

--- a/solution.py
+++ b/solution.py
@@ -49,7 +49,7 @@
 
 
 def local_kernel(starts_hbm, bins_hbm, x_hbm, w_hbm, g_hbm, y_ref, mine_ref, other_ref,
-                 xb, xf, xs, wv, gv, st, bn, ta, tb, win, amat, starts_ref, bins_ref, sems,
+                 xb, xf, xs, zall, wv, gv, st, bn, ta, tb, win, amat, starts_ref, bins_ref, sems,
                  *, nf, nb, nt, nm, nv, nx):
     nvx = nv * nx
     rows = nt * nvx
@@ -96,29 +96,12 @@
         xf[i * chunk:(i + 1) * chunk, :] = xb[i].astype(jnp.float32)
     copies[2].wait()
     copies[3].wait()
-    sums = []
-    for v in range(nv):
-        acc = jnp.zeros((1, 128), jnp.float32)
-        for k in range(nx):
-            col = v * nx + k
-            part = xf[pl.ds(col, nt, stride=nvx), :]
-            xs[:, col * 128:(col + 1) * 128] = part.astype(jnp.bfloat16)
-            sq = jnp.sum(part * part, axis=0, keepdims=True)
-            acc = acc + sq * wv[v, k:k + 1, :]
-        sums.append(jnp.sum(acc, axis=1, keepdims=True))
-    msq = jnp.zeros((1, 128), jnp.float32)
-    for v in range(nv):
-        msq = jnp.where(lane == v, sums[v], msq)
-    tail = as_rows(msq)
-    mine_ref[mine_ref.shape[0] - TAIL:, :] = tail
-    other_ref[other_ref.shape[0] - TAIL:, :] = tail
-
     low = lax.broadcasted_iota(jnp.int32, (nm, 2 * nb), 1) < nb
     sqrt_w = jnp.concatenate([jnp.sqrt(wv[c // nx, c % nx:c % nx + 1, :]) for c in range(nvx)], axis=1)
     span = nx * 128
     zeros = jnp.zeros((2 * nm, 2 * nb), jnp.float32)
 
-    def transform(j):
+    def build(j):
         slot = j % 2
         for i in range(2):
             f = 2 * j + i
@@ -130,8 +113,11 @@
             base = i * 2 * nb
             amat[slot, base:base + nb, :] = (ww * (ca * cb + sa * sb)).astype(jnp.bfloat16)
             amat[slot, base + nb:base + 2 * nb, :] = (ww * (ca * sb - sa * cb)).astype(jnp.bfloat16)
-        q = jnp.dot(amat[slot], xs[...], preferred_element_type=jnp.float32)
-        y_ref[4 * nb * j:4 * nb * (j + 1), :] = (q * sqrt_w).astype(jnp.bfloat16)
+
+    def transform(j, v):
+        cols = slice(v * span, (v + 1) * span)
+        q = jnp.dot(amat[j % 2], xs[:, cols], preferred_element_type=jnp.float32)
+        y_ref[4 * nb * j:4 * nb * (j + 1), cols] = (q * sqrt_w[:, cols]).astype(jnp.bfloat16)
 
     def project(j):
         yf = y_ref[4 * nb * j:4 * nb * (j + 1), :]
@@ -157,22 +143,40 @@
                 ru = part[:nm]
                 rv = pltpu.roll(part[nm:], nb, 1)
                 zs[i].append(jnp.where(low, ru, -ru) + rv)
-        npair = nf // 4
-        base = (j % npair) * nv * 2 * nm
-
-        def put(ref):
-            for v in range(nv):
-                block = jnp.concatenate([zs[0][v], zs[1][v]], axis=0).astype(jnp.bfloat16)
-                ref[base + v * 2 * nm:base + (v + 1) * 2 * nm, :] = block
-
-        pl.when(core == j // npair)(lambda: put(mine_ref))
-        pl.when(core != j // npair)(lambda: put(other_ref))
-
-    transform(0)
+        base = j * nv * 2 * nm
+        for v in range(nv):
+            block = jnp.concatenate([zs[0][v], zs[1][v]], axis=0).astype(jnp.bfloat16)
+            zall[base + v * 2 * nm:base + (v + 1) * 2 * nm, :] = block
+
+    build(0)
+    sums = []
+    for v in range(nv):
+        acc = jnp.zeros((1, 128), jnp.float32)
+        for k in range(nx):
+            col = v * nx + k
+            part = xf[pl.ds(col, nt, stride=nvx), :]
+            xs[:, col * 128:(col + 1) * 128] = part.astype(jnp.bfloat16)
+            sq = jnp.sum(part * part, axis=0, keepdims=True)
+            acc = acc + sq * wv[v, k:k + 1, :]
+        sums.append(jnp.sum(acc, axis=1, keepdims=True))
+        transform(0, v)
+    msq = jnp.zeros((1, 128), jnp.float32)
+    for v in range(nv):
+        msq = jnp.where(lane == v, sums[v], msq)
+    tail = as_rows(msq)
+    mine_ref[mine_ref.shape[0] - TAIL:, :] = tail
+    other_ref[other_ref.shape[0] - TAIL:, :] = tail
     for j in range(1, nf // 2):
-        transform(j)
+        build(j)
+        for v in range(nv):
+            transform(j, v)
         project(j - 1)
     project(nf // 2 - 1)
+    cut = nf // 2 * nv * nm
+    low_half = zall[:cut, :].astype(jnp.float32)
+    high_half = zall[cut:, :].astype(jnp.float32)
+    mine_ref[:cut, :] = jnp.where(core == 0, low_half, high_half).astype(jnp.bfloat16)
+    other_ref[:cut, :] = jnp.where(core == 0, high_half, low_half).astype(jnp.bfloat16)
 
 
 def add_kernel(a_ref, b_ref, o_ref):
@@ -209,7 +213,7 @@
         o_ref[rows + j * step:rows + (j + 1) * step, :] = extra.astype(jnp.bfloat16)
 
 
-def modes_kernel(mine_ref, other_ref, s_ref, y_ref, o_ref, e_ref, *, nf, nb, nm, nv, nx):
+def modes_kernel(mine_ref, other_ref, s_ref, y_ref, o_hbm, e_ref, ov, sems, *, nf, nb, nm, nv, nx):
     nvx = nv * nx
     core = lax.axis_index(CORE)
     first = core == 0
@@ -220,21 +224,34 @@
     low = lax.broadcasted_iota(jnp.int32, (nm, 2 * nb), 1) < nb
     lane = lax.broadcasted_iota(jnp.int32, (nm, nf), 1)
     energy = jnp.zeros((nm, nf), jnp.float32)
-    for f in range(nf):
-        part = halves[f // (nf // 2)]
-        at = (f % (nf // 2)) * nm
-        coef = part[at:at + nm]
-        extra = part[rows + at:rows + at + nm]
-        energy = jnp.where(lane == f, extra[:, 0:1] + extra[:, 1:2] + extra[:, 2:3], energy)
-        left = jnp.concatenate([jnp.where(low, coef, -coef), pltpu.roll(coef, nb, 1)], axis=0)
-        m = jnp.dot(left.astype(jnp.bfloat16), y_ref[2 * nb * f:2 * nb * (f + 1), :],
-                    preferred_element_type=jnp.float32)
-        base = f * 2 * nm * nvx
+    zeros = jnp.zeros((2 * nm, 2 * nb), jnp.float32)
+    pieces = sems.shape[0]
+    per = ov.shape[0] // pieces
+    outs = [pltpu.make_async_copy(ov.at[pl.ds(i * per, per)], o_hbm.at[pl.ds(i * per, per)], sems.at[i])
+            for i in range(pieces)]
+    pairs = nf // 2
+    for j in range(pairs):
+        left = []
+        for i in range(2):
+            f = 2 * j + i
+            part = halves[f // (nf // 2)]
+            at = (f % (nf // 2)) * nm
+            coef = part[at:at + nm]
+            extra = part[rows + at:rows + at + nm]
+            energy = jnp.where(lane == f, extra[:, 0:1] + extra[:, 1:2] + extra[:, 2:3], energy)
+            both = jnp.concatenate([jnp.where(low, coef, -coef), pltpu.roll(coef, nb, 1)], axis=0)
+            left.append(jnp.concatenate([both, zeros] if i == 0 else [zeros, both], axis=1))
+        left = jnp.concatenate(left, axis=0).astype(jnp.bfloat16)
+        m = jnp.dot(left, y_ref[4 * nb * j:4 * nb * (j + 1), :], preferred_element_type=jnp.float32)
+        base = j * 4 * nm * nvx
         for c in range(nvx):
             v = c // nx
-            o_ref[pl.ds(base + c, 2 * nm, stride=nvx), :] = (
-                m[:, c * 128:(c + 1) * 128] * s_ref[v:v + 1, :])
+            ov[pl.ds(base + c, 4 * nm, stride=nvx), :] = m[:, c * 128:(c + 1) * 128] * s_ref[v:v + 1, :]
+        if (j + 1) % (pairs // pieces) == 0:
+            outs[(j + 1) // (pairs // pieces) - 1].start()
     e_ref[...] = jnp.sqrt(energy / nb)
+    for out in outs:
+        out.wait()
 
 
 def shards(snapshots, quad_weight, mode_guess, bins, starts):
@@ -261,6 +278,7 @@
             pltpu.VMEM((nchunk, nt * nvx // nchunk, ny), jnp.bfloat16),
             pltpu.VMEM((nt * nvx, ny), jnp.float32),
             pltpu.VMEM((nt, nvx * ny), jnp.bfloat16),
+            pltpu.VMEM((nf * nv * nm, 128), jnp.bfloat16),
             pltpu.VMEM((nv, nx, ny), jnp.float32),
             pltpu.VMEM((nf, 2, nm, nb), jnp.float32),
             pltpu.VMEM((nb, 128), jnp.int32),
@@ -296,8 +314,9 @@
         functools.partial(modes_kernel, nf=nf, nb=nb, nm=nm, nv=nv, nx=nx),
         out_shape=(jax.ShapeDtypeStruct((nf * 2 * nm * nvx, ny), jnp.float32),
                    jax.ShapeDtypeStruct((nm, nf), jnp.float32)),
-        in_specs=[vmem] * 4, out_specs=(vmem, vmem), compiler_params=params,
-        name="modes_part",
+        in_specs=[vmem] * 4, out_specs=(hbm, vmem),
+        scratch_shapes=[pltpu.VMEM((nf * 2 * nm * nvx, ny), jnp.float32), pltpu.SemaphoreType.DMA((4,))],
+        compiler_params=params, name="modes_part",
     )(coef, coef_other, scale, y)
     return modes.reshape(nf, 2, nm, nv, nx, ny), energy.T
 

time: 52.7 us -> 51.3 us (0.973)
  Pallas kernels: 10.9 us -> 9.41 us
    pallas_call x1, Pallas kernels: 9.05 us -> 7.04 us  [shards(): pl.pallas_call(functools.partial(local_kernel, nf=nf, nb=nb, nt=nt, nm=nm...]
    pallas_call x1, Pallas kernels: 1.47 us -> 2 us  [shards(): pl.pallas_call(functools.partial(modes_kernel, nf=nf, nb=nb, nm=nm, nv=nv...]
where the time goes in v4:
time: 51.3 us; the launch traced here: 51.2 us
  waiting for transfers between devices  22 us (43%)
  starting transfers between devices  19.1 us (37%)
  Pallas kernels  9.41 us (18%)
  between operations  0.68 us (1%)
    ppermute x7, waiting for transfers between devices, shards(): received = lax.ppermute(mine, axis, pairs)  20.2 us
    ppermute x1, starting transfers between devices, shards(): coef_other = lax.ppermute(coef, CORE, PAIR)  7.98 us
    ppermute x7, starting transfers between devices, shards(): received = lax.ppermute(mine, axis, pairs)  7.77 us
    pallas_call x1, Pallas kernels, shards(): pl.pallas_call(functools.partial(local_kernel, nf=nf, nb=nb, nt=nt, nm=nm...  7.04 us
    ppermute x1, starting transfers between devices, shards(): received = lax.ppermute(other, CORE, PAIR)  3.33 us
    pallas_call x1, Pallas kernels, shards(): pl.pallas_call(functools.partial(modes_kernel, nf=nf, nb=nb, nm=nm, nv=nv...  2 us
  transfers between devices with their start and end apart: 9, of which 9 were waited for; matrix products, arithmetic and copies ran while one was open for 0% of the time, Pallas kernels for 0%

profile of v4, /device:TPU:1, one launch (start us, length us, event | category | flops | bytes accessed | tf_op | source)
XLA Modules:
  0.0 51.2 jit_solution(13744676320851274767)
XLA Ops:
  0.6 7.0 %local_part.1 = (bf16[2048,768]{1,0:T(8,128)(2,1)S(1)}, bf16[208,128]{1,0:T(8,128)(2,1)S(1)}, bf16[208,128]{1,0:T(8,128)(2,1)S(1)}) custom-call(s32[64]{0:T(128)} %starts_hbm.1, s32[16]{0:T(128)} %bins_hbm.1, bf16[6144,128]{1,0:T(8,128)(2,1)} %bitcast.4, f32[3,2,128]{2,1,0:T(2,128)} %w_hbm.1, f32[16,2,8,64]{3,2,1,0:T(8,128)} %bitcast.5), custom_call_target="tpu_custom_call" | custom-call | tf_op jit(solution)/shard_map/local_part/pallas_call | solution.py:270
  7.7 3.3 %collective-permute-start = (bf16[208,128]{1,0:T(8,128)(2,1)S(1)}, bf16[208,128]{1,0:T(8,128)(2,1)S(1)}, u32[]{:S(2)}, u32[]{:S(2)}) collective-permute-start(bf16[208,128]{1,0:T(8,128)(2,1)S(1)} %get-tuple-element.10), channel_id=1, source_target_pairs={{0,1},{1,0},{2,3},{3,2},{4,5},{5,4},{6,7},{7,6},{8,9},{9,8},{10,11... | collective-permute-start | bytes 159752 | tf_op jit(solution)/shard_map/ppermute | solution.py:297
  11.0 0.9 %collective-permute-done.b_ref = bf16[208,128]{1,0:T(8,128)(2,1)S(1)} collective-permute-done((bf16[208,128]{1,0:T(8,128)(2,1)S(1)}, bf16[208,128]{1,0:T(8,128)(2,1)S(1)}, u32[]{:S(2)}, u32[]{:S(2)}) %collective-permute-start) | collective-permute-done | bytes 53280 | tf_op jit(solution)/shard_map/ppermute | solution.py:297
  11.9 0.1 collective-permute-start.1
  12.0 3.0 %collective-permute-done.1.b_ref = bf16[208,128]{1,0:T(8,128)(2,1)S(1)} collective-permute-done((bf16[208,128]{1,0:T(8,128)(2,1)S(1)}, bf16[208,128]{1,0:T(8,128)(2,1)S(1)}, u32[]{:S(2)}, u32[]{:S(2)}) %collective-permute-start.1) | collective-permute-done | bytes 53280 | tf_op jit(solution)/shard_map/ppermute | solution.py:304
  15.0 0.1 collective-permute-start.2
  15.1 3.0 %collective-permute-done.2.b_ref = bf16[208,128]{1,0:T(8,128)(2,1)S(1)} collective-permute-done((bf16[208,128]{1,0:T(8,128)(2,1)S(1)}, bf16[208,128]{1,0:T(8,128)(2,1)S(1)}, u32[]{:S(2)}, u32[]{:S(2)}) %collective-permute-start.2) | collective-permute-done | bytes 53280 | tf_op jit(solution)/shard_map/ppermute | solution.py:304
  18.1 0.1 collective-permute-start.3
  18.2 3.0 %collective-permute-done.3.b_ref = bf16[208,128]{1,0:T(8,128)(2,1)S(1)} collective-permute-done((bf16[208,128]{1,0:T(8,128)(2,1)S(1)}, bf16[208,128]{1,0:T(8,128)(2,1)S(1)}, u32[]{:S(2)}, u32[]{:S(2)}) %collective-permute-start.3) | collective-permute-done | bytes 53280 | tf_op jit(solution)/shard_map/ppermute | solution.py:304
  21.2 1.0 %collective-permute-start.4 = (bf16[208,128]{1,0:T(8,128)(2,1)S(1)}, bf16[208,128]{1,0:T(8,128)(2,1)S(1)}, u32[]{:S(2)}, u32[]{:S(2)}) collective-permute-start(bf16[208,128]{1,0:T(8,128)(2,1)S(1)} %add_partials.10.a_ref), channel_id=1, source_target_pairs={{0,96},{96,0},{32,64},{64,32},{1,97},{97,1},{33,65},{65,33},{2,98}... | collective-permute-start | bytes 159752 | tf_op jit(solution)/shard_map/ppermute | solution.py:304
  22.2 3.3 %collective-permute-done.4.b_ref = bf16[208,128]{1,0:T(8,128)(2,1)S(1)} collective-permute-done((bf16[208,128]{1,0:T(8,128)(2,1)S(1)}, bf16[208,128]{1,0:T(8,128)(2,1)S(1)}, u32[]{:S(2)}, u32[]{:S(2)}) %collective-permute-start.4) | collective-permute-done | bytes 53280 | tf_op jit(solution)/shard_map/ppermute | solution.py:304
  25.5 1.3 %collective-permute-start.5 = (bf16[208,128]{1,0:T(8,128)(2,1)S(1)}, bf16[208,128]{1,0:T(8,128)(2,1)S(1)}, u32[]{:S(2)}, u32[]{:S(2)}) collective-permute-start(bf16[208,128]{1,0:T(8,128)(2,1)S(1)} %add_partials.11.a_ref), channel_id=1, source_target_pairs={{0,24},{24,0},{8,16},{16,8},{1,25},{25,1},{9,17},{17,9},{2,26},{26... | collective-permute-start | bytes 159752 | tf_op jit(solution)/shard_map/ppermute | solution.py:304
  26.8 3.3 %collective-permute-done.5.b_ref = bf16[208,128]{1,0:T(8,128)(2,1)S(1)} collective-permute-done((bf16[208,128]{1,0:T(8,128)(2,1)S(1)}, bf16[208,128]{1,0:T(8,128)(2,1)S(1)}, u32[]{:S(2)}, u32[]{:S(2)}) %collective-permute-start.5) | collective-permute-done | bytes 53280 | tf_op jit(solution)/shard_map/ppermute | solution.py:304
  30.1 1.3 %collective-permute-start.6 = (bf16[208,128]{1,0:T(8,128)(2,1)S(1)}, bf16[208,128]{1,0:T(8,128)(2,1)S(1)}, u32[]{:S(2)}, u32[]{:S(2)}) collective-permute-start(bf16[208,128]{1,0:T(8,128)(2,1)S(1)} %add_partials.12.a_ref), channel_id=1, source_target_pairs={{0,2},{2,0},{4,6},{6,4},{1,3},{3,1},{5,7},{7,5},{8,10},{10,8},{12,... | collective-permute-start | bytes 159752 | tf_op jit(solution)/shard_map/ppermute | solution.py:304
  31.4 3.2 %collective-permute-done.6.b_ref = bf16[208,128]{1,0:T(8,128)(2,1)S(1)} collective-permute-done((bf16[208,128]{1,0:T(8,128)(2,1)S(1)}, bf16[208,128]{1,0:T(8,128)(2,1)S(1)}, u32[]{:S(2)}, u32[]{:S(2)}) %collective-permute-start.6) | collective-permute-done | bytes 53280 | tf_op jit(solution)/shard_map/ppermute | solution.py:304
  34.6 3.9 %collective-permute-start.7 = (bf16[208,128]{1,0:T(8,128)(2,1)S(1)}, bf16[208,128]{1,0:T(8,128)(2,1)S(1)}, u32[]{:S(2)}, u32[]{:S(2)}) collective-permute-start(bf16[208,128]{1,0:T(8,128)(2,1)S(1)} %add_partials.13.a_ref), channel_id=1, source_target_pairs={{0,6},{6,0},{2,4},{4,2},{1,7},{7,1},{3,5},{5,3},{8,14},{14,8},{10,... | collective-permute-start | bytes 159752 | tf_op jit(solution)/shard_map/ppermute | solution.py:304
  38.5 1.6 %collective-permute-done.7.b_ref = bf16[208,128]{1,0:T(8,128)(2,1)S(1)} collective-permute-done((bf16[208,128]{1,0:T(8,128)(2,1)S(1)}, bf16[208,128]{1,0:T(8,128)(2,1)S(1)}, u32[]{:S(2)}, u32[]{:S(2)}) %collective-permute-start.7) | collective-permute-done | bytes 53280 | tf_op jit(solution)/shard_map/ppermute | solution.py:304
  40.1 0.2 owner_part.1
  40.3 8.0 %collective-permute-start.8 = (bf16[128,128]{1,0:T(8,128)(2,1)S(1)}, bf16[128,128]{1,0:T(8,128)(2,1)S(1)}, u32[]{:S(2)}, u32[]{:S(2)}) collective-permute-start(bf16[128,128]{1,0:T(8,128)(2,1)S(1)} %get-tuple-element.11.mine_ref), channel_id=1, source_target_pairs={{0,1},{1,0},{2,3},{3,2},{4,5},{5,4},{6,7},{7,6},{8,9},{9,8},{10,11... | collective-permute-start | bytes 98312 | tf_op jit(solution)/shard_map/ppermute | solution.py:312
  48.3 0.9 %collective-permute-done.8.other_ref = bf16[128,128]{1,0:T(8,128)(2,1)S(1)} collective-permute-done((bf16[128,128]{1,0:T(8,128)(2,1)S(1)}, bf16[128,128]{1,0:T(8,128)(2,1)S(1)}, u32[]{:S(2)}, u32[]{:S(2)}) %collective-permute-start.8) | collective-permute-done | bytes 32800 | tf_op jit(solution)/shard_map/ppermute | solution.py:312
  49.2 2.0 %modes_part.1 = (f32[1536,128]{1,0:T(8,128)}, f32[8,16]{1,0:T(8,128)}) custom-call(bf16[128,128]{1,0:T(8,128)(2,1)S(1)} %get-tuple-element.11.mine_ref, bf16[128,128]{1,0:T(8,128)(2,1)S(1)} %collective-permute-done.8.other_ref, f32[8,128]{1,0:T(8,128)S(1)} %get-tuple-element.12.s_ref, bf16[2048,768]{1,0:T(8,128)(2,1)S(1)} %get-tuple-element.13.y_ref), custom_call_target="tpu_custom_call" | custom-call | tf_op jit(solution)/shard_map/modes_part/pallas_call | solution.py:313
  (7 shorter events, 0.2 us)
Async XLA Ops:
  7.7 4.2 %collective-permute-start = (bf16[208,128]{1,0:T(8,128)(2,1)S(1)}, bf16[208,128]{1,0:T(8,128)(2,1)S(1)}, u32[]{:S(2)}, u32[]{:S(2)}) collective-permute-start(bf16[208,128]{1,0:T(8,128)(2,1)S(1)} %get-tuple-element.10), channel_id=1, source_target_pairs={{0,1},{1,0},{2,3},{3,2},{4,5},{5,4},{6,7},{7,6},{8,9},{9,8},{10,11... | collective-permute-start | bytes 159752 | tf_op jit(solution)/shard_map/ppermute | solution.py:297
  11.9 3.1 %collective-permute-start.1 = (bf16[208,128]{1,0:T(8,128)(2,1)S(1)}, bf16[208,128]{1,0:T(8,128)(2,1)S(1)}, u32[]{:S(2)}, u32[]{:S(2)}) collective-permute-start(bf16[208,128]{1,0:T(8,128)(2,1)S(1)} %add_partials.7.a_ref), channel_id=1, source_target_pairs={{0,128},{128,0},{1,129},{129,1},{2,130},{130,2},{3,131},{131,3},{4... | collective-permute-start | bytes 159752 | tf_op jit(solution)/shard_map/ppermute | solution.py:304
  15.0 3.1 %collective-permute-start.2 = (bf16[208,128]{1,0:T(8,128)(2,1)S(1)}, bf16[208,128]{1,0:T(8,128)(2,1)S(1)}, u32[]{:S(2)}, u32[]{:S(2)}) collective-permute-start(bf16[208,128]{1,0:T(8,128)(2,1)S(1)} %add_partials.8.a_ref), channel_id=1, source_target_pairs={{0,32},{32,0},{64,96},{96,64},{1,33},{33,1},{65,97},{97,65},{2,34}... | collective-permute-start | bytes 159752 | tf_op jit(solution)/shard_map/ppermute | solution.py:304
  18.1 3.1 %collective-permute-start.3 = (bf16[208,128]{1,0:T(8,128)(2,1)S(1)}, bf16[208,128]{1,0:T(8,128)(2,1)S(1)}, u32[]{:S(2)}, u32[]{:S(2)}) collective-permute-start(bf16[208,128]{1,0:T(8,128)(2,1)S(1)} %add_partials.9.a_ref), channel_id=1, source_target_pairs={{0,8},{8,0},{16,24},{24,16},{1,9},{9,1},{17,25},{25,17},{2,10},{10... | collective-permute-start | bytes 159752 | tf_op jit(solution)/shard_map/ppermute | solution.py:304
  21.2 4.3 %collective-permute-start.4 = (bf16[208,128]{1,0:T(8,128)(2,1)S(1)}, bf16[208,128]{1,0:T(8,128)(2,1)S(1)}, u32[]{:S(2)}, u32[]{:S(2)}) collective-permute-start(bf16[208,128]{1,0:T(8,128)(2,1)S(1)} %add_partials.10.a_ref), channel_id=1, source_target_pairs={{0,96},{96,0},{32,64},{64,32},{1,97},{97,1},{33,65},{65,33},{2,98}... | collective-permute-start | bytes 159752 | tf_op jit(solution)/shard_map/ppermute | solution.py:304
  25.5 4.5 %collective-permute-start.5 = (bf16[208,128]{1,0:T(8,128)(2,1)S(1)}, bf16[208,128]{1,0:T(8,128)(2,1)S(1)}, u32[]{:S(2)}, u32[]{:S(2)}) collective-permute-start(bf16[208,128]{1,0:T(8,128)(2,1)S(1)} %add_partials.11.a_ref), channel_id=1, source_target_pairs={{0,24},{24,0},{8,16},{16,8},{1,25},{25,1},{9,17},{17,9},{2,26},{26... | collective-permute-start | bytes 159752 | tf_op jit(solution)/shard_map/ppermute | solution.py:304
  30.1 4.5 %collective-permute-start.6 = (bf16[208,128]{1,0:T(8,128)(2,1)S(1)}, bf16[208,128]{1,0:T(8,128)(2,1)S(1)}, u32[]{:S(2)}, u32[]{:S(2)}) collective-permute-start(bf16[208,128]{1,0:T(8,128)(2,1)S(1)} %add_partials.12.a_ref), channel_id=1, source_target_pairs={{0,2},{2,0},{4,6},{6,4},{1,3},{3,1},{5,7},{7,5},{8,10},{10,8},{12,... | collective-permute-start | bytes 159752 | tf_op jit(solution)/shard_map/ppermute | solution.py:304
  34.6 5.5 %collective-permute-start.7 = (bf16[208,128]{1,0:T(8,128)(2,1)S(1)}, bf16[208,128]{1,0:T(8,128)(2,1)S(1)}, u32[]{:S(2)}, u32[]{:S(2)}) collective-permute-start(bf16[208,128]{1,0:T(8,128)(2,1)S(1)} %add_partials.13.a_ref), channel_id=1, source_target_pairs={{0,6},{6,0},{2,4},{4,2},{1,7},{7,1},{3,5},{5,3},{8,14},{14,8},{10,... | collective-permute-start | bytes 159752 | tf_op jit(solution)/shard_map/ppermute | solution.py:304
  40.3 8.8 %collective-permute-start.8 = (bf16[128,128]{1,0:T(8,128)(2,1)S(1)}, bf16[128,128]{1,0:T(8,128)(2,1)S(1)}, u32[]{:S(2)}, u32[]{:S(2)}) collective-permute-start(bf16[128,128]{1,0:T(8,128)(2,1)S(1)} %get-tuple-element.11.mine_ref), channel_id=1, source_target_pairs={{0,1},{1,0},{2,3},{3,2},{4,5},{5,4},{6,7},{7,6},{8,9},{9,8},{10,11... | collective-permute-start | bytes 98312 | tf_op jit(solution)/shard_map/ppermute | solution.py:312

commit v5 on v4

--- a/solution.py
+++ b/solution.py
@@ -8,19 +8,33 @@
 from jax.experimental.pallas import tpu as pltpu
 from jax.sharding import Mesh
 from jax.sharding import PartitionSpec as P
+import numpy as np
 
 NFFT = 256
 EPS = 1e-06
 AXES = ("sx_0", "sx_1", "sx_2", "sy_0", "sy_1")
 SX = AXES[:3]
 SY = AXES[3:]
-NEAR4 = ((0, 1), (1, 0), (2, 3), (3, 2))
-RING4 = ((0, 3), (3, 0), (1, 2), (2, 1))
-PAIR = ((0, 1), (1, 0))
-STAGES = (("sx_0", PAIR), ("sx_1", NEAR4), ("sx_2", NEAR4), ("sx_1", RING4), ("sx_2", RING4),
-          ("sy_0", NEAR4), ("sy_0", RING4))
+SIZES = (2, 4, 4, 4, 2)
+NEAR4 = (1, 0, 3, 2)
+RING4 = (3, 2, 1, 0)
+PAIR = (1, 0)
+ORDER = (
+    ((0, PAIR), (1, NEAR4), (2, NEAR4), (3, NEAR4), (1, RING4), (2, RING4), (3, RING4)),
+    ((1, NEAR4), (0, PAIR), (3, NEAR4), (2, NEAR4), (3, RING4), (1, RING4), (2, RING4)),
+)
 CORE = "sy_1"
 MIB = 1 << 20
+
+
+def stage_pairs(stage):
+    pairs = []
+    for at in np.ndindex(*SIZES):
+        axis, partner = ORDER[at[-1]][stage]
+        to = list(at)
+        to[axis] = partner[at[axis]]
+        pairs.append((int(np.ravel_multi_index(at, SIZES)), int(np.ravel_multi_index(to, SIZES))))
+    return pairs
 
 
 def split3(x):
@@ -213,7 +227,7 @@
         o_ref[rows + j * step:rows + (j + 1) * step, :] = extra.astype(jnp.bfloat16)
 
 
-def modes_kernel(mine_ref, other_ref, s_ref, y_ref, o_hbm, e_ref, ov, sems, *, nf, nb, nm, nv, nx):
+def modes_kernel(mine_ref, other_ref, s_ref, y_ref, o_ref, e_ref, *, nf, nb, nm, nv, nx):
     nvx = nv * nx
     core = lax.axis_index(CORE)
     first = core == 0
@@ -224,34 +238,21 @@
     low = lax.broadcasted_iota(jnp.int32, (nm, 2 * nb), 1) < nb
     lane = lax.broadcasted_iota(jnp.int32, (nm, nf), 1)
     energy = jnp.zeros((nm, nf), jnp.float32)
-    zeros = jnp.zeros((2 * nm, 2 * nb), jnp.float32)
-    pieces = sems.shape[0]
-    per = ov.shape[0] // pieces
-    outs = [pltpu.make_async_copy(ov.at[pl.ds(i * per, per)], o_hbm.at[pl.ds(i * per, per)], sems.at[i])
-            for i in range(pieces)]
-    pairs = nf // 2
-    for j in range(pairs):
-        left = []
-        for i in range(2):
-            f = 2 * j + i
-            part = halves[f // (nf // 2)]
-            at = (f % (nf // 2)) * nm
-            coef = part[at:at + nm]
-            extra = part[rows + at:rows + at + nm]
-            energy = jnp.where(lane == f, extra[:, 0:1] + extra[:, 1:2] + extra[:, 2:3], energy)
-            both = jnp.concatenate([jnp.where(low, coef, -coef), pltpu.roll(coef, nb, 1)], axis=0)
-            left.append(jnp.concatenate([both, zeros] if i == 0 else [zeros, both], axis=1))
-        left = jnp.concatenate(left, axis=0).astype(jnp.bfloat16)
-        m = jnp.dot(left, y_ref[4 * nb * j:4 * nb * (j + 1), :], preferred_element_type=jnp.float32)
-        base = j * 4 * nm * nvx
+    for f in range(nf):
+        part = halves[f // (nf // 2)]
+        at = (f % (nf // 2)) * nm
+        coef = part[at:at + nm]
+        extra = part[rows + at:rows + at + nm]
+        energy = jnp.where(lane == f, extra[:, 0:1] + extra[:, 1:2] + extra[:, 2:3], energy)
+        left = jnp.concatenate([jnp.where(low, coef, -coef), pltpu.roll(coef, nb, 1)], axis=0)
+        m = jnp.dot(left.astype(jnp.bfloat16), y_ref[2 * nb * f:2 * nb * (f + 1), :],
+                    preferred_element_type=jnp.float32)
+        base = f * 2 * nm * nvx
         for c in range(nvx):
             v = c // nx
-            ov[pl.ds(base + c, 4 * nm, stride=nvx), :] = m[:, c * 128:(c + 1) * 128] * s_ref[v:v + 1, :]
-        if (j + 1) % (pairs // pieces) == 0:
-            outs[(j + 1) // (pairs // pieces) - 1].start()
+            o_ref[pl.ds(base + c, 2 * nm, stride=nvx), :] = (
+                m[:, c * 128:(c + 1) * 128] * s_ref[v:v + 1, :])
     e_ref[...] = jnp.sqrt(energy / nb)
-    for out in outs:
-        out.wait()
 
 
 def shards(snapshots, quad_weight, mode_guess, bins, starts):
@@ -294,14 +295,15 @@
         compiler_params=params,
         name="local_part",
     )(*[pltpu.with_memory_space_constraint(a, pltpu.HBM) for a in (starts, bins, x, quad_weight, guess)])
-    received = lax.ppermute(other, CORE, PAIR)
-    for axis, pairs in STAGES:
+    swap = ((0, 1), (1, 0))
+    received = lax.ppermute(other, CORE, swap)
+    for stage in range(len(ORDER[0])):
         mine = pl.pallas_call(
             add_kernel,
             out_shape=jax.ShapeDtypeStruct((packed, 128), jnp.bfloat16),
             in_specs=[vmem, vmem], out_specs=vmem, compiler_params=params, name="add_partials",
         )(mine, received)
-        received = lax.ppermute(mine, axis, pairs)
+        received = lax.ppermute(mine, AXES, stage_pairs(stage))
     coef, scale = pl.pallas_call(
         functools.partial(owner_kernel, nv=nv, nm=nm, count=float(nt * grid_points),
                           denom=float(nv * grid_points)),
@@ -309,20 +311,19 @@
                    jax.ShapeDtypeStruct((8, 128), jnp.float32)),
         in_specs=[vmem, vmem], out_specs=(vmem, vmem), compiler_params=params, name="owner_part",
     )(mine, received)
-    coef_other = lax.ppermute(coef, CORE, PAIR)
+    coef_other = lax.ppermute(coef, CORE, swap)
     modes, energy = pl.pallas_call(
         functools.partial(modes_kernel, nf=nf, nb=nb, nm=nm, nv=nv, nx=nx),
         out_shape=(jax.ShapeDtypeStruct((nf * 2 * nm * nvx, ny), jnp.float32),
                    jax.ShapeDtypeStruct((nm, nf), jnp.float32)),
-        in_specs=[vmem] * 4, out_specs=(hbm, vmem),
-        scratch_shapes=[pltpu.VMEM((nf * 2 * nm * nvx, ny), jnp.float32), pltpu.SemaphoreType.DMA((4,))],
-        compiler_params=params, name="modes_part",
+        in_specs=[vmem] * 4, out_specs=(vmem, vmem), compiler_params=params,
+        name="modes_part",
     )(coef, coef_other, scale, y)
     return modes.reshape(nf, 2, nm, nv, nx, ny), energy.T
 
 
 def solution(mesh):
-    finer = Mesh(mesh.devices.reshape(2, 4, 4, 4, 2), AXES)
+    finer = Mesh(mesh.devices.reshape(SIZES), AXES)
     placed = (P(None, None, SX, SY), P(None, SX, SY), P(), P(), P())
     return jax.shard_map(
         shards,

time: 51.3 us -> 51.2 us (level)
  starting transfers between devices: 19.1 us -> 21.9 us
  waiting for transfers between devices: 22 us -> 19.6 us
  Pallas kernels: 9.41 us -> 8.88 us
    ppermute x9, starting transfers between devices: 19.1 us -> 21.9 us  [the longest x7 10.5 us: shards(): received = lax.ppermute(mine, AXES, stage_pairs(stage))]
    ppermute x9, waiting for transfers between devices: 22 us -> 19.6 us  [the longest x7 17.9 us: shards(): received = lax.ppermute(mine, AXES, stage_pairs(stage))]
    pallas_call x1, Pallas kernels: 2 us -> 1.47 us  [shards(): pl.pallas_call(functools.partial(modes_kernel, nf=nf, nb=nb, nm=nm, nv=nv...]
where the time goes in v5:
time: 51.2 us; the launch traced here: 51.1 us
  starting transfers between devices  21.9 us (43%)
  waiting for transfers between devices  19.6 us (38%)
  Pallas kernels  8.88 us (17%)
  between operations  0.68 us (1%)
    ppermute x7, waiting for transfers between devices, shards(): received = lax.ppermute(mine, AXES, stage_pairs(stage))  17.9 us
    ppermute x7, starting transfers between devices, shards(): received = lax.ppermute(mine, AXES, stage_pairs(stage))  10.5 us
    ppermute x1, starting transfers between devices, shards(): coef_other = lax.ppermute(coef, CORE, swap)  8.09 us
    pallas_call x1, Pallas kernels, shards(): pl.pallas_call(functools.partial(local_kernel, nf=nf, nb=nb, nt=nt, nm=nm...  7.04 us
    ppermute x1, starting transfers between devices, shards(): received = lax.ppermute(other, CORE, swap)  3.33 us
    pallas_call x1, Pallas kernels, shards(): pl.pallas_call(functools.partial(modes_kernel, nf=nf, nb=nb, nm=nm, nv=nv...  1.47 us
  transfers between devices with their start and end apart: 9, of which 9 were waited for; matrix products, arithmetic and copies ran while one was open for 0% of the time, Pallas kernels for 0%

profile of v5, /device:TPU:1, one launch (start us, length us, event | category | flops | bytes accessed | tf_op | source)
XLA Modules:
  0.0 51.1 jit_solution(1831755703142774931)
XLA Ops:
  0.6 7.0 %local_part.1 = (bf16[2048,768]{1,0:T(8,128)(2,1)S(1)}, bf16[208,128]{1,0:T(8,128)(2,1)S(1)}, bf16[208,128]{1,0:T(8,128)(2,1)S(1)}) custom-call(s32[64]{0:T(128)} %starts_hbm.1, s32[16]{0:T(128)} %bins_hbm.1, bf16[6144,128]{1,0:T(8,128)(2,1)} %bitcast.4, f32[3,2,128]{2,1,0:T(2,128)} %w_hbm.1, f32[16,2,8,64]{3,2,1,0:T(8,128)} %bitcast.5), custom_call_target="tpu_custom_call" | custom-call | tf_op jit(solution)/shard_map/local_part/pallas_call | solution.py:271
  7.7 3.3 %collective-permute-start = (bf16[208,128]{1,0:T(8,128)(2,1)S(1)}, bf16[208,128]{1,0:T(8,128)(2,1)S(1)}, u32[]{:S(2)}, u32[]{:S(2)}) collective-permute-start(bf16[208,128]{1,0:T(8,128)(2,1)S(1)} %get-tuple-element.10), channel_id=1, source_target_pairs={{0,1},{1,0},{2,3},{3,2},{4,5},{5,4},{6,7},{7,6},{8,9},{9,8},{10,11... | collective-permute-start | bytes 159752 | tf_op jit(solution)/shard_map/ppermute | solution.py:299
  11.0 0.9 %collective-permute-done.b_ref = bf16[208,128]{1,0:T(8,128)(2,1)S(1)} collective-permute-done((bf16[208,128]{1,0:T(8,128)(2,1)S(1)}, bf16[208,128]{1,0:T(8,128)(2,1)S(1)}, u32[]{:S(2)}, u32[]{:S(2)}) %collective-permute-start) | collective-permute-done | bytes 53280 | tf_op jit(solution)/shard_map/ppermute | solution.py:299
  11.9 0.1 collective-permute-start.1
  12.0 3.0 %collective-permute-done.1.b_ref = bf16[208,128]{1,0:T(8,128)(2,1)S(1)} collective-permute-done((bf16[208,128]{1,0:T(8,128)(2,1)S(1)}, bf16[208,128]{1,0:T(8,128)(2,1)S(1)}, u32[]{:S(2)}, u32[]{:S(2)}) %collective-permute-start.1) | collective-permute-done | bytes 53280 | tf_op jit(solution)/shard_map/ppermute | solution.py:306
  15.0 0.1 collective-permute-start.2
  15.1 3.0 %collective-permute-done.2.b_ref = bf16[208,128]{1,0:T(8,128)(2,1)S(1)} collective-permute-done((bf16[208,128]{1,0:T(8,128)(2,1)S(1)}, bf16[208,128]{1,0:T(8,128)(2,1)S(1)}, u32[]{:S(2)}, u32[]{:S(2)}) %collective-permute-start.2) | collective-permute-done | bytes 53280 | tf_op jit(solution)/shard_map/ppermute | solution.py:306
  18.1 1.5 %collective-permute-start.3 = (bf16[208,128]{1,0:T(8,128)(2,1)S(1)}, bf16[208,128]{1,0:T(8,128)(2,1)S(1)}, u32[]{:S(2)}, u32[]{:S(2)}) collective-permute-start(bf16[208,128]{1,0:T(8,128)(2,1)S(1)} %add_partials.9.a_ref), channel_id=1, source_target_pairs={{0,8},{1,3},{2,10},{3,1},{4,12},{5,7},{6,14},{7,5},{8,0},{9,11},{1... | collective-permute-start | bytes 159752 | tf_op jit(solution)/shard_map/ppermute | solution.py:306
  19.6 3.0 %collective-permute-done.3.b_ref = bf16[208,128]{1,0:T(8,128)(2,1)S(1)} collective-permute-done((bf16[208,128]{1,0:T(8,128)(2,1)S(1)}, bf16[208,128]{1,0:T(8,128)(2,1)S(1)}, u32[]{:S(2)}, u32[]{:S(2)}) %collective-permute-start.3) | collective-permute-done | bytes 53280 | tf_op jit(solution)/shard_map/ppermute | solution.py:306
  22.7 0.1 collective-permute-start.4
  22.8 3.0 %collective-permute-done.4.b_ref = bf16[208,128]{1,0:T(8,128)(2,1)S(1)} collective-permute-done((bf16[208,128]{1,0:T(8,128)(2,1)S(1)}, bf16[208,128]{1,0:T(8,128)(2,1)S(1)}, u32[]{:S(2)}, u32[]{:S(2)}) %collective-permute-start.4) | collective-permute-done | bytes 53280 | tf_op jit(solution)/shard_map/ppermute | solution.py:306
  25.8 3.9 %collective-permute-start.5 = (bf16[208,128]{1,0:T(8,128)(2,1)S(1)}, bf16[208,128]{1,0:T(8,128)(2,1)S(1)}, u32[]{:S(2)}, u32[]{:S(2)}) collective-permute-start(bf16[208,128]{1,0:T(8,128)(2,1)S(1)} %add_partials.11.a_ref), channel_id=1, source_target_pairs={{0,96},{1,7},{2,98},{3,5},{4,100},{5,3},{6,102},{7,1},{8,104},{9,1... | collective-permute-start | bytes 159752 | tf_op jit(solution)/shard_map/ppermute | solution.py:306
  29.7 1.6 %collective-permute-done.5.b_ref = bf16[208,128]{1,0:T(8,128)(2,1)S(1)} collective-permute-done((bf16[208,128]{1,0:T(8,128)(2,1)S(1)}, bf16[208,128]{1,0:T(8,128)(2,1)S(1)}, u32[]{:S(2)}, u32[]{:S(2)}) %collective-permute-start.5) | collective-permute-done | bytes 53280 | tf_op jit(solution)/shard_map/ppermute | solution.py:306
  31.3 2.6 %collective-permute-start.6 = (bf16[208,128]{1,0:T(8,128)(2,1)S(1)}, bf16[208,128]{1,0:T(8,128)(2,1)S(1)}, u32[]{:S(2)}, u32[]{:S(2)}) collective-permute-start(bf16[208,128]{1,0:T(8,128)(2,1)S(1)} %add_partials.12.a_ref), channel_id=1, source_target_pairs={{0,24},{1,97},{2,26},{3,99},{4,28},{5,101},{6,30},{7,103},{8,16},{... | collective-permute-start | bytes 159752 | tf_op jit(solution)/shard_map/ppermute | solution.py:306
  33.9 2.3 %collective-permute-done.6.b_ref = bf16[208,128]{1,0:T(8,128)(2,1)S(1)} collective-permute-done((bf16[208,128]{1,0:T(8,128)(2,1)S(1)}, bf16[208,128]{1,0:T(8,128)(2,1)S(1)}, u32[]{:S(2)}, u32[]{:S(2)}) %collective-permute-start.6) | collective-permute-done | bytes 53280 | tf_op jit(solution)/shard_map/ppermute | solution.py:306
  36.2 2.2 %collective-permute-start.7 = (bf16[208,128]{1,0:T(8,128)(2,1)S(1)}, bf16[208,128]{1,0:T(8,128)(2,1)S(1)}, u32[]{:S(2)}, u32[]{:S(2)}) collective-permute-start(bf16[208,128]{1,0:T(8,128)(2,1)S(1)} %add_partials.13.a_ref), channel_id=1, source_target_pairs={{0,6},{1,25},{2,4},{3,27},{4,2},{5,29},{6,0},{7,31},{8,14},{9,17},... | collective-permute-start | bytes 159752 | tf_op jit(solution)/shard_map/ppermute | solution.py:306
  38.4 2.1 %collective-permute-done.7.b_ref = bf16[208,128]{1,0:T(8,128)(2,1)S(1)} collective-permute-done((bf16[208,128]{1,0:T(8,128)(2,1)S(1)}, bf16[208,128]{1,0:T(8,128)(2,1)S(1)}, u32[]{:S(2)}, u32[]{:S(2)}) %collective-permute-start.7) | collective-permute-done | bytes 53280 | tf_op jit(solution)/shard_map/ppermute | solution.py:306
  40.5 0.2 owner_part.1
  40.7 8.1 %collective-permute-start.8 = (bf16[128,128]{1,0:T(8,128)(2,1)S(1)}, bf16[128,128]{1,0:T(8,128)(2,1)S(1)}, u32[]{:S(2)}, u32[]{:S(2)}) collective-permute-start(bf16[128,128]{1,0:T(8,128)(2,1)S(1)} %get-tuple-element.11.mine_ref), channel_id=1, source_target_pairs={{0,1},{1,0},{2,3},{3,2},{4,5},{5,4},{6,7},{7,6},{8,9},{9,8},{10,11... | collective-permute-start | bytes 98312 | tf_op jit(solution)/shard_map/ppermute | solution.py:314
  48.8 0.9 %collective-permute-done.8.other_ref = bf16[128,128]{1,0:T(8,128)(2,1)S(1)} collective-permute-done((bf16[128,128]{1,0:T(8,128)(2,1)S(1)}, bf16[128,128]{1,0:T(8,128)(2,1)S(1)}, u32[]{:S(2)}, u32[]{:S(2)}) %collective-permute-start.8) | collective-permute-done | bytes 32800 | tf_op jit(solution)/shard_map/ppermute | solution.py:314
  49.6 1.5 %modes_part.1 = (f32[1536,128]{1,0:T(8,128)}, f32[8,16]{1,0:T(8,128)}) custom-call(bf16[128,128]{1,0:T(8,128)(2,1)S(1)} %get-tuple-element.11.mine_ref, bf16[128,128]{1,0:T(8,128)(2,1)S(1)} %collective-permute-done.8.other_ref, f32[8,128]{1,0:T(8,128)S(1)} %get-tuple-element.12.s_ref, bf16[2048,768]{1,0:T(8,128)(2,1)S(1)} %get-tuple-element.13.y_ref), custom_call_target="tpu_custom_call" | custom-call | tf_op jit(solution)/shard_map/modes_part/pallas_call | solution.py:315
  (7 shorter events, 0.2 us)
Async XLA Ops:
  7.7 4.2 %collective-permute-start = (bf16[208,128]{1,0:T(8,128)(2,1)S(1)}, bf16[208,128]{1,0:T(8,128)(2,1)S(1)}, u32[]{:S(2)}, u32[]{:S(2)}) collective-permute-start(bf16[208,128]{1,0:T(8,128)(2,1)S(1)} %get-tuple-element.10), channel_id=1, source_target_pairs={{0,1},{1,0},{2,3},{3,2},{4,5},{5,4},{6,7},{7,6},{8,9},{9,8},{10,11... | collective-permute-start | bytes 159752 | tf_op jit(solution)/shard_map/ppermute | solution.py:299
  11.9 3.1 %collective-permute-start.1 = (bf16[208,128]{1,0:T(8,128)(2,1)S(1)}, bf16[208,128]{1,0:T(8,128)(2,1)S(1)}, u32[]{:S(2)}, u32[]{:S(2)}) collective-permute-start(bf16[208,128]{1,0:T(8,128)(2,1)S(1)} %add_partials.7.a_ref), channel_id=1, source_target_pairs={{0,128},{1,33},{2,130},{3,35},{4,132},{5,37},{6,134},{7,39},{8,136... | collective-permute-start | bytes 159752 | tf_op jit(solution)/shard_map/ppermute | solution.py:306
  15.0 3.1 %collective-permute-start.2 = (bf16[208,128]{1,0:T(8,128)(2,1)S(1)}, bf16[208,128]{1,0:T(8,128)(2,1)S(1)}, u32[]{:S(2)}, u32[]{:S(2)}) collective-permute-start(bf16[208,128]{1,0:T(8,128)(2,1)S(1)} %add_partials.8.a_ref), channel_id=1, source_target_pairs={{0,32},{1,129},{2,34},{3,131},{4,36},{5,133},{6,38},{7,135},{8,40}... | collective-permute-start | bytes 159752 | tf_op jit(solution)/shard_map/ppermute | solution.py:306
  18.1 4.5 %collective-permute-start.3 = (bf16[208,128]{1,0:T(8,128)(2,1)S(1)}, bf16[208,128]{1,0:T(8,128)(2,1)S(1)}, u32[]{:S(2)}, u32[]{:S(2)}) collective-permute-start(bf16[208,128]{1,0:T(8,128)(2,1)S(1)} %add_partials.9.a_ref), channel_id=1, source_target_pairs={{0,8},{1,3},{2,10},{3,1},{4,12},{5,7},{6,14},{7,5},{8,0},{9,11},{1... | collective-permute-start | bytes 159752 | tf_op jit(solution)/shard_map/ppermute | solution.py:306
  22.7 3.1 %collective-permute-start.4 = (bf16[208,128]{1,0:T(8,128)(2,1)S(1)}, bf16[208,128]{1,0:T(8,128)(2,1)S(1)}, u32[]{:S(2)}, u32[]{:S(2)}) collective-permute-start(bf16[208,128]{1,0:T(8,128)(2,1)S(1)} %add_partials.10.a_ref), channel_id=1, source_target_pairs={{0,2},{1,9},{2,0},{3,11},{4,6},{5,13},{6,4},{7,15},{8,10},{9,1},{1... | collective-permute-start | bytes 159752 | tf_op jit(solution)/shard_map/ppermute | solution.py:306
  25.8 5.5 %collective-permute-start.5 = (bf16[208,128]{1,0:T(8,128)(2,1)S(1)}, bf16[208,128]{1,0:T(8,128)(2,1)S(1)}, u32[]{:S(2)}, u32[]{:S(2)}) collective-permute-start(bf16[208,128]{1,0:T(8,128)(2,1)S(1)} %add_partials.11.a_ref), channel_id=1, source_target_pairs={{0,96},{1,7},{2,98},{3,5},{4,100},{5,3},{6,102},{7,1},{8,104},{9,1... | collective-permute-start | bytes 159752 | tf_op jit(solution)/shard_map/ppermute | solution.py:306
  31.3 4.9 %collective-permute-start.6 = (bf16[208,128]{1,0:T(8,128)(2,1)S(1)}, bf16[208,128]{1,0:T(8,128)(2,1)S(1)}, u32[]{:S(2)}, u32[]{:S(2)}) collective-permute-start(bf16[208,128]{1,0:T(8,128)(2,1)S(1)} %add_partials.12.a_ref), channel_id=1, source_target_pairs={{0,24},{1,97},{2,26},{3,99},{4,28},{5,101},{6,30},{7,103},{8,16},{... | collective-permute-start | bytes 159752 | tf_op jit(solution)/shard_map/ppermute | solution.py:306
  36.2 4.3 %collective-permute-start.7 = (bf16[208,128]{1,0:T(8,128)(2,1)S(1)}, bf16[208,128]{1,0:T(8,128)(2,1)S(1)}, u32[]{:S(2)}, u32[]{:S(2)}) collective-permute-start(bf16[208,128]{1,0:T(8,128)(2,1)S(1)} %add_partials.13.a_ref), channel_id=1, source_target_pairs={{0,6},{1,25},{2,4},{3,27},{4,2},{5,29},{6,0},{7,31},{8,14},{9,17},... | collective-permute-start | bytes 159752 | tf_op jit(solution)/shard_map/ppermute | solution.py:306
  40.7 8.9 %collective-permute-start.8 = (bf16[128,128]{1,0:T(8,128)(2,1)S(1)}, bf16[128,128]{1,0:T(8,128)(2,1)S(1)}, u32[]{:S(2)}, u32[]{:S(2)}) collective-permute-start(bf16[128,128]{1,0:T(8,128)(2,1)S(1)} %get-tuple-element.11.mine_ref), channel_id=1, source_target_pairs={{0,1},{1,0},{2,3},{3,2},{4,5},{5,4},{6,7},{7,6},{8,9},{9,8},{10,11... | collective-permute-start | bytes 98312 | tf_op jit(solution)/shard_map/ppermute | solution.py:314

commit v6 on v5

--- a/solution.py
+++ b/solution.py
@@ -19,22 +19,26 @@
 NEAR4 = (1, 0, 3, 2)
 RING4 = (3, 2, 1, 0)
 PAIR = (1, 0)
-ORDER = (
-    ((0, PAIR), (1, NEAR4), (2, NEAR4), (3, NEAR4), (1, RING4), (2, RING4), (3, RING4)),
-    ((1, NEAR4), (0, PAIR), (3, NEAR4), (2, NEAR4), (3, RING4), (1, RING4), (2, RING4)),
-)
+STAGES = ((0, PAIR), (1, NEAR4), (2, NEAR4), (1, RING4), (2, RING4), (3, NEAR4), (3, RING4))
 CORE = "sy_1"
 MIB = 1 << 20
 
 
-def stage_pairs(stage):
+def stage_pairs(axis, partner):
     pairs = []
     for at in np.ndindex(*SIZES):
-        axis, partner = ORDER[at[-1]][stage]
         to = list(at)
         to[axis] = partner[at[axis]]
+        to[-1] = 1 - at[-1]
         pairs.append((int(np.ravel_multi_index(at, SIZES)), int(np.ravel_multi_index(to, SIZES))))
     return pairs
+
+
+def owned_half():
+    total = lax.axis_index(AXES[0])
+    for name in AXES[1:]:
+        total = total + lax.axis_index(name)
+    return total & 1
 
 
 def split3(x):
@@ -67,7 +71,7 @@
                  *, nf, nb, nt, nm, nv, nx):
     nvx = nv * nx
     rows = nt * nvx
-    core = lax.axis_index(CORE)
+    own = owned_half()
     nchunk = xb.shape[0]
     chunk = rows // nchunk
 
@@ -189,8 +193,8 @@
     cut = nf // 2 * nv * nm
     low_half = zall[:cut, :].astype(jnp.float32)
     high_half = zall[cut:, :].astype(jnp.float32)
-    mine_ref[:cut, :] = jnp.where(core == 0, low_half, high_half).astype(jnp.bfloat16)
-    other_ref[:cut, :] = jnp.where(core == 0, high_half, low_half).astype(jnp.bfloat16)
+    mine_ref[:cut, :] = jnp.where(own == 0, low_half, high_half).astype(jnp.bfloat16)
+    other_ref[:cut, :] = jnp.where(own == 0, high_half, low_half).astype(jnp.bfloat16)
 
 
 def add_kernel(a_ref, b_ref, o_ref):
@@ -229,8 +233,7 @@
 
 def modes_kernel(mine_ref, other_ref, s_ref, y_ref, o_ref, e_ref, *, nf, nb, nm, nv, nx):
     nvx = nv * nx
-    core = lax.axis_index(CORE)
-    first = core == 0
+    first = owned_half() == 0
     mine = mine_ref[...].astype(jnp.float32)
     other = other_ref[...].astype(jnp.float32)
     halves = (jnp.where(first, mine, other), jnp.where(first, other, mine))
@@ -297,13 +300,13 @@
     )(*[pltpu.with_memory_space_constraint(a, pltpu.HBM) for a in (starts, bins, x, quad_weight, guess)])
     swap = ((0, 1), (1, 0))
     received = lax.ppermute(other, CORE, swap)
-    for stage in range(len(ORDER[0])):
+    for stage in STAGES:
         mine = pl.pallas_call(
             add_kernel,
             out_shape=jax.ShapeDtypeStruct((packed, 128), jnp.bfloat16),
             in_specs=[vmem, vmem], out_specs=vmem, compiler_params=params, name="add_partials",
         )(mine, received)
-        received = lax.ppermute(mine, AXES, stage_pairs(stage))
+        received = lax.ppermute(mine, AXES, stage_pairs(*stage))
     coef, scale = pl.pallas_call(
         functools.partial(owner_kernel, nv=nv, nm=nm, count=float(nt * grid_points),
                           denom=float(nv * grid_points)),

time: 51.2 us -> 49.5 us (0.967)
  starting transfers between devices: 21.9 us -> 11.4 us
  waiting for transfers between devices: 19.6 us -> 28.5 us
    ppermute x7, waiting for transfers between devices: 17.9 us -> 26.7 us  [shards(): received = lax.ppermute(mine, AXES, stage_pairs(*stage))]
    ppermute x1, starting transfers between devices: 8.09 us -> 0.48 us  [shards(): coef_other = lax.ppermute(coef, CORE, swap)]
    ppermute x7, starting transfers between devices: 10.5 us -> 7.54 us  [shards(): received = lax.ppermute(mine, AXES, stage_pairs(*stage))]
where the time goes in v6:
time: 49.5 us; the launch traced here: 49.4 us
  waiting for transfers between devices  28.5 us (58%)
  starting transfers between devices  11.4 us (23%)
  Pallas kernels  8.89 us (18%)
  between operations  0.67 us (1%)
    ppermute x7, waiting for transfers between devices, shards(): received = lax.ppermute(mine, AXES, stage_pairs(*stage))  26.7 us
    ppermute x7, starting transfers between devices, shards(): received = lax.ppermute(mine, AXES, stage_pairs(*stage))  7.54 us
    pallas_call x1, Pallas kernels, shards(): pl.pallas_call(functools.partial(local_kernel, nf=nf, nb=nb, nt=nt, nm=nm...  7.03 us
    ppermute x1, starting transfers between devices, shards(): received = lax.ppermute(other, CORE, swap)  3.33 us
    pallas_call x1, Pallas kernels, shards(): pl.pallas_call(functools.partial(modes_kernel, nf=nf, nb=nb, nm=nm, nv=nv...  1.48 us
  transfers between devices with their start and end apart: 9, of which 9 were waited for; matrix products, arithmetic and copies ran while one was open for 0% of the time, Pallas kernels for 0%

profile of v6, /device:TPU:1, one launch (start us, length us, event | category | flops | bytes accessed | tf_op | source)
XLA Modules:
  0.0 49.4 jit_solution(15650673650392257401)
XLA Ops:
  0.6 7.0 %local_part.1 = (bf16[2048,768]{1,0:T(8,128)(2,1)S(1)}, bf16[208,128]{1,0:T(8,128)(2,1)S(1)}, bf16[208,128]{1,0:T(8,128)(2,1)S(1)}) custom-call(s32[64]{0:T(128)} %starts_hbm.1, s32[16]{0:T(128)} %bins_hbm.1, bf16[6144,128]{1,0:T(8,128)(2,1)} %bitcast.4, f32[3,2,128]{2,1,0:T(2,128)} %w_hbm.1, f32[16,2,8,64]{3,2,1,0:T(8,128)} %bitcast.5), custom_call_target="tpu_custom_call" | custom-call | tf_op jit(solution)/shard_map/local_part/pallas_call | solution.py:274
  7.7 3.3 %collective-permute-start = (bf16[208,128]{1,0:T(8,128)(2,1)S(1)}, bf16[208,128]{1,0:T(8,128)(2,1)S(1)}, u32[]{:S(2)}, u32[]{:S(2)}) collective-permute-start(bf16[208,128]{1,0:T(8,128)(2,1)S(1)} %get-tuple-element.10), channel_id=1, source_target_pairs={{0,1},{1,0},{2,3},{3,2},{4,5},{5,4},{6,7},{7,6},{8,9},{9,8},{10,11... | collective-permute-start | bytes 159752 | tf_op jit(solution)/shard_map/ppermute | solution.py:302
  11.0 0.9 %collective-permute-done.b_ref = bf16[208,128]{1,0:T(8,128)(2,1)S(1)} collective-permute-done((bf16[208,128]{1,0:T(8,128)(2,1)S(1)}, bf16[208,128]{1,0:T(8,128)(2,1)S(1)}, u32[]{:S(2)}, u32[]{:S(2)}) %collective-permute-start) | collective-permute-done | bytes 53280 | tf_op jit(solution)/shard_map/ppermute | solution.py:302
  11.9 0.2 collective-permute-start.1
  12.1 3.7 %collective-permute-done.1.b_ref = bf16[208,128]{1,0:T(8,128)(2,1)S(1)} collective-permute-done((bf16[208,128]{1,0:T(8,128)(2,1)S(1)}, bf16[208,128]{1,0:T(8,128)(2,1)S(1)}, u32[]{:S(2)}, u32[]{:S(2)}) %collective-permute-start.1) | collective-permute-done | bytes 53280 | tf_op jit(solution)/shard_map/ppermute | solution.py:309
  15.8 0.1 collective-permute-start.2
  15.9 3.8 %collective-permute-done.2.b_ref = bf16[208,128]{1,0:T(8,128)(2,1)S(1)} collective-permute-done((bf16[208,128]{1,0:T(8,128)(2,1)S(1)}, bf16[208,128]{1,0:T(8,128)(2,1)S(1)}, u32[]{:S(2)}, u32[]{:S(2)}) %collective-permute-start.2) | collective-permute-done | bytes 53280 | tf_op jit(solution)/shard_map/ppermute | solution.py:309
  19.7 0.1 collective-permute-start.3
  19.8 3.8 %collective-permute-done.3.b_ref = bf16[208,128]{1,0:T(8,128)(2,1)S(1)} collective-permute-done((bf16[208,128]{1,0:T(8,128)(2,1)S(1)}, bf16[208,128]{1,0:T(8,128)(2,1)S(1)}, u32[]{:S(2)}, u32[]{:S(2)}) %collective-permute-start.3) | collective-permute-done | bytes 53280 | tf_op jit(solution)/shard_map/ppermute | solution.py:309
  23.7 1.0 %collective-permute-start.4 = (bf16[208,128]{1,0:T(8,128)(2,1)S(1)}, bf16[208,128]{1,0:T(8,128)(2,1)S(1)}, u32[]{:S(2)}, u32[]{:S(2)}) collective-permute-start(bf16[208,128]{1,0:T(8,128)(2,1)S(1)} %add_partials.10.a_ref), channel_id=1, source_target_pairs={{0,97},{1,96},{2,99},{3,98},{4,101},{5,100},{6,103},{7,102},{8,105... | collective-permute-start | bytes 159752 | tf_op jit(solution)/shard_map/ppermute | solution.py:309
  24.7 4.1 %collective-permute-done.4.b_ref = bf16[208,128]{1,0:T(8,128)(2,1)S(1)} collective-permute-done((bf16[208,128]{1,0:T(8,128)(2,1)S(1)}, bf16[208,128]{1,0:T(8,128)(2,1)S(1)}, u32[]{:S(2)}, u32[]{:S(2)}) %collective-permute-start.4) | collective-permute-done | bytes 53280 | tf_op jit(solution)/shard_map/ppermute | solution.py:309
  28.8 1.2 %collective-permute-start.5 = (bf16[208,128]{1,0:T(8,128)(2,1)S(1)}, bf16[208,128]{1,0:T(8,128)(2,1)S(1)}, u32[]{:S(2)}, u32[]{:S(2)}) collective-permute-start(bf16[208,128]{1,0:T(8,128)(2,1)S(1)} %add_partials.11.a_ref), channel_id=1, source_target_pairs={{0,25},{1,24},{2,27},{3,26},{4,29},{5,28},{6,31},{7,30},{8,17},{9,... | collective-permute-start | bytes 159752 | tf_op jit(solution)/shard_map/ppermute | solution.py:309
  30.0 3.9 %collective-permute-done.5.b_ref = bf16[208,128]{1,0:T(8,128)(2,1)S(1)} collective-permute-done((bf16[208,128]{1,0:T(8,128)(2,1)S(1)}, bf16[208,128]{1,0:T(8,128)(2,1)S(1)}, u32[]{:S(2)}, u32[]{:S(2)}) %collective-permute-start.5) | collective-permute-done | bytes 53280 | tf_op jit(solution)/shard_map/ppermute | solution.py:309
  34.0 1.5 %collective-permute-start.6 = (bf16[208,128]{1,0:T(8,128)(2,1)S(1)}, bf16[208,128]{1,0:T(8,128)(2,1)S(1)}, u32[]{:S(2)}, u32[]{:S(2)}) collective-permute-start(bf16[208,128]{1,0:T(8,128)(2,1)S(1)} %add_partials.12.a_ref), channel_id=1, source_target_pairs={{0,3},{1,2},{2,1},{3,0},{4,7},{5,6},{6,5},{7,4},{8,11},{9,10},{10,... | collective-permute-start | bytes 159752 | tf_op jit(solution)/shard_map/ppermute | solution.py:309
  35.5 4.7 %collective-permute-done.6.b_ref = bf16[208,128]{1,0:T(8,128)(2,1)S(1)} collective-permute-done((bf16[208,128]{1,0:T(8,128)(2,1)S(1)}, bf16[208,128]{1,0:T(8,128)(2,1)S(1)}, u32[]{:S(2)}, u32[]{:S(2)}) %collective-permute-start.6) | collective-permute-done | bytes 53280 | tf_op jit(solution)/shard_map/ppermute | solution.py:309
  40.2 3.4 %collective-permute-start.7 = (bf16[208,128]{1,0:T(8,128)(2,1)S(1)}, bf16[208,128]{1,0:T(8,128)(2,1)S(1)}, u32[]{:S(2)}, u32[]{:S(2)}) collective-permute-start(bf16[208,128]{1,0:T(8,128)(2,1)S(1)} %add_partials.13.a_ref), channel_id=1, source_target_pairs={{0,7},{1,6},{2,5},{3,4},{4,3},{5,2},{6,1},{7,0},{8,15},{9,14},{10,... | collective-permute-start | bytes 159752 | tf_op jit(solution)/shard_map/ppermute | solution.py:309
  43.6 2.8 %collective-permute-done.7.b_ref = bf16[208,128]{1,0:T(8,128)(2,1)S(1)} collective-permute-done((bf16[208,128]{1,0:T(8,128)(2,1)S(1)}, bf16[208,128]{1,0:T(8,128)(2,1)S(1)}, u32[]{:S(2)}, u32[]{:S(2)}) %collective-permute-start.7) | collective-permute-done | bytes 53280 | tf_op jit(solution)/shard_map/ppermute | solution.py:309
  46.4 0.2 owner_part.1
  46.5 0.5 collective-permute-start.8
  47.0 0.9 %collective-permute-done.8.other_ref = bf16[128,128]{1,0:T(8,128)(2,1)S(1)} collective-permute-done((bf16[128,128]{1,0:T(8,128)(2,1)S(1)}, bf16[128,128]{1,0:T(8,128)(2,1)S(1)}, u32[]{:S(2)}, u32[]{:S(2)}) %collective-permute-start.8) | collective-permute-done | bytes 32800 | tf_op jit(solution)/shard_map/ppermute | solution.py:317
  47.9 1.5 %modes_part.1 = (f32[1536,128]{1,0:T(8,128)}, f32[8,16]{1,0:T(8,128)}) custom-call(bf16[128,128]{1,0:T(8,128)(2,1)S(1)} %get-tuple-element.11.mine_ref, bf16[128,128]{1,0:T(8,128)(2,1)S(1)} %collective-permute-done.8.other_ref, f32[8,128]{1,0:T(8,128)S(1)} %get-tuple-element.12.s_ref, bf16[2048,768]{1,0:T(8,128)(2,1)S(1)} %get-tuple-element.13.y_ref), custom_call_target="tpu_custom_call" | custom-call | tf_op jit(solution)/shard_map/modes_part/pallas_call | solution.py:318
  (7 shorter events, 0.2 us)
Async XLA Ops:
  7.7 4.2 %collective-permute-start = (bf16[208,128]{1,0:T(8,128)(2,1)S(1)}, bf16[208,128]{1,0:T(8,128)(2,1)S(1)}, u32[]{:S(2)}, u32[]{:S(2)}) collective-permute-start(bf16[208,128]{1,0:T(8,128)(2,1)S(1)} %get-tuple-element.10), channel_id=1, source_target_pairs={{0,1},{1,0},{2,3},{3,2},{4,5},{5,4},{6,7},{7,6},{8,9},{9,8},{10,11... | collective-permute-start | bytes 159752 | tf_op jit(solution)/shard_map/ppermute | solution.py:302
  11.9 3.9 %collective-permute-start.1 = (bf16[208,128]{1,0:T(8,128)(2,1)S(1)}, bf16[208,128]{1,0:T(8,128)(2,1)S(1)}, u32[]{:S(2)}, u32[]{:S(2)}) collective-permute-start(bf16[208,128]{1,0:T(8,128)(2,1)S(1)} %add_partials.7.a_ref), channel_id=1, source_target_pairs={{0,129},{1,128},{2,131},{3,130},{4,133},{5,132},{6,135},{7,134},{8... | collective-permute-start | bytes 159752 | tf_op jit(solution)/shard_map/ppermute | solution.py:309
  15.8 3.9 %collective-permute-start.2 = (bf16[208,128]{1,0:T(8,128)(2,1)S(1)}, bf16[208,128]{1,0:T(8,128)(2,1)S(1)}, u32[]{:S(2)}, u32[]{:S(2)}) collective-permute-start(bf16[208,128]{1,0:T(8,128)(2,1)S(1)} %add_partials.8.a_ref), channel_id=1, source_target_pairs={{0,33},{1,32},{2,35},{3,34},{4,37},{5,36},{6,39},{7,38},{8,41},{9,... | collective-permute-start | bytes 159752 | tf_op jit(solution)/shard_map/ppermute | solution.py:309
  19.7 3.9 %collective-permute-start.3 = (bf16[208,128]{1,0:T(8,128)(2,1)S(1)}, bf16[208,128]{1,0:T(8,128)(2,1)S(1)}, u32[]{:S(2)}, u32[]{:S(2)}) collective-permute-start(bf16[208,128]{1,0:T(8,128)(2,1)S(1)} %add_partials.9.a_ref), channel_id=1, source_target_pairs={{0,9},{1,8},{2,11},{3,10},{4,13},{5,12},{6,15},{7,14},{8,1},{9,0},... | collective-permute-start | bytes 159752 | tf_op jit(solution)/shard_map/ppermute | solution.py:309
  23.7 5.1 %collective-permute-start.4 = (bf16[208,128]{1,0:T(8,128)(2,1)S(1)}, bf16[208,128]{1,0:T(8,128)(2,1)S(1)}, u32[]{:S(2)}, u32[]{:S(2)}) collective-permute-start(bf16[208,128]{1,0:T(8,128)(2,1)S(1)} %add_partials.10.a_ref), channel_id=1, source_target_pairs={{0,97},{1,96},{2,99},{3,98},{4,101},{5,100},{6,103},{7,102},{8,105... | collective-permute-start | bytes 159752 | tf_op jit(solution)/shard_map/ppermute | solution.py:309
  28.8 5.1 %collective-permute-start.5 = (bf16[208,128]{1,0:T(8,128)(2,1)S(1)}, bf16[208,128]{1,0:T(8,128)(2,1)S(1)}, u32[]{:S(2)}, u32[]{:S(2)}) collective-permute-start(bf16[208,128]{1,0:T(8,128)(2,1)S(1)} %add_partials.11.a_ref), channel_id=1, source_target_pairs={{0,25},{1,24},{2,27},{3,26},{4,29},{5,28},{6,31},{7,30},{8,17},{9,... | collective-permute-start | bytes 159752 | tf_op jit(solution)/shard_map/ppermute | solution.py:309
  34.0 6.2 %collective-permute-start.6 = (bf16[208,128]{1,0:T(8,128)(2,1)S(1)}, bf16[208,128]{1,0:T(8,128)(2,1)S(1)}, u32[]{:S(2)}, u32[]{:S(2)}) collective-permute-start(bf16[208,128]{1,0:T(8,128)(2,1)S(1)} %add_partials.12.a_ref), channel_id=1, source_target_pairs={{0,3},{1,2},{2,1},{3,0},{4,7},{5,6},{6,5},{7,4},{8,11},{9,10},{10,... | collective-permute-start | bytes 159752 | tf_op jit(solution)/shard_map/ppermute | solution.py:309
  40.2 6.1 %collective-permute-start.7 = (bf16[208,128]{1,0:T(8,128)(2,1)S(1)}, bf16[208,128]{1,0:T(8,128)(2,1)S(1)}, u32[]{:S(2)}, u32[]{:S(2)}) collective-permute-start(bf16[208,128]{1,0:T(8,128)(2,1)S(1)} %add_partials.13.a_ref), channel_id=1, source_target_pairs={{0,7},{1,6},{2,5},{3,4},{4,3},{5,2},{6,1},{7,0},{8,15},{9,14},{10,... | collective-permute-start | bytes 159752 | tf_op jit(solution)/shard_map/ppermute | solution.py:309
  46.5 1.3 %collective-permute-start.8 = (bf16[128,128]{1,0:T(8,128)(2,1)S(1)}, bf16[128,128]{1,0:T(8,128)(2,1)S(1)}, u32[]{:S(2)}, u32[]{:S(2)}) collective-permute-start(bf16[128,128]{1,0:T(8,128)(2,1)S(1)} %get-tuple-element.11.mine_ref), channel_id=1, source_target_pairs={{0,1},{1,0},{2,3},{3,2},{4,5},{5,4},{6,7},{7,6},{8,9},{9,8},{10,11... | collective-permute-start | bytes 98312 | tf_op jit(solution)/shard_map/ppermute | solution.py:317

commit v7 on v6

--- a/solution.py
+++ b/solution.py
@@ -16,20 +16,19 @@
 SX = AXES[:3]
 SY = AXES[3:]
 SIZES = (2, 4, 4, 4, 2)
-NEAR4 = (1, 0, 3, 2)
-RING4 = (3, 2, 1, 0)
-PAIR = (1, 0)
-STAGES = ((0, PAIR), (1, NEAR4), (2, NEAR4), (1, RING4), (2, RING4), (3, NEAR4), (3, RING4))
+STEPS = (((0, 1), (3, 1)), ((1, 1), (1, 3)), ((2, 1), (2, 3)))
+LAST = ((3, 3),)
 CORE = "sy_1"
 MIB = 1 << 20
 
 
-def stage_pairs(axis, partner):
+def flip_pairs(*flips):
     pairs = []
     for at in np.ndindex(*SIZES):
         to = list(at)
-        to[axis] = partner[at[axis]]
-        to[-1] = 1 - at[-1]
+        for axis, mask in flips:
+            to[axis] ^= mask
+            to[-1] ^= 1
         pairs.append((int(np.ravel_multi_index(at, SIZES)), int(np.ravel_multi_index(to, SIZES))))
     return pairs
 
@@ -197,9 +196,13 @@
     other_ref[:cut, :] = jnp.where(own == 0, high_half, low_half).astype(jnp.bfloat16)
 
 
-def add_kernel(a_ref, b_ref, o_ref):
+def add_kernel(*refs):
+    o_ref = refs[-1]
     cut = o_ref.shape[0] - TAIL
-    total = a_ref[...].astype(jnp.float32) + b_ref[...].astype(jnp.float32)
+    terms = [r[...].astype(jnp.float32) for r in refs[:-1]]
+    while len(terms) > 1:
+        terms = [terms[i] + terms[i + 1] for i in range(0, len(terms), 2)]
+    total = terms[0]
     o_ref[:cut, :] = total[:cut].astype(jnp.bfloat16)
     o_ref[cut:, :] = as_rows(from_rows(total[cut:]))
 
@@ -299,21 +302,23 @@
         name="local_part",
     )(*[pltpu.with_memory_space_constraint(a, pltpu.HBM) for a in (starts, bins, x, quad_weight, guess)])
     swap = ((0, 1), (1, 0))
-    received = lax.ppermute(other, CORE, swap)
-    for stage in STAGES:
+    received = [lax.ppermute(other, CORE, swap)]
+    for step in STEPS + (LAST,):
         mine = pl.pallas_call(
             add_kernel,
             out_shape=jax.ShapeDtypeStruct((packed, 128), jnp.bfloat16),
-            in_specs=[vmem, vmem], out_specs=vmem, compiler_params=params, name="add_partials",
-        )(mine, received)
-        received = lax.ppermute(mine, AXES, stage_pairs(*stage))
+            in_specs=[vmem] * (1 + len(received)), out_specs=vmem, compiler_params=params,
+            name="add_partials",
+        )(mine, *received)
+        moves = [step] if len(step) == 1 else [step[:1], step[1:], step]
+        received = [lax.ppermute(mine, AXES, flip_pairs(*move)) for move in moves]
     coef, scale = pl.pallas_call(
         functools.partial(owner_kernel, nv=nv, nm=nm, count=float(nt * grid_points),
                           denom=float(nv * grid_points)),
         out_shape=(jax.ShapeDtypeStruct((nf * nm, 128), jnp.bfloat16),
                    jax.ShapeDtypeStruct((8, 128), jnp.float32)),
         in_specs=[vmem, vmem], out_specs=(vmem, vmem), compiler_params=params, name="owner_part",
-    )(mine, received)
+    )(mine, *received)
     coef_other = lax.ppermute(coef, CORE, swap)
     modes, energy = pl.pallas_call(
         functools.partial(modes_kernel, nf=nf, nb=nb, nm=nm, nv=nv, nx=nx),

time: 49.5 us -> 46.5 us (0.939)
  waiting for transfers between devices: 28.5 us -> 17.7 us
  starting transfers between devices: 11.4 us -> 19.2 us
    ppermute x8 -> x11, waiting for transfers between devices: 27.6 us -> 16.8 us  [the longest x10 15.9 us: shards(): received = [lax.ppermute(mine, AXES, flip_pairs(*move)) for move in moves]]
    ppermute x8 -> x11, starting transfers between devices: 10.9 us -> 18.7 us  [the longest x10 15.4 us: shards(): received = [lax.ppermute(mine, AXES, flip_pairs(*move)) for move in moves]]
  transfers between devices with their start and end apart: 9 -> 12, of which waited for: 9 -> 10; matrix products, arithmetic and copies ran while one was open for 0% -> 0% of each run, Pallas kernels for 0% -> 0%
where the time goes in v7:
time: 46.5 us; the launch traced here: 46.3 us
  starting transfers between devices  19.2 us (41%)
  waiting for transfers between devices  17.7 us (38%)
  Pallas kernels  8.85 us (19%)
  between operations  0.66 us (1%)
    ppermute x10, waiting for transfers between devices, shards(): received = [lax.ppermute(mine, AXES, flip_pairs(*move)) for move in moves]  15.9 us
    ppermute x10, starting transfers between devices, shards(): received = [lax.ppermute(mine, AXES, flip_pairs(*move)) for move in moves]  15.4 us
    pallas_call x1, Pallas kernels, shards(): pl.pallas_call(functools.partial(local_kernel, nf=nf, nb=nb, nt=nt, nm=nm...  7.03 us
    ppermute x1, starting transfers between devices, shards(): received = [lax.ppermute(other, CORE, swap)]  3.33 us
    pallas_call x1, Pallas kernels, shards(): pl.pallas_call(functools.partial(modes_kernel, nf=nf, nb=nb, nm=nm, nv=nv...  1.48 us
  transfers between devices with their start and end apart: 12, of which 10 were waited for; matrix products, arithmetic and copies ran while one was open for 0% of the time, Pallas kernels for 0%

profile of v7, /device:TPU:1, one launch (start us, length us, event | category | flops | bytes accessed | tf_op | source)
XLA Modules:
  0.0 46.3 jit_solution(7019587095577272482)
XLA Ops:
  0.6 7.0 %local_part.1 = (bf16[2048,768]{1,0:T(8,128)(2,1)S(1)}, bf16[208,128]{1,0:T(8,128)(2,1)S(1)}, bf16[208,128]{1,0:T(8,128)(2,1)S(1)}) custom-call(s32[64]{0:T(128)} %starts_hbm.1, s32[16]{0:T(128)} %bins_hbm.1, bf16[6144,128]{1,0:T(8,128)(2,1)} %bitcast.4, f32[3,2,128]{2,1,0:T(2,128)} %w_hbm.1, f32[16,2,8,64]{3,2,1,0:T(8,128)} %bitcast.5), custom_call_target="tpu_custom_call" | custom-call | tf_op jit(solution)/shard_map/local_part/pallas_call | solution.py:277
  7.7 3.3 %collective-permute-start = (bf16[208,128]{1,0:T(8,128)(2,1)S(1)}, bf16[208,128]{1,0:T(8,128)(2,1)S(1)}, u32[]{:S(2)}, u32[]{:S(2)}) collective-permute-start(bf16[208,128]{1,0:T(8,128)(2,1)S(1)} %get-tuple-element.10), channel_id=1, source_target_pairs={{0,1},{1,0},{2,3},{3,2},{4,5},{5,4},{6,7},{7,6},{8,9},{9,8},{10,11... | collective-permute-start | bytes 159752 | tf_op jit(solution)/shard_map/ppermute | solution.py:305
  11.0 0.9 %collective-permute-done.refs_1_ = bf16[208,128]{1,0:T(8,128)(2,1)S(1)} collective-permute-done((bf16[208,128]{1,0:T(8,128)(2,1)S(1)}, bf16[208,128]{1,0:T(8,128)(2,1)S(1)}, u32[]{:S(2)}, u32[]{:S(2)}) %collective-permute-start) | collective-permute-done | bytes 53280 | tf_op jit(solution)/shard_map/ppermute | solution.py:305
  11.9 2.7 %collective-permute-start.3 = (bf16[208,128]{1,0:T(8,128)(2,1)S(1)}, bf16[208,128]{1,0:T(8,128)(2,1)S(1)}, u32[]{:S(2)}, u32[]{:S(2)}) collective-permute-start(bf16[208,128]{1,0:T(8,128)(2,1)S(1)} %add_partials.4.refs_0_), channel_id=1, source_target_pairs={{0,130},{1,131},{2,128},{3,129},{4,134},{5,135},{6,132},{7,133},{8... | collective-permute-start | bytes 159752 | tf_op jit(solution)/shard_map/ppermute | solution.py:314
  14.6 0.0 collective-permute-start.2
  14.6 1.2 %collective-permute-start.1 = (bf16[208,128]{1,0:T(8,128)(2,1)S(1)}, bf16[208,128]{1,0:T(8,128)(2,1)S(1)}, u32[]{:S(2)}, u32[]{:S(2)}) collective-permute-start(bf16[208,128]{1,0:T(8,128)(2,1)S(1)} %add_partials.4.refs_0_), channel_id=1, source_target_pairs={{0,129},{1,128},{2,131},{3,130},{4,133},{5,132},{6,135},{7,134},{8... | collective-permute-start | bytes 159752 | tf_op jit(solution)/shard_map/ppermute | solution.py:314
  15.8 1.0 %collective-permute-done.3.refs_3_ = bf16[208,128]{1,0:T(8,128)(2,1)S(1)} collective-permute-done((bf16[208,128]{1,0:T(8,128)(2,1)S(1)}, bf16[208,128]{1,0:T(8,128)(2,1)S(1)}, u32[]{:S(2)}, u32[]{:S(2)}) %collective-permute-start.3) | collective-permute-done | bytes 53280 | tf_op jit(solution)/shard_map/ppermute | solution.py:314
  16.8 3.4 %collective-permute-done.2.refs_2_ = bf16[208,128]{1,0:T(8,128)(2,1)S(1)} collective-permute-done((bf16[208,128]{1,0:T(8,128)(2,1)S(1)}, bf16[208,128]{1,0:T(8,128)(2,1)S(1)}, u32[]{:S(2)}, u32[]{:S(2)}) %collective-permute-start.2) | collective-permute-done | bytes 53280 | tf_op jit(solution)/shard_map/ppermute | solution.py:314
  20.2 0.2 collective-permute-done.1.refs_1_
  20.4 2.5 %collective-permute-start.6 = (bf16[208,128]{1,0:T(8,128)(2,1)S(1)}, bf16[208,128]{1,0:T(8,128)(2,1)S(1)}, u32[]{:S(2)}, u32[]{:S(2)}) collective-permute-start(bf16[208,128]{1,0:T(8,128)(2,1)S(1)} %add_partials.5.refs_0_), channel_id=1, source_target_pairs={{0,64},{1,65},{2,66},{3,67},{4,68},{5,69},{6,70},{7,71},{8,72},{9,... | collective-permute-start | bytes 159752 | tf_op jit(solution)/shard_map/ppermute | solution.py:314
  22.9 1.4 %collective-permute-start.5 = (bf16[208,128]{1,0:T(8,128)(2,1)S(1)}, bf16[208,128]{1,0:T(8,128)(2,1)S(1)}, u32[]{:S(2)}, u32[]{:S(2)}) collective-permute-start(bf16[208,128]{1,0:T(8,128)(2,1)S(1)} %add_partials.5.refs_0_), channel_id=1, source_target_pairs={{0,97},{1,96},{2,99},{3,98},{4,101},{5,100},{6,103},{7,102},{8,105... | collective-permute-start | bytes 159752 | tf_op jit(solution)/shard_map/ppermute | solution.py:314
  24.4 0.0 collective-permute-start.4
  24.4 0.6 %collective-permute-done.6.refs_3_ = bf16[208,128]{1,0:T(8,128)(2,1)S(1)} collective-permute-done((bf16[208,128]{1,0:T(8,128)(2,1)S(1)}, bf16[208,128]{1,0:T(8,128)(2,1)S(1)}, u32[]{:S(2)}, u32[]{:S(2)}) %collective-permute-start.6) | collective-permute-done | bytes 53280 | tf_op jit(solution)/shard_map/ppermute | solution.py:314
  25.0 3.5 %collective-permute-done.5.refs_2_ = bf16[208,128]{1,0:T(8,128)(2,1)S(1)} collective-permute-done((bf16[208,128]{1,0:T(8,128)(2,1)S(1)}, bf16[208,128]{1,0:T(8,128)(2,1)S(1)}, u32[]{:S(2)}, u32[]{:S(2)}) %collective-permute-start.5) | collective-permute-done | bytes 53280 | tf_op jit(solution)/shard_map/ppermute | solution.py:314
  28.5 0.0 collective-permute-done.4.refs_1_
  28.6 3.0 %collective-permute-start.9 = (bf16[208,128]{1,0:T(8,128)(2,1)S(1)}, bf16[208,128]{1,0:T(8,128)(2,1)S(1)}, u32[]{:S(2)}, u32[]{:S(2)}) collective-permute-start(bf16[208,128]{1,0:T(8,128)(2,1)S(1)} %add_partials.6.refs_0_), channel_id=1, source_target_pairs={{0,16},{1,17},{2,18},{3,19},{4,20},{5,21},{6,22},{7,23},{8,24},{9,... | collective-permute-start | bytes 159752 | tf_op jit(solution)/shard_map/ppermute | solution.py:314
  31.6 1.3 %collective-permute-start.8 = (bf16[208,128]{1,0:T(8,128)(2,1)S(1)}, bf16[208,128]{1,0:T(8,128)(2,1)S(1)}, u32[]{:S(2)}, u32[]{:S(2)}) collective-permute-start(bf16[208,128]{1,0:T(8,128)(2,1)S(1)} %add_partials.6.refs_0_), channel_id=1, source_target_pairs={{0,25},{1,24},{2,27},{3,26},{4,29},{5,28},{6,31},{7,30},{8,17},{9,... | collective-permute-start | bytes 159752 | tf_op jit(solution)/shard_map/ppermute | solution.py:314
  32.9 0.0 collective-permute-start.7
  32.9 0.2 collective-permute-done.9.refs_3_
  33.2 4.0 %collective-permute-done.8.refs_2_ = bf16[208,128]{1,0:T(8,128)(2,1)S(1)} collective-permute-done((bf16[208,128]{1,0:T(8,128)(2,1)S(1)}, bf16[208,128]{1,0:T(8,128)(2,1)S(1)}, u32[]{:S(2)}, u32[]{:S(2)}) %collective-permute-start.8) | collective-permute-done | bytes 53280 | tf_op jit(solution)/shard_map/ppermute | solution.py:314
  37.2 0.0 collective-permute-done.7.refs_1_
  37.2 3.2 %collective-permute-start.10 = (bf16[208,128]{1,0:T(8,128)(2,1)S(1)}, bf16[208,128]{1,0:T(8,128)(2,1)S(1)}, u32[]{:S(2)}, u32[]{:S(2)}) collective-permute-start(bf16[208,128]{1,0:T(8,128)(2,1)S(1)} %add_partials.7.a_ref), channel_id=1, source_target_pairs={{0,7},{1,6},{2,5},{3,4},{4,3},{5,2},{6,1},{7,0},{8,15},{9,14},{10,... | collective-permute-start | bytes 159752 | tf_op jit(solution)/shard_map/ppermute | solution.py:314
  40.4 2.9 %collective-permute-done.10.b_ref = bf16[208,128]{1,0:T(8,128)(2,1)S(1)} collective-permute-done((bf16[208,128]{1,0:T(8,128)(2,1)S(1)}, bf16[208,128]{1,0:T(8,128)(2,1)S(1)}, u32[]{:S(2)}, u32[]{:S(2)}) %collective-permute-start.10) | collective-permute-done | bytes 53280 | tf_op jit(solution)/shard_map/ppermute | solution.py:314
  43.4 0.2 owner_part.1
  43.5 0.5 collective-permute-start.11
  44.0 0.9 %collective-permute-done.11.other_ref = bf16[128,128]{1,0:T(8,128)(2,1)S(1)} collective-permute-done((bf16[128,128]{1,0:T(8,128)(2,1)S(1)}, bf16[128,128]{1,0:T(8,128)(2,1)S(1)}, u32[]{:S(2)}, u32[]{:S(2)}) %collective-permute-start.11) | collective-permute-done | bytes 32800 | tf_op jit(solution)/shard_map/ppermute | solution.py:322
  44.9 1.5 %modes_part.1 = (f32[1536,128]{1,0:T(8,128)}, f32[8,16]{1,0:T(8,128)}) custom-call(bf16[128,128]{1,0:T(8,128)(2,1)S(1)} %get-tuple-element.11.mine_ref, bf16[128,128]{1,0:T(8,128)(2,1)S(1)} %collective-permute-done.11.other_ref, f32[8,128]{1,0:T(8,128)S(1)} %get-tuple-element.12.s_ref, bf16[2048,768]{1,0:T(8,128)(2,1)S(1)} %get-tuple-element.13.y_ref), custom_call_target="tpu_custom_call" | custom-call | tf_op jit(solution)/shard_map/modes_part/pallas_call | solution.py:323
  (4 shorter events, 0.2 us)
Async XLA Ops:
  7.7 4.2 %collective-permute-start = (bf16[208,128]{1,0:T(8,128)(2,1)S(1)}, bf16[208,128]{1,0:T(8,128)(2,1)S(1)}, u32[]{:S(2)}, u32[]{:S(2)}) collective-permute-start(bf16[208,128]{1,0:T(8,128)(2,1)S(1)} %get-tuple-element.10), channel_id=1, source_target_pairs={{0,1},{1,0},{2,3},{3,2},{4,5},{5,4},{6,7},{7,6},{8,9},{9,8},{10,11... | collective-permute-start | bytes 159752 | tf_op jit(solution)/shard_map/ppermute | solution.py:305
  11.9 4.9 %collective-permute-start.3 = (bf16[208,128]{1,0:T(8,128)(2,1)S(1)}, bf16[208,128]{1,0:T(8,128)(2,1)S(1)}, u32[]{:S(2)}, u32[]{:S(2)}) collective-permute-start(bf16[208,128]{1,0:T(8,128)(2,1)S(1)} %add_partials.4.refs_0_), channel_id=1, source_target_pairs={{0,130},{1,131},{2,128},{3,129},{4,134},{5,135},{6,132},{7,133},{8... | collective-permute-start | bytes 159752 | tf_op jit(solution)/shard_map/ppermute | solution.py:314
  14.6 5.6 %collective-permute-start.2 = (bf16[208,128]{1,0:T(8,128)(2,1)S(1)}, bf16[208,128]{1,0:T(8,128)(2,1)S(1)}, u32[]{:S(2)}, u32[]{:S(2)}) collective-permute-start(bf16[208,128]{1,0:T(8,128)(2,1)S(1)} %add_partials.4.refs_0_), channel_id=1, source_target_pairs={{0,3},{1,2},{2,1},{3,0},{4,7},{5,6},{6,5},{7,4},{8,11},{9,10},{10,... | collective-permute-start | bytes 159752 | tf_op jit(solution)/shard_map/ppermute | solution.py:314
  14.6 5.8 %collective-permute-start.1 = (bf16[208,128]{1,0:T(8,128)(2,1)S(1)}, bf16[208,128]{1,0:T(8,128)(2,1)S(1)}, u32[]{:S(2)}, u32[]{:S(2)}) collective-permute-start(bf16[208,128]{1,0:T(8,128)(2,1)S(1)} %add_partials.4.refs_0_), channel_id=1, source_target_pairs={{0,129},{1,128},{2,131},{3,130},{4,133},{5,132},{6,135},{7,134},{8... | collective-permute-start | bytes 159752 | tf_op jit(solution)/shard_map/ppermute | solution.py:314
  20.4 4.6 %collective-permute-start.6 = (bf16[208,128]{1,0:T(8,128)(2,1)S(1)}, bf16[208,128]{1,0:T(8,128)(2,1)S(1)}, u32[]{:S(2)}, u32[]{:S(2)}) collective-permute-start(bf16[208,128]{1,0:T(8,128)(2,1)S(1)} %add_partials.5.refs_0_), channel_id=1, source_target_pairs={{0,64},{1,65},{2,66},{3,67},{4,68},{5,69},{6,70},{7,71},{8,72},{9,... | collective-permute-start | bytes 159752 | tf_op jit(solution)/shard_map/ppermute | solution.py:314
  22.9 5.6 %collective-permute-start.5 = (bf16[208,128]{1,0:T(8,128)(2,1)S(1)}, bf16[208,128]{1,0:T(8,128)(2,1)S(1)}, u32[]{:S(2)}, u32[]{:S(2)}) collective-permute-start(bf16[208,128]{1,0:T(8,128)(2,1)S(1)} %add_partials.5.refs_0_), channel_id=1, source_target_pairs={{0,97},{1,96},{2,99},{3,98},{4,101},{5,100},{6,103},{7,102},{8,105... | collective-permute-start | bytes 159752 | tf_op jit(solution)/shard_map/ppermute | solution.py:314
  24.4 4.2 %collective-permute-start.4 = (bf16[208,128]{1,0:T(8,128)(2,1)S(1)}, bf16[208,128]{1,0:T(8,128)(2,1)S(1)}, u32[]{:S(2)}, u32[]{:S(2)}) collective-permute-start(bf16[208,128]{1,0:T(8,128)(2,1)S(1)} %add_partials.5.refs_0_), channel_id=1, source_target_pairs={{0,33},{1,32},{2,35},{3,34},{4,37},{5,36},{6,39},{7,38},{8,41},{9,... | collective-permute-start | bytes 159752 | tf_op jit(solution)/shard_map/ppermute | solution.py:314
  28.6 4.6 %collective-permute-start.9 = (bf16[208,128]{1,0:T(8,128)(2,1)S(1)}, bf16[208,128]{1,0:T(8,128)(2,1)S(1)}, u32[]{:S(2)}, u32[]{:S(2)}) collective-permute-start(bf16[208,128]{1,0:T(8,128)(2,1)S(1)} %add_partials.6.refs_0_), channel_id=1, source_target_pairs={{0,16},{1,17},{2,18},{3,19},{4,20},{5,21},{6,22},{7,23},{8,24},{9,... | collective-permute-start | bytes 159752 | tf_op jit(solution)/shard_map/ppermute | solution.py:314
  31.6 5.6 %collective-permute-start.8 = (bf16[208,128]{1,0:T(8,128)(2,1)S(1)}, bf16[208,128]{1,0:T(8,128)(2,1)S(1)}, u32[]{:S(2)}, u32[]{:S(2)}) collective-permute-start(bf16[208,128]{1,0:T(8,128)(2,1)S(1)} %add_partials.6.refs_0_), channel_id=1, source_target_pairs={{0,25},{1,24},{2,27},{3,26},{4,29},{5,28},{6,31},{7,30},{8,17},{9,... | collective-permute-start | bytes 159752 | tf_op jit(solution)/shard_map/ppermute | solution.py:314
  32.9 4.3 %collective-permute-start.7 = (bf16[208,128]{1,0:T(8,128)(2,1)S(1)}, bf16[208,128]{1,0:T(8,128)(2,1)S(1)}, u32[]{:S(2)}, u32[]{:S(2)}) collective-permute-start(bf16[208,128]{1,0:T(8,128)(2,1)S(1)} %add_partials.6.refs_0_), channel_id=1, source_target_pairs={{0,9},{1,8},{2,11},{3,10},{4,13},{5,12},{6,15},{7,14},{8,1},{9,0},... | collective-permute-start | bytes 159752 | tf_op jit(solution)/shard_map/ppermute | solution.py:314
  37.2 6.1 %collective-permute-start.10 = (bf16[208,128]{1,0:T(8,128)(2,1)S(1)}, bf16[208,128]{1,0:T(8,128)(2,1)S(1)}, u32[]{:S(2)}, u32[]{:S(2)}) collective-permute-start(bf16[208,128]{1,0:T(8,128)(2,1)S(1)} %add_partials.7.a_ref), channel_id=1, source_target_pairs={{0,7},{1,6},{2,5},{3,4},{4,3},{5,2},{6,1},{7,0},{8,15},{9,14},{10,... | collective-permute-start | bytes 159752 | tf_op jit(solution)/shard_map/ppermute | solution.py:314
  43.5 1.3 %collective-permute-start.11 = (bf16[128,128]{1,0:T(8,128)(2,1)S(1)}, bf16[128,128]{1,0:T(8,128)(2,1)S(1)}, u32[]{:S(2)}, u32[]{:S(2)}) collective-permute-start(bf16[128,128]{1,0:T(8,128)(2,1)S(1)} %get-tuple-element.11.mine_ref), channel_id=1, source_target_pairs={{0,1},{1,0},{2,3},{3,2},{4,5},{5,4},{6,7},{7,6},{8,9},{9,8},{10,11... | collective-permute-start | bytes 98312 | tf_op jit(solution)/shard_map/ppermute | solution.py:322

commit v8 on v7

--- a/solution.py
+++ b/solution.py
@@ -16,7 +16,7 @@
 SX = AXES[:3]
 SY = AXES[3:]
 SIZES = (2, 4, 4, 4, 2)
-STEPS = (((0, 1), (3, 1)), ((1, 1), (1, 3)), ((2, 1), (2, 3)))
+STEPS = (((1, 1), (2, 1)), ((1, 3), (2, 3)), ((0, 1), (3, 1)))
 LAST = ((3, 3),)
 CORE = "sy_1"
 MIB = 1 << 20

time: 46.5 us -> 46.1 us (level)
  waiting for transfers between devices: 17.7 us -> 15.8 us
  starting transfers between devices: 19.2 us -> 20.6 us
    ppermute x10, waiting for transfers between devices: 15.9 us -> 14.1 us  [shards(): received = [lax.ppermute(mine, AXES, flip_pairs(*move)) for move in moves]]
    ppermute x10, starting transfers between devices: 15.4 us -> 16.9 us  [shards(): received = [lax.ppermute(mine, AXES, flip_pairs(*move)) for move in moves]]
where the time goes in v8:
time: 46.1 us; the launch traced here: 46 us
  starting transfers between devices  20.6 us (45%)
  waiting for transfers between devices  15.8 us (34%)
  Pallas kernels  8.85 us (19%)
  between operations  0.66 us (1%)
    ppermute x10, starting transfers between devices, shards(): received = [lax.ppermute(mine, AXES, flip_pairs(*move)) for move in moves]  16.9 us
    ppermute x10, waiting for transfers between devices, shards(): received = [lax.ppermute(mine, AXES, flip_pairs(*move)) for move in moves]  14.1 us
    pallas_call x1, Pallas kernels, shards(): pl.pallas_call(functools.partial(local_kernel, nf=nf, nb=nb, nt=nt, nm=nm...  7.03 us
    ppermute x1, starting transfers between devices, shards(): received = [lax.ppermute(other, CORE, swap)]  3.33 us
    pallas_call x1, Pallas kernels, shards(): pl.pallas_call(functools.partial(modes_kernel, nf=nf, nb=nb, nm=nm, nv=nv...  1.48 us
  transfers between devices with their start and end apart: 12, of which 10 were waited for; matrix products, arithmetic and copies ran while one was open for 0% of the time, Pallas kernels for 0%

profile of v8, /device:TPU:1, one launch (start us, length us, event | category | flops | bytes accessed | tf_op | source)
XLA Modules:
  0.0 46.0 jit_solution(12031096064351875032)
XLA Ops:
  0.6 7.0 %local_part.1 = (bf16[2048,768]{1,0:T(8,128)(2,1)S(1)}, bf16[208,128]{1,0:T(8,128)(2,1)S(1)}, bf16[208,128]{1,0:T(8,128)(2,1)S(1)}) custom-call(s32[64]{0:T(128)} %starts_hbm.1, s32[16]{0:T(128)} %bins_hbm.1, bf16[6144,128]{1,0:T(8,128)(2,1)} %bitcast.4, f32[3,2,128]{2,1,0:T(2,128)} %w_hbm.1, f32[16,2,8,64]{3,2,1,0:T(8,128)} %bitcast.5), custom_call_target="tpu_custom_call" | custom-call | tf_op jit(solution)/shard_map/local_part/pallas_call | solution.py:277
  7.7 3.3 %collective-permute-start = (bf16[208,128]{1,0:T(8,128)(2,1)S(1)}, bf16[208,128]{1,0:T(8,128)(2,1)S(1)}, u32[]{:S(2)}, u32[]{:S(2)}) collective-permute-start(bf16[208,128]{1,0:T(8,128)(2,1)S(1)} %get-tuple-element.10), channel_id=1, source_target_pairs={{0,1},{1,0},{2,3},{3,2},{4,5},{5,4},{6,7},{7,6},{8,9},{9,8},{10,11... | collective-permute-start | bytes 159752 | tf_op jit(solution)/shard_map/ppermute | solution.py:305
  11.0 0.9 %collective-permute-done.refs_1_ = bf16[208,128]{1,0:T(8,128)(2,1)S(1)} collective-permute-done((bf16[208,128]{1,0:T(8,128)(2,1)S(1)}, bf16[208,128]{1,0:T(8,128)(2,1)S(1)}, u32[]{:S(2)}, u32[]{:S(2)}) %collective-permute-start) | collective-permute-done | bytes 53280 | tf_op jit(solution)/shard_map/ppermute | solution.py:305
  11.9 0.6 %collective-permute-start.3 = (bf16[208,128]{1,0:T(8,128)(2,1)S(1)}, bf16[208,128]{1,0:T(8,128)(2,1)S(1)}, u32[]{:S(2)}, u32[]{:S(2)}) collective-permute-start(bf16[208,128]{1,0:T(8,128)(2,1)S(1)} %add_partials.4.refs_0_), channel_id=1, source_target_pairs={{0,40},{1,41},{2,42},{3,43},{4,44},{5,45},{6,46},{7,47},{8,32},{9,... | collective-permute-start | bytes 159752 | tf_op jit(solution)/shard_map/ppermute | solution.py:314
  12.5 0.7 %collective-permute-start.2 = (bf16[208,128]{1,0:T(8,128)(2,1)S(1)}, bf16[208,128]{1,0:T(8,128)(2,1)S(1)}, u32[]{:S(2)}, u32[]{:S(2)}) collective-permute-start(bf16[208,128]{1,0:T(8,128)(2,1)S(1)} %add_partials.4.refs_0_), channel_id=1, source_target_pairs={{0,9},{1,8},{2,11},{3,10},{4,13},{5,12},{6,15},{7,14},{8,1},{9,0},... | collective-permute-start | bytes 159752 | tf_op jit(solution)/shard_map/ppermute | solution.py:314
  13.2 1.8 %collective-permute-start.1 = (bf16[208,128]{1,0:T(8,128)(2,1)S(1)}, bf16[208,128]{1,0:T(8,128)(2,1)S(1)}, u32[]{:S(2)}, u32[]{:S(2)}) collective-permute-start(bf16[208,128]{1,0:T(8,128)(2,1)S(1)} %add_partials.4.refs_0_), channel_id=1, source_target_pairs={{0,33},{1,32},{2,35},{3,34},{4,37},{5,36},{6,39},{7,38},{8,41},{9,... | collective-permute-start | bytes 159752 | tf_op jit(solution)/shard_map/ppermute | solution.py:314
  14.9 1.0 %collective-permute-done.3.refs_3_ = bf16[208,128]{1,0:T(8,128)(2,1)S(1)} collective-permute-done((bf16[208,128]{1,0:T(8,128)(2,1)S(1)}, bf16[208,128]{1,0:T(8,128)(2,1)S(1)}, u32[]{:S(2)}, u32[]{:S(2)}) %collective-permute-start.3) | collective-permute-done | bytes 53280 | tf_op jit(solution)/shard_map/ppermute | solution.py:314
  15.9 2.0 %collective-permute-done.2.refs_2_ = bf16[208,128]{1,0:T(8,128)(2,1)S(1)} collective-permute-done((bf16[208,128]{1,0:T(8,128)(2,1)S(1)}, bf16[208,128]{1,0:T(8,128)(2,1)S(1)}, u32[]{:S(2)}, u32[]{:S(2)}) %collective-permute-start.2) | collective-permute-done | bytes 53280 | tf_op jit(solution)/shard_map/ppermute | solution.py:314
  17.9 0.0 collective-permute-done.1.refs_1_
  17.9 3.3 %collective-permute-start.6 = (bf16[208,128]{1,0:T(8,128)(2,1)S(1)}, bf16[208,128]{1,0:T(8,128)(2,1)S(1)}, u32[]{:S(2)}, u32[]{:S(2)}) collective-permute-start(bf16[208,128]{1,0:T(8,128)(2,1)S(1)} %add_partials.5.refs_0_), channel_id=1, source_target_pairs={{0,120},{1,121},{2,122},{3,123},{4,124},{5,125},{6,126},{7,127},{8... | collective-permute-start | bytes 159752 | tf_op jit(solution)/shard_map/ppermute | solution.py:314
  21.2 0.7 %collective-permute-start.5 = (bf16[208,128]{1,0:T(8,128)(2,1)S(1)}, bf16[208,128]{1,0:T(8,128)(2,1)S(1)}, u32[]{:S(2)}, u32[]{:S(2)}) collective-permute-start(bf16[208,128]{1,0:T(8,128)(2,1)S(1)} %add_partials.5.refs_0_), channel_id=1, source_target_pairs={{0,25},{1,24},{2,27},{3,26},{4,29},{5,28},{6,31},{7,30},{8,17},{9,... | collective-permute-start | bytes 159752 | tf_op jit(solution)/shard_map/ppermute | solution.py:314
  22.0 1.4 %collective-permute-start.4 = (bf16[208,128]{1,0:T(8,128)(2,1)S(1)}, bf16[208,128]{1,0:T(8,128)(2,1)S(1)}, u32[]{:S(2)}, u32[]{:S(2)}) collective-permute-start(bf16[208,128]{1,0:T(8,128)(2,1)S(1)} %add_partials.5.refs_0_), channel_id=1, source_target_pairs={{0,97},{1,96},{2,99},{3,98},{4,101},{5,100},{6,103},{7,102},{8,105... | collective-permute-start | bytes 159752 | tf_op jit(solution)/shard_map/ppermute | solution.py:314
  23.4 1.0 %collective-permute-done.6.refs_3_ = bf16[208,128]{1,0:T(8,128)(2,1)S(1)} collective-permute-done((bf16[208,128]{1,0:T(8,128)(2,1)S(1)}, bf16[208,128]{1,0:T(8,128)(2,1)S(1)}, u32[]{:S(2)}, u32[]{:S(2)}) %collective-permute-start.6) | collective-permute-done | bytes 53280 | tf_op jit(solution)/shard_map/ppermute | solution.py:314
  24.3 2.5 %collective-permute-done.5.refs_2_ = bf16[208,128]{1,0:T(8,128)(2,1)S(1)} collective-permute-done((bf16[208,128]{1,0:T(8,128)(2,1)S(1)}, bf16[208,128]{1,0:T(8,128)(2,1)S(1)}, u32[]{:S(2)}, u32[]{:S(2)}) %collective-permute-start.5) | collective-permute-done | bytes 53280 | tf_op jit(solution)/shard_map/ppermute | solution.py:314
  26.8 0.0 collective-permute-done.4.refs_1_
  26.9 4.4 %collective-permute-start.9 = (bf16[208,128]{1,0:T(8,128)(2,1)S(1)}, bf16[208,128]{1,0:T(8,128)(2,1)S(1)}, u32[]{:S(2)}, u32[]{:S(2)}) collective-permute-start(bf16[208,128]{1,0:T(8,128)(2,1)S(1)} %add_partials.6.refs_0_), channel_id=1, source_target_pairs={{0,130},{1,131},{2,128},{3,129},{4,134},{5,135},{6,132},{7,133},{8... | collective-permute-start | bytes 159752 | tf_op jit(solution)/shard_map/ppermute | solution.py:314
  31.3 0.0 collective-permute-start.8
  31.3 0.7 %collective-permute-start.7 = (bf16[208,128]{1,0:T(8,128)(2,1)S(1)}, bf16[208,128]{1,0:T(8,128)(2,1)S(1)}, u32[]{:S(2)}, u32[]{:S(2)}) collective-permute-start(bf16[208,128]{1,0:T(8,128)(2,1)S(1)} %add_partials.6.refs_0_), channel_id=1, source_target_pairs={{0,129},{1,128},{2,131},{3,130},{4,133},{5,132},{6,135},{7,134},{8... | collective-permute-start | bytes 159752 | tf_op jit(solution)/shard_map/ppermute | solution.py:314
  31.9 0.9 %collective-permute-done.9.refs_3_ = bf16[208,128]{1,0:T(8,128)(2,1)S(1)} collective-permute-done((bf16[208,128]{1,0:T(8,128)(2,1)S(1)}, bf16[208,128]{1,0:T(8,128)(2,1)S(1)}, u32[]{:S(2)}, u32[]{:S(2)}) %collective-permute-start.9) | collective-permute-done | bytes 53280 | tf_op jit(solution)/shard_map/ppermute | solution.py:314
  32.8 3.8 %collective-permute-done.8.refs_2_ = bf16[208,128]{1,0:T(8,128)(2,1)S(1)} collective-permute-done((bf16[208,128]{1,0:T(8,128)(2,1)S(1)}, bf16[208,128]{1,0:T(8,128)(2,1)S(1)}, u32[]{:S(2)}, u32[]{:S(2)}) %collective-permute-start.8) | collective-permute-done | bytes 53280 | tf_op jit(solution)/shard_map/ppermute | solution.py:314
  36.6 0.2 collective-permute-done.7.refs_1_
  36.9 3.3 %collective-permute-start.10 = (bf16[208,128]{1,0:T(8,128)(2,1)S(1)}, bf16[208,128]{1,0:T(8,128)(2,1)S(1)}, u32[]{:S(2)}, u32[]{:S(2)}) collective-permute-start(bf16[208,128]{1,0:T(8,128)(2,1)S(1)} %add_partials.7.a_ref), channel_id=1, source_target_pairs={{0,7},{1,6},{2,5},{3,4},{4,3},{5,2},{6,1},{7,0},{8,15},{9,14},{10,... | collective-permute-start | bytes 159752 | tf_op jit(solution)/shard_map/ppermute | solution.py:314
  40.2 2.8 %collective-permute-done.10.b_ref = bf16[208,128]{1,0:T(8,128)(2,1)S(1)} collective-permute-done((bf16[208,128]{1,0:T(8,128)(2,1)S(1)}, bf16[208,128]{1,0:T(8,128)(2,1)S(1)}, u32[]{:S(2)}, u32[]{:S(2)}) %collective-permute-start.10) | collective-permute-done | bytes 53280 | tf_op jit(solution)/shard_map/ppermute | solution.py:314
  43.0 0.2 owner_part.1
  43.2 0.5 %collective-permute-start.11 = (bf16[128,128]{1,0:T(8,128)(2,1)S(1)}, bf16[128,128]{1,0:T(8,128)(2,1)S(1)}, u32[]{:S(2)}, u32[]{:S(2)}) collective-permute-start(bf16[128,128]{1,0:T(8,128)(2,1)S(1)} %get-tuple-element.11.mine_ref), channel_id=1, source_target_pairs={{0,1},{1,0},{2,3},{3,2},{4,5},{5,4},{6,7},{7,6},{8,9},{9,8},{10,11... | collective-permute-start | bytes 98312 | tf_op jit(solution)/shard_map/ppermute | solution.py:322
  43.6 0.9 %collective-permute-done.11.other_ref = bf16[128,128]{1,0:T(8,128)(2,1)S(1)} collective-permute-done((bf16[128,128]{1,0:T(8,128)(2,1)S(1)}, bf16[128,128]{1,0:T(8,128)(2,1)S(1)}, u32[]{:S(2)}, u32[]{:S(2)}) %collective-permute-start.11) | collective-permute-done | bytes 32800 | tf_op jit(solution)/shard_map/ppermute | solution.py:322
  44.5 1.5 %modes_part.1 = (f32[1536,128]{1,0:T(8,128)}, f32[8,16]{1,0:T(8,128)}) custom-call(bf16[128,128]{1,0:T(8,128)(2,1)S(1)} %get-tuple-element.11.mine_ref, bf16[128,128]{1,0:T(8,128)(2,1)S(1)} %collective-permute-done.11.other_ref, f32[8,128]{1,0:T(8,128)S(1)} %get-tuple-element.12.s_ref, bf16[2048,768]{1,0:T(8,128)(2,1)S(1)} %get-tuple-element.13.y_ref), custom_call_target="tpu_custom_call" | custom-call | tf_op jit(solution)/shard_map/modes_part/pallas_call | solution.py:323
  (4 shorter events, 0.2 us)
Async XLA Ops:
  7.7 4.2 %collective-permute-start = (bf16[208,128]{1,0:T(8,128)(2,1)S(1)}, bf16[208,128]{1,0:T(8,128)(2,1)S(1)}, u32[]{:S(2)}, u32[]{:S(2)}) collective-permute-start(bf16[208,128]{1,0:T(8,128)(2,1)S(1)} %get-tuple-element.10), channel_id=1, source_target_pairs={{0,1},{1,0},{2,3},{3,2},{4,5},{5,4},{6,7},{7,6},{8,9},{9,8},{10,11... | collective-permute-start | bytes 159752 | tf_op jit(solution)/shard_map/ppermute | solution.py:305
  11.9 4.0 %collective-permute-start.3 = (bf16[208,128]{1,0:T(8,128)(2,1)S(1)}, bf16[208,128]{1,0:T(8,128)(2,1)S(1)}, u32[]{:S(2)}, u32[]{:S(2)}) collective-permute-start(bf16[208,128]{1,0:T(8,128)(2,1)S(1)} %add_partials.4.refs_0_), channel_id=1, source_target_pairs={{0,40},{1,41},{2,42},{3,43},{4,44},{5,45},{6,46},{7,47},{8,32},{9,... | collective-permute-start | bytes 159752 | tf_op jit(solution)/shard_map/ppermute | solution.py:314
  12.5 5.4 %collective-permute-start.2 = (bf16[208,128]{1,0:T(8,128)(2,1)S(1)}, bf16[208,128]{1,0:T(8,128)(2,1)S(1)}, u32[]{:S(2)}, u32[]{:S(2)}) collective-permute-start(bf16[208,128]{1,0:T(8,128)(2,1)S(1)} %add_partials.4.refs_0_), channel_id=1, source_target_pairs={{0,9},{1,8},{2,11},{3,10},{4,13},{5,12},{6,15},{7,14},{8,1},{9,0},... | collective-permute-start | bytes 159752 | tf_op jit(solution)/shard_map/ppermute | solution.py:314
  13.2 4.7 %collective-permute-start.1 = (bf16[208,128]{1,0:T(8,128)(2,1)S(1)}, bf16[208,128]{1,0:T(8,128)(2,1)S(1)}, u32[]{:S(2)}, u32[]{:S(2)}) collective-permute-start(bf16[208,128]{1,0:T(8,128)(2,1)S(1)} %add_partials.4.refs_0_), channel_id=1, source_target_pairs={{0,33},{1,32},{2,35},{3,34},{4,37},{5,36},{6,39},{7,38},{8,41},{9,... | collective-permute-start | bytes 159752 | tf_op jit(solution)/shard_map/ppermute | solution.py:314
  17.9 6.4 %collective-permute-start.6 = (bf16[208,128]{1,0:T(8,128)(2,1)S(1)}, bf16[208,128]{1,0:T(8,128)(2,1)S(1)}, u32[]{:S(2)}, u32[]{:S(2)}) collective-permute-start(bf16[208,128]{1,0:T(8,128)(2,1)S(1)} %add_partials.5.refs_0_), channel_id=1, source_target_pairs={{0,120},{1,121},{2,122},{3,123},{4,124},{5,125},{6,126},{7,127},{8... | collective-permute-start | bytes 159752 | tf_op jit(solution)/shard_map/ppermute | solution.py:314
  21.2 5.6 %collective-permute-start.5 = (bf16[208,128]{1,0:T(8,128)(2,1)S(1)}, bf16[208,128]{1,0:T(8,128)(2,1)S(1)}, u32[]{:S(2)}, u32[]{:S(2)}) collective-permute-start(bf16[208,128]{1,0:T(8,128)(2,1)S(1)} %add_partials.5.refs_0_), channel_id=1, source_target_pairs={{0,25},{1,24},{2,27},{3,26},{4,29},{5,28},{6,31},{7,30},{8,17},{9,... | collective-permute-start | bytes 159752 | tf_op jit(solution)/shard_map/ppermute | solution.py:314
  22.0 4.9 %collective-permute-start.4 = (bf16[208,128]{1,0:T(8,128)(2,1)S(1)}, bf16[208,128]{1,0:T(8,128)(2,1)S(1)}, u32[]{:S(2)}, u32[]{:S(2)}) collective-permute-start(bf16[208,128]{1,0:T(8,128)(2,1)S(1)} %add_partials.5.refs_0_), channel_id=1, source_target_pairs={{0,97},{1,96},{2,99},{3,98},{4,101},{5,100},{6,103},{7,102},{8,105... | collective-permute-start | bytes 159752 | tf_op jit(solution)/shard_map/ppermute | solution.py:314
  26.9 5.9 %collective-permute-start.9 = (bf16[208,128]{1,0:T(8,128)(2,1)S(1)}, bf16[208,128]{1,0:T(8,128)(2,1)S(1)}, u32[]{:S(2)}, u32[]{:S(2)}) collective-permute-start(bf16[208,128]{1,0:T(8,128)(2,1)S(1)} %add_partials.6.refs_0_), channel_id=1, source_target_pairs={{0,130},{1,131},{2,128},{3,129},{4,134},{5,135},{6,132},{7,133},{8... | collective-permute-start | bytes 159752 | tf_op jit(solution)/shard_map/ppermute | solution.py:314
  31.3 5.3 %collective-permute-start.8 = (bf16[208,128]{1,0:T(8,128)(2,1)S(1)}, bf16[208,128]{1,0:T(8,128)(2,1)S(1)}, u32[]{:S(2)}, u32[]{:S(2)}) collective-permute-start(bf16[208,128]{1,0:T(8,128)(2,1)S(1)} %add_partials.6.refs_0_), channel_id=1, source_target_pairs={{0,3},{1,2},{2,1},{3,0},{4,7},{5,6},{6,5},{7,4},{8,11},{9,10},{10,... | collective-permute-start | bytes 159752 | tf_op jit(solution)/shard_map/ppermute | solution.py:314
  31.3 5.5 %collective-permute-start.7 = (bf16[208,128]{1,0:T(8,128)(2,1)S(1)}, bf16[208,128]{1,0:T(8,128)(2,1)S(1)}, u32[]{:S(2)}, u32[]{:S(2)}) collective-permute-start(bf16[208,128]{1,0:T(8,128)(2,1)S(1)} %add_partials.6.refs_0_), channel_id=1, source_target_pairs={{0,129},{1,128},{2,131},{3,130},{4,133},{5,132},{6,135},{7,134},{8... | collective-permute-start | bytes 159752 | tf_op jit(solution)/shard_map/ppermute | solution.py:314
  36.9 6.1 %collective-permute-start.10 = (bf16[208,128]{1,0:T(8,128)(2,1)S(1)}, bf16[208,128]{1,0:T(8,128)(2,1)S(1)}, u32[]{:S(2)}, u32[]{:S(2)}) collective-permute-start(bf16[208,128]{1,0:T(8,128)(2,1)S(1)} %add_partials.7.a_ref), channel_id=1, source_target_pairs={{0,7},{1,6},{2,5},{3,4},{4,3},{5,2},{6,1},{7,0},{8,15},{9,14},{10,... | collective-permute-start | bytes 159752 | tf_op jit(solution)/shard_map/ppermute | solution.py:314
  43.2 1.3 %collective-permute-start.11 = (bf16[128,128]{1,0:T(8,128)(2,1)S(1)}, bf16[128,128]{1,0:T(8,128)(2,1)S(1)}, u32[]{:S(2)}, u32[]{:S(2)}) collective-permute-start(bf16[128,128]{1,0:T(8,128)(2,1)S(1)} %get-tuple-element.11.mine_ref), channel_id=1, source_target_pairs={{0,1},{1,0},{2,3},{3,2},{4,5},{5,4},{6,7},{7,6},{8,9},{9,8},{10,11... | collective-permute-start | bytes 98312 | tf_op jit(solution)/shard_map/ppermute | solution.py:322

commit v9 on v8

--- a/solution.py
+++ b/solution.py
@@ -16,7 +16,7 @@
 SX = AXES[:3]
 SY = AXES[3:]
 SIZES = (2, 4, 4, 4, 2)
-STEPS = (((1, 1), (2, 1)), ((1, 3), (2, 3)), ((0, 1), (3, 1)))
+STEPS = (((0, 1), (3, 1)), ((1, 1), (2, 1)), ((1, 3), (2, 3)))
 LAST = ((3, 3),)
 CORE = "sy_1"
 MIB = 1 << 20

time: 46.1 us -> 46 us (level)
  starting transfers between devices: 20.6 us -> 19.7 us
  waiting for transfers between devices: 15.8 us -> 16.7 us
    ppermute x10, starting transfers between devices: 16.9 us -> 15.9 us  [shards(): received = [lax.ppermute(mine, AXES, flip_pairs(*move)) for move in moves]]
    ppermute x10, waiting for transfers between devices: 14.1 us -> 15 us  [shards(): received = [lax.ppermute(mine, AXES, flip_pairs(*move)) for move in moves]]
where the time goes in v9:
time: 46 us; the launch traced here: 45.9 us
  starting transfers between devices  19.7 us (43%)
  waiting for transfers between devices  16.7 us (36%)
  Pallas kernels  8.85 us (19%)
  between operations  0.66 us (1%)
    ppermute x10, starting transfers between devices, shards(): received = [lax.ppermute(mine, AXES, flip_pairs(*move)) for move in moves]  15.9 us
    ppermute x10, waiting for transfers between devices, shards(): received = [lax.ppermute(mine, AXES, flip_pairs(*move)) for move in moves]  15 us
    pallas_call x1, Pallas kernels, shards(): pl.pallas_call(functools.partial(local_kernel, nf=nf, nb=nb, nt=nt, nm=nm...  7.03 us
    ppermute x1, starting transfers between devices, shards(): received = [lax.ppermute(other, CORE, swap)]  3.33 us
    pallas_call x1, Pallas kernels, shards(): pl.pallas_call(functools.partial(modes_kernel, nf=nf, nb=nb, nm=nm, nv=nv...  1.48 us
  transfers between devices with their start and end apart: 12, of which 10 were waited for; matrix products, arithmetic and copies ran while one was open for 0% of the time, Pallas kernels for 0%

profile of v9, /device:TPU:1, one launch (start us, length us, event | category | flops | bytes accessed | tf_op | source)
XLA Modules:
  0.0 45.9 jit_solution(9303773303593551969)
XLA Ops:
  0.6 7.0 %local_part.1 = (bf16[2048,768]{1,0:T(8,128)(2,1)S(1)}, bf16[208,128]{1,0:T(8,128)(2,1)S(1)}, bf16[208,128]{1,0:T(8,128)(2,1)S(1)}) custom-call(s32[64]{0:T(128)} %starts_hbm.1, s32[16]{0:T(128)} %bins_hbm.1, bf16[6144,128]{1,0:T(8,128)(2,1)} %bitcast.4, f32[3,2,128]{2,1,0:T(2,128)} %w_hbm.1, f32[16,2,8,64]{3,2,1,0:T(8,128)} %bitcast.5), custom_call_target="tpu_custom_call" | custom-call | tf_op jit(solution)/shard_map/local_part/pallas_call | solution.py:277
  7.7 3.3 %collective-permute-start = (bf16[208,128]{1,0:T(8,128)(2,1)S(1)}, bf16[208,128]{1,0:T(8,128)(2,1)S(1)}, u32[]{:S(2)}, u32[]{:S(2)}) collective-permute-start(bf16[208,128]{1,0:T(8,128)(2,1)S(1)} %get-tuple-element.10), channel_id=1, source_target_pairs={{0,1},{1,0},{2,3},{3,2},{4,5},{5,4},{6,7},{7,6},{8,9},{9,8},{10,11... | collective-permute-start | bytes 159752 | tf_op jit(solution)/shard_map/ppermute | solution.py:305
  11.0 0.9 %collective-permute-done.refs_1_ = bf16[208,128]{1,0:T(8,128)(2,1)S(1)} collective-permute-done((bf16[208,128]{1,0:T(8,128)(2,1)S(1)}, bf16[208,128]{1,0:T(8,128)(2,1)S(1)}, u32[]{:S(2)}, u32[]{:S(2)}) %collective-permute-start) | collective-permute-done | bytes 53280 | tf_op jit(solution)/shard_map/ppermute | solution.py:305
  11.9 2.7 %collective-permute-start.3 = (bf16[208,128]{1,0:T(8,128)(2,1)S(1)}, bf16[208,128]{1,0:T(8,128)(2,1)S(1)}, u32[]{:S(2)}, u32[]{:S(2)}) collective-permute-start(bf16[208,128]{1,0:T(8,128)(2,1)S(1)} %add_partials.4.refs_0_), channel_id=1, source_target_pairs={{0,130},{1,131},{2,128},{3,129},{4,134},{5,135},{6,132},{7,133},{8... | collective-permute-start | bytes 159752 | tf_op jit(solution)/shard_map/ppermute | solution.py:314
  14.6 0.0 collective-permute-start.2
  14.6 1.2 %collective-permute-start.1 = (bf16[208,128]{1,0:T(8,128)(2,1)S(1)}, bf16[208,128]{1,0:T(8,128)(2,1)S(1)}, u32[]{:S(2)}, u32[]{:S(2)}) collective-permute-start(bf16[208,128]{1,0:T(8,128)(2,1)S(1)} %add_partials.4.refs_0_), channel_id=1, source_target_pairs={{0,129},{1,128},{2,131},{3,130},{4,133},{5,132},{6,135},{7,134},{8... | collective-permute-start | bytes 159752 | tf_op jit(solution)/shard_map/ppermute | solution.py:314
  15.8 1.0 %collective-permute-done.3.refs_3_ = bf16[208,128]{1,0:T(8,128)(2,1)S(1)} collective-permute-done((bf16[208,128]{1,0:T(8,128)(2,1)S(1)}, bf16[208,128]{1,0:T(8,128)(2,1)S(1)}, u32[]{:S(2)}, u32[]{:S(2)}) %collective-permute-start.3) | collective-permute-done | bytes 53280 | tf_op jit(solution)/shard_map/ppermute | solution.py:314
  16.8 3.4 %collective-permute-done.2.refs_2_ = bf16[208,128]{1,0:T(8,128)(2,1)S(1)} collective-permute-done((bf16[208,128]{1,0:T(8,128)(2,1)S(1)}, bf16[208,128]{1,0:T(8,128)(2,1)S(1)}, u32[]{:S(2)}, u32[]{:S(2)}) %collective-permute-start.2) | collective-permute-done | bytes 53280 | tf_op jit(solution)/shard_map/ppermute | solution.py:314
  20.2 0.2 collective-permute-done.1.refs_1_
  20.4 2.0 %collective-permute-start.6 = (bf16[208,128]{1,0:T(8,128)(2,1)S(1)}, bf16[208,128]{1,0:T(8,128)(2,1)S(1)}, u32[]{:S(2)}, u32[]{:S(2)}) collective-permute-start(bf16[208,128]{1,0:T(8,128)(2,1)S(1)} %add_partials.5.refs_0_), channel_id=1, source_target_pairs={{0,40},{1,41},{2,42},{3,43},{4,44},{5,45},{6,46},{7,47},{8,32},{9,... | collective-permute-start | bytes 159752 | tf_op jit(solution)/shard_map/ppermute | solution.py:314
  22.4 0.7 %collective-permute-start.5 = (bf16[208,128]{1,0:T(8,128)(2,1)S(1)}, bf16[208,128]{1,0:T(8,128)(2,1)S(1)}, u32[]{:S(2)}, u32[]{:S(2)}) collective-permute-start(bf16[208,128]{1,0:T(8,128)(2,1)S(1)} %add_partials.5.refs_0_), channel_id=1, source_target_pairs={{0,9},{1,8},{2,11},{3,10},{4,13},{5,12},{6,15},{7,14},{8,1},{9,0},... | collective-permute-start | bytes 159752 | tf_op jit(solution)/shard_map/ppermute | solution.py:314
  23.1 0.3 collective-permute-start.4
  23.4 1.0 %collective-permute-done.6.refs_3_ = bf16[208,128]{1,0:T(8,128)(2,1)S(1)} collective-permute-done((bf16[208,128]{1,0:T(8,128)(2,1)S(1)}, bf16[208,128]{1,0:T(8,128)(2,1)S(1)}, u32[]{:S(2)}, u32[]{:S(2)}) %collective-permute-start.6) | collective-permute-done | bytes 53280 | tf_op jit(solution)/shard_map/ppermute | solution.py:314
  24.4 2.4 %collective-permute-done.5.refs_2_ = bf16[208,128]{1,0:T(8,128)(2,1)S(1)} collective-permute-done((bf16[208,128]{1,0:T(8,128)(2,1)S(1)}, bf16[208,128]{1,0:T(8,128)(2,1)S(1)}, u32[]{:S(2)}, u32[]{:S(2)}) %collective-permute-start.5) | collective-permute-done | bytes 53280 | tf_op jit(solution)/shard_map/ppermute | solution.py:314
  26.8 0.0 collective-permute-done.4.refs_1_
  26.8 4.3 %collective-permute-start.9 = (bf16[208,128]{1,0:T(8,128)(2,1)S(1)}, bf16[208,128]{1,0:T(8,128)(2,1)S(1)}, u32[]{:S(2)}, u32[]{:S(2)}) collective-permute-start(bf16[208,128]{1,0:T(8,128)(2,1)S(1)} %add_partials.6.refs_0_), channel_id=1, source_target_pairs={{0,120},{1,121},{2,122},{3,123},{4,124},{5,125},{6,126},{7,127},{8... | collective-permute-start | bytes 159752 | tf_op jit(solution)/shard_map/ppermute | solution.py:314
  31.1 0.8 %collective-permute-start.8 = (bf16[208,128]{1,0:T(8,128)(2,1)S(1)}, bf16[208,128]{1,0:T(8,128)(2,1)S(1)}, u32[]{:S(2)}, u32[]{:S(2)}) collective-permute-start(bf16[208,128]{1,0:T(8,128)(2,1)S(1)} %add_partials.6.refs_0_), channel_id=1, source_target_pairs={{0,25},{1,24},{2,27},{3,26},{4,29},{5,28},{6,31},{7,30},{8,17},{9,... | collective-permute-start | bytes 159752 | tf_op jit(solution)/shard_map/ppermute | solution.py:314
  31.9 0.4 collective-permute-start.7
  32.3 1.0 %collective-permute-done.9.refs_3_ = bf16[208,128]{1,0:T(8,128)(2,1)S(1)} collective-permute-done((bf16[208,128]{1,0:T(8,128)(2,1)S(1)}, bf16[208,128]{1,0:T(8,128)(2,1)S(1)}, u32[]{:S(2)}, u32[]{:S(2)}) %collective-permute-start.9) | collective-permute-done | bytes 53280 | tf_op jit(solution)/shard_map/ppermute | solution.py:314
  33.2 3.5 %collective-permute-done.8.refs_2_ = bf16[208,128]{1,0:T(8,128)(2,1)S(1)} collective-permute-done((bf16[208,128]{1,0:T(8,128)(2,1)S(1)}, bf16[208,128]{1,0:T(8,128)(2,1)S(1)}, u32[]{:S(2)}, u32[]{:S(2)}) %collective-permute-start.8) | collective-permute-done | bytes 53280 | tf_op jit(solution)/shard_map/ppermute | solution.py:314
  36.7 0.0 collective-permute-done.7.refs_1_
  36.8 3.5 %collective-permute-start.10 = (bf16[208,128]{1,0:T(8,128)(2,1)S(1)}, bf16[208,128]{1,0:T(8,128)(2,1)S(1)}, u32[]{:S(2)}, u32[]{:S(2)}) collective-permute-start(bf16[208,128]{1,0:T(8,128)(2,1)S(1)} %add_partials.7.a_ref), channel_id=1, source_target_pairs={{0,7},{1,6},{2,5},{3,4},{4,3},{5,2},{6,1},{7,0},{8,15},{9,14},{10,... | collective-permute-start | bytes 159752 | tf_op jit(solution)/shard_map/ppermute | solution.py:314
  40.3 2.6 %collective-permute-done.10.b_ref = bf16[208,128]{1,0:T(8,128)(2,1)S(1)} collective-permute-done((bf16[208,128]{1,0:T(8,128)(2,1)S(1)}, bf16[208,128]{1,0:T(8,128)(2,1)S(1)}, u32[]{:S(2)}, u32[]{:S(2)}) %collective-permute-start.10) | collective-permute-done | bytes 53280 | tf_op jit(solution)/shard_map/ppermute | solution.py:314
  42.9 0.2 owner_part.1
  43.1 0.5 %collective-permute-start.11 = (bf16[128,128]{1,0:T(8,128)(2,1)S(1)}, bf16[128,128]{1,0:T(8,128)(2,1)S(1)}, u32[]{:S(2)}, u32[]{:S(2)}) collective-permute-start(bf16[128,128]{1,0:T(8,128)(2,1)S(1)} %get-tuple-element.11.mine_ref), channel_id=1, source_target_pairs={{0,1},{1,0},{2,3},{3,2},{4,5},{5,4},{6,7},{7,6},{8,9},{9,8},{10,11... | collective-permute-start | bytes 98312 | tf_op jit(solution)/shard_map/ppermute | solution.py:322
  43.6 0.9 %collective-permute-done.11.other_ref = bf16[128,128]{1,0:T(8,128)(2,1)S(1)} collective-permute-done((bf16[128,128]{1,0:T(8,128)(2,1)S(1)}, bf16[128,128]{1,0:T(8,128)(2,1)S(1)}, u32[]{:S(2)}, u32[]{:S(2)}) %collective-permute-start.11) | collective-permute-done | bytes 32800 | tf_op jit(solution)/shard_map/ppermute | solution.py:322
  44.4 1.5 %modes_part.1 = (f32[1536,128]{1,0:T(8,128)}, f32[8,16]{1,0:T(8,128)}) custom-call(bf16[128,128]{1,0:T(8,128)(2,1)S(1)} %get-tuple-element.11.mine_ref, bf16[128,128]{1,0:T(8,128)(2,1)S(1)} %collective-permute-done.11.other_ref, f32[8,128]{1,0:T(8,128)S(1)} %get-tuple-element.12.s_ref, bf16[2048,768]{1,0:T(8,128)(2,1)S(1)} %get-tuple-element.13.y_ref), custom_call_target="tpu_custom_call" | custom-call | tf_op jit(solution)/shard_map/modes_part/pallas_call | solution.py:323
  (4 shorter events, 0.2 us)
Async XLA Ops:
  7.7 4.2 %collective-permute-start = (bf16[208,128]{1,0:T(8,128)(2,1)S(1)}, bf16[208,128]{1,0:T(8,128)(2,1)S(1)}, u32[]{:S(2)}, u32[]{:S(2)}) collective-permute-start(bf16[208,128]{1,0:T(8,128)(2,1)S(1)} %get-tuple-element.10), channel_id=1, source_target_pairs={{0,1},{1,0},{2,3},{3,2},{4,5},{5,4},{6,7},{7,6},{8,9},{9,8},{10,11... | collective-permute-start | bytes 159752 | tf_op jit(solution)/shard_map/ppermute | solution.py:305
  11.9 4.9 %collective-permute-start.3 = (bf16[208,128]{1,0:T(8,128)(2,1)S(1)}, bf16[208,128]{1,0:T(8,128)(2,1)S(1)}, u32[]{:S(2)}, u32[]{:S(2)}) collective-permute-start(bf16[208,128]{1,0:T(8,128)(2,1)S(1)} %add_partials.4.refs_0_), channel_id=1, source_target_pairs={{0,130},{1,131},{2,128},{3,129},{4,134},{5,135},{6,132},{7,133},{8... | collective-permute-start | bytes 159752 | tf_op jit(solution)/shard_map/ppermute | solution.py:314
  14.6 5.6 %collective-permute-start.2 = (bf16[208,128]{1,0:T(8,128)(2,1)S(1)}, bf16[208,128]{1,0:T(8,128)(2,1)S(1)}, u32[]{:S(2)}, u32[]{:S(2)}) collective-permute-start(bf16[208,128]{1,0:T(8,128)(2,1)S(1)} %add_partials.4.refs_0_), channel_id=1, source_target_pairs={{0,3},{1,2},{2,1},{3,0},{4,7},{5,6},{6,5},{7,4},{8,11},{9,10},{10,... | collective-permute-start | bytes 159752 | tf_op jit(solution)/shard_map/ppermute | solution.py:314
  14.6 5.8 %collective-permute-start.1 = (bf16[208,128]{1,0:T(8,128)(2,1)S(1)}, bf16[208,128]{1,0:T(8,128)(2,1)S(1)}, u32[]{:S(2)}, u32[]{:S(2)}) collective-permute-start(bf16[208,128]{1,0:T(8,128)(2,1)S(1)} %add_partials.4.refs_0_), channel_id=1, source_target_pairs={{0,129},{1,128},{2,131},{3,130},{4,133},{5,132},{6,135},{7,134},{8... | collective-permute-start | bytes 159752 | tf_op jit(solution)/shard_map/ppermute | solution.py:314
  20.4 4.0 %collective-permute-start.6 = (bf16[208,128]{1,0:T(8,128)(2,1)S(1)}, bf16[208,128]{1,0:T(8,128)(2,1)S(1)}, u32[]{:S(2)}, u32[]{:S(2)}) collective-permute-start(bf16[208,128]{1,0:T(8,128)(2,1)S(1)} %add_partials.5.refs_0_), channel_id=1, source_target_pairs={{0,40},{1,41},{2,42},{3,43},{4,44},{5,45},{6,46},{7,47},{8,32},{9,... | collective-permute-start | bytes 159752 | tf_op jit(solution)/shard_map/ppermute | solution.py:314
  22.4 4.4 %collective-permute-start.5 = (bf16[208,128]{1,0:T(8,128)(2,1)S(1)}, bf16[208,128]{1,0:T(8,128)(2,1)S(1)}, u32[]{:S(2)}, u32[]{:S(2)}) collective-permute-start(bf16[208,128]{1,0:T(8,128)(2,1)S(1)} %add_partials.5.refs_0_), channel_id=1, source_target_pairs={{0,9},{1,8},{2,11},{3,10},{4,13},{5,12},{6,15},{7,14},{8,1},{9,0},... | collective-permute-start | bytes 159752 | tf_op jit(solution)/shard_map/ppermute | solution.py:314
  23.1 3.7 %collective-permute-start.4 = (bf16[208,128]{1,0:T(8,128)(2,1)S(1)}, bf16[208,128]{1,0:T(8,128)(2,1)S(1)}, u32[]{:S(2)}, u32[]{:S(2)}) collective-permute-start(bf16[208,128]{1,0:T(8,128)(2,1)S(1)} %add_partials.5.refs_0_), channel_id=1, source_target_pairs={{0,33},{1,32},{2,35},{3,34},{4,37},{5,36},{6,39},{7,38},{8,41},{9,... | collective-permute-start | bytes 159752 | tf_op jit(solution)/shard_map/ppermute | solution.py:314
  26.8 6.4 %collective-permute-start.9 = (bf16[208,128]{1,0:T(8,128)(2,1)S(1)}, bf16[208,128]{1,0:T(8,128)(2,1)S(1)}, u32[]{:S(2)}, u32[]{:S(2)}) collective-permute-start(bf16[208,128]{1,0:T(8,128)(2,1)S(1)} %add_partials.6.refs_0_), channel_id=1, source_target_pairs={{0,120},{1,121},{2,122},{3,123},{4,124},{5,125},{6,126},{7,127},{8... | collective-permute-start | bytes 159752 | tf_op jit(solution)/shard_map/ppermute | solution.py:314
  31.1 5.6 %collective-permute-start.8 = (bf16[208,128]{1,0:T(8,128)(2,1)S(1)}, bf16[208,128]{1,0:T(8,128)(2,1)S(1)}, u32[]{:S(2)}, u32[]{:S(2)}) collective-permute-start(bf16[208,128]{1,0:T(8,128)(2,1)S(1)} %add_partials.6.refs_0_), channel_id=1, source_target_pairs={{0,25},{1,24},{2,27},{3,26},{4,29},{5,28},{6,31},{7,30},{8,17},{9,... | collective-permute-start | bytes 159752 | tf_op jit(solution)/shard_map/ppermute | solution.py:314
  31.9 4.8 %collective-permute-start.7 = (bf16[208,128]{1,0:T(8,128)(2,1)S(1)}, bf16[208,128]{1,0:T(8,128)(2,1)S(1)}, u32[]{:S(2)}, u32[]{:S(2)}) collective-permute-start(bf16[208,128]{1,0:T(8,128)(2,1)S(1)} %add_partials.6.refs_0_), channel_id=1, source_target_pairs={{0,97},{1,96},{2,99},{3,98},{4,101},{5,100},{6,103},{7,102},{8,105... | collective-permute-start | bytes 159752 | tf_op jit(solution)/shard_map/ppermute | solution.py:314
  36.8 6.1 %collective-permute-start.10 = (bf16[208,128]{1,0:T(8,128)(2,1)S(1)}, bf16[208,128]{1,0:T(8,128)(2,1)S(1)}, u32[]{:S(2)}, u32[]{:S(2)}) collective-permute-start(bf16[208,128]{1,0:T(8,128)(2,1)S(1)} %add_partials.7.a_ref), channel_id=1, source_target_pairs={{0,7},{1,6},{2,5},{3,4},{4,3},{5,2},{6,1},{7,0},{8,15},{9,14},{10,... | collective-permute-start | bytes 159752 | tf_op jit(solution)/shard_map/ppermute | solution.py:314
  43.1 1.3 %collective-permute-start.11 = (bf16[128,128]{1,0:T(8,128)(2,1)S(1)}, bf16[128,128]{1,0:T(8,128)(2,1)S(1)}, u32[]{:S(2)}, u32[]{:S(2)}) collective-permute-start(bf16[128,128]{1,0:T(8,128)(2,1)S(1)} %get-tuple-element.11.mine_ref), channel_id=1, source_target_pairs={{0,1},{1,0},{2,3},{3,2},{4,5},{5,4},{6,7},{7,6},{8,9},{9,8},{10,11... | collective-permute-start | bytes 98312 | tf_op jit(solution)/shard_map/ppermute | solution.py:322

commit v10 on v7

--- a/solution.py
+++ b/solution.py
@@ -148,13 +148,11 @@
         ghi, glo = split2(jnp.concatenate(both, axis=0))
         proj = jnp.dot(jnp.concatenate([ghi, glo], axis=0), yf, preferred_element_type=jnp.float32)
         proj = proj[:4 * nm] + proj[4 * nm:]
-        phi, plo = split2(proj)
-        pst = jnp.concatenate([phi, plo], axis=0)
+        pst = proj.astype(jnp.bfloat16)
         zs = [[], []]
         for v in range(nv):
             r = lax.dot_general(pst[:, v * span:(v + 1) * span], yf[:, v * span:(v + 1) * span],
                                 (((1,), (1,)), ((), ())), preferred_element_type=jnp.float32)
-            r = r[:4 * nm] + r[4 * nm:]
             for i in range(2):
                 part = r[i * 2 * nm:(i + 1) * 2 * nm, i * 2 * nb:(i + 1) * 2 * nb]
                 ru = part[:nm]

time: 46.5 us -> 46.4 us (level)
  no operation moved by 1% of the time
where the time goes in v10:
time: 46.4 us; the launch traced here: 46.2 us
  starting transfers between devices  19.2 us (41%)
  waiting for transfers between devices  17.7 us (38%)
  Pallas kernels  8.74 us (19%)
  between operations  0.66 us (1%)
    ppermute x10, waiting for transfers between devices, shards(): received = [lax.ppermute(mine, AXES, flip_pairs(*move)) for move in moves]  15.9 us
    ppermute x10, starting transfers between devices, shards(): received = [lax.ppermute(mine, AXES, flip_pairs(*move)) for move in moves]  15.4 us
    pallas_call x1, Pallas kernels, shards(): pl.pallas_call(functools.partial(local_kernel, nf=nf, nb=nb, nt=nt, nm=nm...  6.93 us
    ppermute x1, starting transfers between devices, shards(): received = [lax.ppermute(other, CORE, swap)]  3.33 us
    pallas_call x1, Pallas kernels, shards(): pl.pallas_call(functools.partial(modes_kernel, nf=nf, nb=nb, nm=nm, nv=nv...  1.48 us
  transfers between devices with their start and end apart: 12, of which 10 were waited for; matrix products, arithmetic and copies ran while one was open for 0% of the time, Pallas kernels for 0%

profile of v10, /device:TPU:1, one launch (start us, length us, event | category | flops | bytes accessed | tf_op | source)
XLA Modules:
  0.0 46.2 jit_solution(9830071972381803327)
XLA Ops:
  0.6 6.9 %local_part.1 = (bf16[2048,768]{1,0:T(8,128)(2,1)S(1)}, bf16[208,128]{1,0:T(8,128)(2,1)S(1)}, bf16[208,128]{1,0:T(8,128)(2,1)S(1)}) custom-call(s32[64]{0:T(128)} %starts_hbm.1, s32[16]{0:T(128)} %bins_hbm.1, bf16[6144,128]{1,0:T(8,128)(2,1)} %bitcast.4, f32[3,2,128]{2,1,0:T(2,128)} %w_hbm.1, f32[16,2,8,64]{3,2,1,0:T(8,128)} %bitcast.5), custom_call_target="tpu_custom_call" | custom-call | tf_op jit(solution)/shard_map/local_part/pallas_call | solution.py:275
  7.6 3.3 %collective-permute-start = (bf16[208,128]{1,0:T(8,128)(2,1)S(1)}, bf16[208,128]{1,0:T(8,128)(2,1)S(1)}, u32[]{:S(2)}, u32[]{:S(2)}) collective-permute-start(bf16[208,128]{1,0:T(8,128)(2,1)S(1)} %get-tuple-element.10), channel_id=1, source_target_pairs={{0,1},{1,0},{2,3},{3,2},{4,5},{5,4},{6,7},{7,6},{8,9},{9,8},{10,11... | collective-permute-start | bytes 159752 | tf_op jit(solution)/shard_map/ppermute | solution.py:303
  10.9 0.9 %collective-permute-done.refs_1_ = bf16[208,128]{1,0:T(8,128)(2,1)S(1)} collective-permute-done((bf16[208,128]{1,0:T(8,128)(2,1)S(1)}, bf16[208,128]{1,0:T(8,128)(2,1)S(1)}, u32[]{:S(2)}, u32[]{:S(2)}) %collective-permute-start) | collective-permute-done | bytes 53280 | tf_op jit(solution)/shard_map/ppermute | solution.py:303
  11.8 2.7 %collective-permute-start.3 = (bf16[208,128]{1,0:T(8,128)(2,1)S(1)}, bf16[208,128]{1,0:T(8,128)(2,1)S(1)}, u32[]{:S(2)}, u32[]{:S(2)}) collective-permute-start(bf16[208,128]{1,0:T(8,128)(2,1)S(1)} %add_partials.4.refs_0_), channel_id=1, source_target_pairs={{0,130},{1,131},{2,128},{3,129},{4,134},{5,135},{6,132},{7,133},{8... | collective-permute-start | bytes 159752 | tf_op jit(solution)/shard_map/ppermute | solution.py:312
  14.5 0.0 collective-permute-start.2
  14.5 1.2 %collective-permute-start.1 = (bf16[208,128]{1,0:T(8,128)(2,1)S(1)}, bf16[208,128]{1,0:T(8,128)(2,1)S(1)}, u32[]{:S(2)}, u32[]{:S(2)}) collective-permute-start(bf16[208,128]{1,0:T(8,128)(2,1)S(1)} %add_partials.4.refs_0_), channel_id=1, source_target_pairs={{0,129},{1,128},{2,131},{3,130},{4,133},{5,132},{6,135},{7,134},{8... | collective-permute-start | bytes 159752 | tf_op jit(solution)/shard_map/ppermute | solution.py:312
  15.7 1.0 %collective-permute-done.3.refs_3_ = bf16[208,128]{1,0:T(8,128)(2,1)S(1)} collective-permute-done((bf16[208,128]{1,0:T(8,128)(2,1)S(1)}, bf16[208,128]{1,0:T(8,128)(2,1)S(1)}, u32[]{:S(2)}, u32[]{:S(2)}) %collective-permute-start.3) | collective-permute-done | bytes 53280 | tf_op jit(solution)/shard_map/ppermute | solution.py:312
  16.7 3.4 %collective-permute-done.2.refs_2_ = bf16[208,128]{1,0:T(8,128)(2,1)S(1)} collective-permute-done((bf16[208,128]{1,0:T(8,128)(2,1)S(1)}, bf16[208,128]{1,0:T(8,128)(2,1)S(1)}, u32[]{:S(2)}, u32[]{:S(2)}) %collective-permute-start.2) | collective-permute-done | bytes 53280 | tf_op jit(solution)/shard_map/ppermute | solution.py:312
  20.1 0.2 collective-permute-done.1.refs_1_
  20.3 2.5 %collective-permute-start.6 = (bf16[208,128]{1,0:T(8,128)(2,1)S(1)}, bf16[208,128]{1,0:T(8,128)(2,1)S(1)}, u32[]{:S(2)}, u32[]{:S(2)}) collective-permute-start(bf16[208,128]{1,0:T(8,128)(2,1)S(1)} %add_partials.5.refs_0_), channel_id=1, source_target_pairs={{0,64},{1,65},{2,66},{3,67},{4,68},{5,69},{6,70},{7,71},{8,72},{9,... | collective-permute-start | bytes 159752 | tf_op jit(solution)/shard_map/ppermute | solution.py:312
  22.8 1.4 %collective-permute-start.5 = (bf16[208,128]{1,0:T(8,128)(2,1)S(1)}, bf16[208,128]{1,0:T(8,128)(2,1)S(1)}, u32[]{:S(2)}, u32[]{:S(2)}) collective-permute-start(bf16[208,128]{1,0:T(8,128)(2,1)S(1)} %add_partials.5.refs_0_), channel_id=1, source_target_pairs={{0,97},{1,96},{2,99},{3,98},{4,101},{5,100},{6,103},{7,102},{8,105... | collective-permute-start | bytes 159752 | tf_op jit(solution)/shard_map/ppermute | solution.py:312
  24.2 0.0 collective-permute-start.4
  24.2 0.6 %collective-permute-done.6.refs_3_ = bf16[208,128]{1,0:T(8,128)(2,1)S(1)} collective-permute-done((bf16[208,128]{1,0:T(8,128)(2,1)S(1)}, bf16[208,128]{1,0:T(8,128)(2,1)S(1)}, u32[]{:S(2)}, u32[]{:S(2)}) %collective-permute-start.6) | collective-permute-done | bytes 53280 | tf_op jit(solution)/shard_map/ppermute | solution.py:312
  24.9 3.6 %collective-permute-done.5.refs_2_ = bf16[208,128]{1,0:T(8,128)(2,1)S(1)} collective-permute-done((bf16[208,128]{1,0:T(8,128)(2,1)S(1)}, bf16[208,128]{1,0:T(8,128)(2,1)S(1)}, u32[]{:S(2)}, u32[]{:S(2)}) %collective-permute-start.5) | collective-permute-done | bytes 53280 | tf_op jit(solution)/shard_map/ppermute | solution.py:312
  28.4 0.0 collective-permute-done.4.refs_1_
  28.5 3.0 %collective-permute-start.9 = (bf16[208,128]{1,0:T(8,128)(2,1)S(1)}, bf16[208,128]{1,0:T(8,128)(2,1)S(1)}, u32[]{:S(2)}, u32[]{:S(2)}) collective-permute-start(bf16[208,128]{1,0:T(8,128)(2,1)S(1)} %add_partials.6.refs_0_), channel_id=1, source_target_pairs={{0,16},{1,17},{2,18},{3,19},{4,20},{5,21},{6,22},{7,23},{8,24},{9,... | collective-permute-start | bytes 159752 | tf_op jit(solution)/shard_map/ppermute | solution.py:312
  31.5 1.3 %collective-permute-start.8 = (bf16[208,128]{1,0:T(8,128)(2,1)S(1)}, bf16[208,128]{1,0:T(8,128)(2,1)S(1)}, u32[]{:S(2)}, u32[]{:S(2)}) collective-permute-start(bf16[208,128]{1,0:T(8,128)(2,1)S(1)} %add_partials.6.refs_0_), channel_id=1, source_target_pairs={{0,25},{1,24},{2,27},{3,26},{4,29},{5,28},{6,31},{7,30},{8,17},{9,... | collective-permute-start | bytes 159752 | tf_op jit(solution)/shard_map/ppermute | solution.py:312
  32.8 0.0 collective-permute-start.7
  32.8 0.2 collective-permute-done.9.refs_3_
  33.0 4.0 %collective-permute-done.8.refs_2_ = bf16[208,128]{1,0:T(8,128)(2,1)S(1)} collective-permute-done((bf16[208,128]{1,0:T(8,128)(2,1)S(1)}, bf16[208,128]{1,0:T(8,128)(2,1)S(1)}, u32[]{:S(2)}, u32[]{:S(2)}) %collective-permute-start.8) | collective-permute-done | bytes 53280 | tf_op jit(solution)/shard_map/ppermute | solution.py:312
  37.1 0.0 collective-permute-done.7.refs_1_
  37.1 3.2 %collective-permute-start.10 = (bf16[208,128]{1,0:T(8,128)(2,1)S(1)}, bf16[208,128]{1,0:T(8,128)(2,1)S(1)}, u32[]{:S(2)}, u32[]{:S(2)}) collective-permute-start(bf16[208,128]{1,0:T(8,128)(2,1)S(1)} %add_partials.7.a_ref), channel_id=1, source_target_pairs={{0,7},{1,6},{2,5},{3,4},{4,3},{5,2},{6,1},{7,0},{8,15},{9,14},{10,... | collective-permute-start | bytes 159752 | tf_op jit(solution)/shard_map/ppermute | solution.py:312
  40.3 2.9 %collective-permute-done.10.b_ref = bf16[208,128]{1,0:T(8,128)(2,1)S(1)} collective-permute-done((bf16[208,128]{1,0:T(8,128)(2,1)S(1)}, bf16[208,128]{1,0:T(8,128)(2,1)S(1)}, u32[]{:S(2)}, u32[]{:S(2)}) %collective-permute-start.10) | collective-permute-done | bytes 53280 | tf_op jit(solution)/shard_map/ppermute | solution.py:312
  43.3 0.2 owner_part.1
  43.4 0.5 collective-permute-start.11
  43.9 0.9 %collective-permute-done.11.other_ref = bf16[128,128]{1,0:T(8,128)(2,1)S(1)} collective-permute-done((bf16[128,128]{1,0:T(8,128)(2,1)S(1)}, bf16[128,128]{1,0:T(8,128)(2,1)S(1)}, u32[]{:S(2)}, u32[]{:S(2)}) %collective-permute-start.11) | collective-permute-done | bytes 32800 | tf_op jit(solution)/shard_map/ppermute | solution.py:320
  44.8 1.5 %modes_part.1 = (f32[1536,128]{1,0:T(8,128)}, f32[8,16]{1,0:T(8,128)}) custom-call(bf16[128,128]{1,0:T(8,128)(2,1)S(1)} %get-tuple-element.11.mine_ref, bf16[128,128]{1,0:T(8,128)(2,1)S(1)} %collective-permute-done.11.other_ref, f32[8,128]{1,0:T(8,128)S(1)} %get-tuple-element.12.s_ref, bf16[2048,768]{1,0:T(8,128)(2,1)S(1)} %get-tuple-element.13.y_ref), custom_call_target="tpu_custom_call" | custom-call | tf_op jit(solution)/shard_map/modes_part/pallas_call | solution.py:321
  (4 shorter events, 0.2 us)
Async XLA Ops:
  7.6 4.2 %collective-permute-start = (bf16[208,128]{1,0:T(8,128)(2,1)S(1)}, bf16[208,128]{1,0:T(8,128)(2,1)S(1)}, u32[]{:S(2)}, u32[]{:S(2)}) collective-permute-start(bf16[208,128]{1,0:T(8,128)(2,1)S(1)} %get-tuple-element.10), channel_id=1, source_target_pairs={{0,1},{1,0},{2,3},{3,2},{4,5},{5,4},{6,7},{7,6},{8,9},{9,8},{10,11... | collective-permute-start | bytes 159752 | tf_op jit(solution)/shard_map/ppermute | solution.py:303
  11.8 4.9 %collective-permute-start.3 = (bf16[208,128]{1,0:T(8,128)(2,1)S(1)}, bf16[208,128]{1,0:T(8,128)(2,1)S(1)}, u32[]{:S(2)}, u32[]{:S(2)}) collective-permute-start(bf16[208,128]{1,0:T(8,128)(2,1)S(1)} %add_partials.4.refs_0_), channel_id=1, source_target_pairs={{0,130},{1,131},{2,128},{3,129},{4,134},{5,135},{6,132},{7,133},{8... | collective-permute-start | bytes 159752 | tf_op jit(solution)/shard_map/ppermute | solution.py:312
  14.5 5.6 %collective-permute-start.2 = (bf16[208,128]{1,0:T(8,128)(2,1)S(1)}, bf16[208,128]{1,0:T(8,128)(2,1)S(1)}, u32[]{:S(2)}, u32[]{:S(2)}) collective-permute-start(bf16[208,128]{1,0:T(8,128)(2,1)S(1)} %add_partials.4.refs_0_), channel_id=1, source_target_pairs={{0,3},{1,2},{2,1},{3,0},{4,7},{5,6},{6,5},{7,4},{8,11},{9,10},{10,... | collective-permute-start | bytes 159752 | tf_op jit(solution)/shard_map/ppermute | solution.py:312
  14.5 5.8 %collective-permute-start.1 = (bf16[208,128]{1,0:T(8,128)(2,1)S(1)}, bf16[208,128]{1,0:T(8,128)(2,1)S(1)}, u32[]{:S(2)}, u32[]{:S(2)}) collective-permute-start(bf16[208,128]{1,0:T(8,128)(2,1)S(1)} %add_partials.4.refs_0_), channel_id=1, source_target_pairs={{0,129},{1,128},{2,131},{3,130},{4,133},{5,132},{6,135},{7,134},{8... | collective-permute-start | bytes 159752 | tf_op jit(solution)/shard_map/ppermute | solution.py:312
  20.3 4.6 %collective-permute-start.6 = (bf16[208,128]{1,0:T(8,128)(2,1)S(1)}, bf16[208,128]{1,0:T(8,128)(2,1)S(1)}, u32[]{:S(2)}, u32[]{:S(2)}) collective-permute-start(bf16[208,128]{1,0:T(8,128)(2,1)S(1)} %add_partials.5.refs_0_), channel_id=1, source_target_pairs={{0,64},{1,65},{2,66},{3,67},{4,68},{5,69},{6,70},{7,71},{8,72},{9,... | collective-permute-start | bytes 159752 | tf_op jit(solution)/shard_map/ppermute | solution.py:312
  22.8 5.6 %collective-permute-start.5 = (bf16[208,128]{1,0:T(8,128)(2,1)S(1)}, bf16[208,128]{1,0:T(8,128)(2,1)S(1)}, u32[]{:S(2)}, u32[]{:S(2)}) collective-permute-start(bf16[208,128]{1,0:T(8,128)(2,1)S(1)} %add_partials.5.refs_0_), channel_id=1, source_target_pairs={{0,97},{1,96},{2,99},{3,98},{4,101},{5,100},{6,103},{7,102},{8,105... | collective-permute-start | bytes 159752 | tf_op jit(solution)/shard_map/ppermute | solution.py:312
  24.2 4.2 %collective-permute-start.4 = (bf16[208,128]{1,0:T(8,128)(2,1)S(1)}, bf16[208,128]{1,0:T(8,128)(2,1)S(1)}, u32[]{:S(2)}, u32[]{:S(2)}) collective-permute-start(bf16[208,128]{1,0:T(8,128)(2,1)S(1)} %add_partials.5.refs_0_), channel_id=1, source_target_pairs={{0,33},{1,32},{2,35},{3,34},{4,37},{5,36},{6,39},{7,38},{8,41},{9,... | collective-permute-start | bytes 159752 | tf_op jit(solution)/shard_map/ppermute | solution.py:312
  28.5 4.6 %collective-permute-start.9 = (bf16[208,128]{1,0:T(8,128)(2,1)S(1)}, bf16[208,128]{1,0:T(8,128)(2,1)S(1)}, u32[]{:S(2)}, u32[]{:S(2)}) collective-permute-start(bf16[208,128]{1,0:T(8,128)(2,1)S(1)} %add_partials.6.refs_0_), channel_id=1, source_target_pairs={{0,16},{1,17},{2,18},{3,19},{4,20},{5,21},{6,22},{7,23},{8,24},{9,... | collective-permute-start | bytes 159752 | tf_op jit(solution)/shard_map/ppermute | solution.py:312
  31.5 5.6 %collective-permute-start.8 = (bf16[208,128]{1,0:T(8,128)(2,1)S(1)}, bf16[208,128]{1,0:T(8,128)(2,1)S(1)}, u32[]{:S(2)}, u32[]{:S(2)}) collective-permute-start(bf16[208,128]{1,0:T(8,128)(2,1)S(1)} %add_partials.6.refs_0_), channel_id=1, source_target_pairs={{0,25},{1,24},{2,27},{3,26},{4,29},{5,28},{6,31},{7,30},{8,17},{9,... | collective-permute-start | bytes 159752 | tf_op jit(solution)/shard_map/ppermute | solution.py:312
  32.8 4.3 %collective-permute-start.7 = (bf16[208,128]{1,0:T(8,128)(2,1)S(1)}, bf16[208,128]{1,0:T(8,128)(2,1)S(1)}, u32[]{:S(2)}, u32[]{:S(2)}) collective-permute-start(bf16[208,128]{1,0:T(8,128)(2,1)S(1)} %add_partials.6.refs_0_), channel_id=1, source_target_pairs={{0,9},{1,8},{2,11},{3,10},{4,13},{5,12},{6,15},{7,14},{8,1},{9,0},... | collective-permute-start | bytes 159752 | tf_op jit(solution)/shard_map/ppermute | solution.py:312
  37.1 6.1 %collective-permute-start.10 = (bf16[208,128]{1,0:T(8,128)(2,1)S(1)}, bf16[208,128]{1,0:T(8,128)(2,1)S(1)}, u32[]{:S(2)}, u32[]{:S(2)}) collective-permute-start(bf16[208,128]{1,0:T(8,128)(2,1)S(1)} %add_partials.7.a_ref), channel_id=1, source_target_pairs={{0,7},{1,6},{2,5},{3,4},{4,3},{5,2},{6,1},{7,0},{8,15},{9,14},{10,... | collective-permute-start | bytes 159752 | tf_op jit(solution)/shard_map/ppermute | solution.py:312
  43.4 1.3 %collective-permute-start.11 = (bf16[128,128]{1,0:T(8,128)(2,1)S(1)}, bf16[128,128]{1,0:T(8,128)(2,1)S(1)}, u32[]{:S(2)}, u32[]{:S(2)}) collective-permute-start(bf16[128,128]{1,0:T(8,128)(2,1)S(1)} %get-tuple-element.11.mine_ref), channel_id=1, source_target_pairs={{0,1},{1,0},{2,3},{3,2},{4,5},{5,4},{6,7},{7,6},{8,9},{9,8},{10,11... | collective-permute-start | bytes 98312 | tf_op jit(solution)/shard_map/ppermute | solution.py:320
